TPU v7x, 32 devices: a whole 2x2x4 slice. The times are simulated.
32 devices in a mesh: pole: 2 (over y), row: 8 (over z, x), col: 2 (over core).
Axes of the slice: x: 2, y: 2, z: 4, core: 2. Of those that a mesh axis runs over, the one named last changes fastest.
Arguments:
- known_inverse: float32 [16, 128, 1024], P('pole', 'col', 'row'), parts along dimension 0, may hold values from -1 to 3, as said below
- first_factor: float32 [2048, 512], P(('pole', 'row')), parts along dimension 0, may hold values from -0.5 to 0.5
- first_corner: float32 [1024, 512], P('pole'), parts along dimension 0, may hold values from -1 to 5, as said below
- first_ancestors: int32 [1024], P('pole'), parts along dimension 0, may hold values from 0 to 1023, as said below
- second_factor: float32 [2048, 512], P(('pole', 'row')), parts along dimension 0, may hold values from -0.75 to 0.75
- second_link: float32 [1024, 512], P('pole'), parts along dimension 0, may hold values from -0.25 to 0.25
- second_corner: float32 [1024, 512], P('pole', 'col'), parts along dimension 0, may hold values from -1 to 5, as said below
- second_ancestors: int32 [512], P('pole'), parts along dimension 0, may hold values from 0 to 1023, as said below
Outputs:
- first_column: float32 [2048, 512], P(('pole', 'row'), 'col'), parts along dimension 0
- first_diagonal: float32 [1024, 512], P('pole', 'col'), parts along dimension 0
- second_column: float32 [2048, 512], P(('pole', 'row'), 'col'), parts along dimension 0
- second_cross: float32 [1024, 512], P('pole', 'col'), parts along dimension 0
- second_diagonal: float32 [1024, 512], P('pole', 'col'), parts along dimension 0
There are 2 independent parts, one for each index of `pole`. A program takes and returns all parts, laid end to end along the dimension named above; each array names one. Nothing has to cross between parts.
Inputs may be any that keep to these rules, and one draw needn't show every extreme that they name: `known_inverse`: K is symmetric. `first_corner`: symmetric. `second_corner`: symmetric. `first_ancestors`: distinct row numbers; every block of 128 consecutive row numbers starting at a multiple of 128 holds at least one of them. `second_ancestors`: distinct row numbers, each of which is also in first_ancestors; every block of 128 consecutive row numbers starting at a multiple of 128 holds at least one of them.
All inputs are finite; a program needn't handle non-finite values.
Results may differ from a plain program's by a relative error of at most 0.000084.
Values sent between devices are 32-bit elements; how exact they have to be, the bound alone decides.
No kernel may reach another device: no remote copies, remote signals or barrier semaphores. Data moves between devices by JAX's collectives and lax.ppermute only.
A program may use at most 128 MiB of HBM per device.

v0:
```python
import jax
import jax.numpy as jnp
from jax import lax
from jax.sharding import PartitionSpec as P

HIGH = lax.Precision.HIGHEST


def product(left, right):
    return jnp.dot(left, right, precision=HIGH, preferred_element_type=jnp.float32)


def transposed_product(left, right):
    return lax.dot_general(
        left, right, (((0,), (0,)), ((), ())), precision=HIGH, preferred_element_type=jnp.float32
    )


def local_mask(ancestors, row_start, block_rows):
    global_rows = row_start + jnp.arange(block_rows, dtype=jnp.int32)
    return jnp.any(ancestors[:, None] == global_rows[None, :], axis=0).astype(jnp.float32)[:, None]


def on_device(
    known_inverse,
    first_factor,
    first_corner,
    first_ancestors,
    second_factor,
    second_link,
    second_corner,
    second_ancestors,
):
    groups, share_rows, block_rows = known_inverse.shape
    half_width = second_corner.shape[1]
    col_index = lax.axis_index("col")
    row_start = lax.axis_index("row") * block_rows
    first_mask = local_mask(first_ancestors, row_start, block_rows)
    second_mask = local_mask(second_ancestors, row_start, block_rows)
    first_masked = first_factor * first_mask
    second_masked = second_factor * second_mask
    share_start = col_index * share_rows
    first_piece = lax.dynamic_slice_in_dim(first_masked, share_start, share_rows, 0)
    second_piece = lax.dynamic_slice_in_dim(second_masked, share_start, share_rows, 0)
    columns = known_inverse.reshape(groups * share_rows, block_rows)

    def add_piece(piece):
        return transposed_product(columns, piece)

    first_partial = add_piece(lax.all_gather(first_piece, "row", axis=0, tiled=True))
    second_partial = add_piece(lax.all_gather(second_piece, "row", axis=0, tiled=True))
    first_image = lax.psum_scatter(first_partial, "col", scatter_dimension=1, tiled=True)
    first_column = -(first_image * first_mask)
    first_full = lax.all_gather(first_column, "col", axis=1, tiled=True)
    diagonal_partial = transposed_product(first_masked, first_column)
    corner_half = lax.dynamic_slice_in_dim(first_corner, col_index * half_width, half_width, 1)
    first_diagonal = corner_half - lax.psum(diagonal_partial, "row")
    diagonal_full = lax.all_gather(first_diagonal, "col", axis=1, tiled=True)
    second_image = lax.psum_scatter(second_partial, "col", scatter_dimension=1, tiled=True)
    link_half = lax.dynamic_slice_in_dim(second_link, col_index * half_width, half_width, 1)
    second_column = -((second_image + product(first_full, link_half)) * second_mask)
    second_half = lax.dynamic_slice_in_dim(second_masked, col_index * half_width, half_width, 1)
    cross_partial = transposed_product(first_full, second_half)
    closing_partial = transposed_product(second_masked, second_column)
    cross_total, closing_total = lax.psum((cross_partial, closing_partial), "row")
    second_cross = -(cross_total + product(diagonal_full, link_half))
    second_diagonal = second_corner - closing_total - transposed_product(second_link, second_cross)
    return (first_column, first_diagonal, second_column, second_cross, second_diagonal)


def solution(mesh):
    return jax.shard_map(
        on_device,
        mesh=mesh,
        in_specs=(
            P("pole", "col", "row"),
            P(("pole", "row"), None),
            P("pole", None),
            P("pole"),
            P(("pole", "row"), None),
            P("pole", None),
            P("pole", "col"),
            P("pole"),
        ),
        out_specs=(
            P(("pole", "row"), "col"),
            P("pole", "col"),
            P(("pole", "row"), "col"),
            P("pole", "col"),
            P("pole", "col"),
        ),
        check_vma=False,
    )
```

profile of v0, /device:TPU:0, one launch (start us, length us, event | category | flops | bytes accessed | tf_op | source)
XLA Modules:
  0.0 233.3 jit_solution(5799603692559722448)
XLA Ops:
  7.3 0.7 copy-done.8
  8.0 0.1 compare_reduce_fusion
  8.2 1.0 broadcast_multiply_fusion.1
  9.2 0.7 constant_dynamic-slice_fusion.1
  9.9 0.0 all-gather.6.cloned.1.call-start
  10.0 0.6 copy-done.9
  10.6 0.1 compare_reduce_fusion.1
  10.7 0.1 broadcast_multiply_fusion
  10.8 0.7 constant_dynamic-slice_fusion
  11.5 0.0 reduce-scatter.3.cloned.1.call-start
  11.5 42.2 %all-gather.4.cloned.1.call-done = f32[512,512]{1,0:T(8,128)} async-done(((f32[64,512]{1,0:T(8,128)}), f32[512,512]{1,0:T(8,128)}) %all-gather.4.cloned.1.call-update) | async-done | bytes 1048592 | tf_op jit(solution)/shard_map/all_gather | solution.py:50
  53.7 3.7 %convolution_bitcast_fusion.2 = f32[128,512]{0,1:T(8,128)} fusion(f32[512,512]{1,0:T(8,128)} %all-gather.4.cloned.1.call-done, f32[512,128]{1,0:T(8,128)S(1)} %bitcast.22), kind=kOutput, calls=%fused_computation.5 | convolution fusion | flops 402653184 | bytes 1572864 | tf_op jit(solution)/shard_map/dot_general | solution.py:14
  57.5 0.0 reduce-scatter.5.cloned.1.call-start
  57.5 37.9 %all-gather.6.cloned.1.call-done = f32[512,512]{1,0:T(8,128)} async-done(((f32[64,512]{1,0:T(8,128)}), f32[512,512]{1,0:T(8,128)}) %all-gather.6.cloned.1.call-update) | async-done | bytes 1048592 | tf_op jit(solution)/shard_map/all_gather | solution.py:51
  95.4 3.7 %convolution_bitcast_fusion.1 = f32[128,512]{0,1:T(8,128)} fusion(f32[512,512]{1,0:T(8,128)} %all-gather.6.cloned.1.call-done, f32[512,128]{1,0:T(8,128)S(1)} %bitcast.23), kind=kOutput, calls=%fused_computation.4 | convolution fusion | flops 402653184 | bytes 1572864 | tf_op jit(solution)/shard_map/dot_general | solution.py:14
  99.2 0.0 all-reduce.3.cloned.1.call-start
  99.2 5.5 %reduce-scatter.3.cloned.1.call-done = f32[128,256]{0,1:T(8,128)} async-done(((f32[128,512]{0,1:T(8,128)}), f32[128,256]{0,1:T(8,128)}) %reduce-scatter.3.cloned.1.call-update) | async-done | bytes 131088 | tf_op jit(solution)/shard_map/reduce_scatter | solution.py:52
  104.7 0.9 multiply_negate_fusion
  105.6 2.0 all_gather.14
  107.6 1.4 fusion.6
  109.0 1.4 fusion.11
  110.4 5.9 %reduce-scatter.5.cloned.1.call-done = f32[128,256]{0,1:T(8,128)} async-done(((f32[128,512]{0,1:T(8,128)}), f32[128,256]{0,1:T(8,128)}) %reduce-scatter.5.cloned.1.call-update) | async-done | bytes 131088 | tf_op jit(solution)/shard_map/reduce_scatter | solution.py:59
  116.3 1.9 fusion.3
  118.2 1.4 fusion.12
  119.6 0.0 all-gather.8.cloned.1.call-start
  119.7 91.4 %all-reduce.3.cloned.1.call-done = (f32[512,256]{1,0:T(8,128)}, f32[512,256]{1,0:T(8,128)}, f32[512,256]{1,0:T(8,128)}) async-done(((f32[512,256]{1,0:T(8,128)}, f32[512,256]{1,0:T(8,128)}, f32[512,256]{1,0:T(8,128)}), (f32[512,256]{1,0:T(8,128)}, f32[512,256]{1,0:T(8,128)}, f32[512,256]{1,0:T(8,128)})) %all-reduce.3.cloned.1.call-update) | async-done | bytes 1572880 | tf_op jit(solution)/shard_map/psum | solution.py:57
  211.1 1.9 dynamic-slice_subtract_fusion
  213.1 0.8 copy.19
  213.8 0.8 copy.20
  214.6 6.9 %all-gather.8.cloned.1.call-done = f32[512,512]{1,0:T(8,128)} async-done(((f32[512,256]{1,0:T(8,128)}), f32[512,512]{1,0:T(8,128)}) %all-gather.8.cloned.1.call-update) | async-done | bytes 1048592 | tf_op jit(solution)/shard_map/all_gather | solution.py:58
  221.5 2.3 fusion
  223.8 2.6 %fusion.1 = f32[512,256]{1,0:T(8,128)} fusion(f32[512,256]{1,0:T(8,128)S(1)} %fusion, f32[512,512]{1,0:T(8,128)S(1)} %copy-done, f32[512,256]{1,0:T(8,128)S(1)} %copy-done.3, f32[512,256]{1,0:T(8,128)S(1)} %copy-done.4), kind=kOutput, calls=%fused_computation.3 | convolution fusion | flops 805568512 | bytes 3145728 | tf_op jit(solution)/shard_map/dot_general | solution.py:14
  (28 shorter events, 0.2 us)
Async XLA Ops:
  7.2 109.1 %copy-start = (f32[512,512]{1,0:T(8,128)S(1)}, f32[512,512]{1,0:T(8,128)}, u32[]{:S(2)}) copy-start(f32[512,512]{1,0:T(8,128)} %param.13) | copy-start | bytes 3145732
  7.2 46.5 %all-gather.4.cloned.1.call-start = ((), (), s32[]{:S(2)}) async-start(), calls=%async_computation.2 | async-start | bytes 1179648 | tf_op jit(solution)/shard_map/all_gather | solution.py:50
  7.2 0.8 copy-start.8
  9.2 1.5 copy-start.6
  9.9 0.7 copy-start.9
  9.9 85.5 %all-gather.6.cloned.1.call-start = ((), (), s32[]{:S(2)}) async-start(), calls=%async_computation.4 | async-start | bytes 1179648 | tf_op jit(solution)/shard_map/all_gather | solution.py:51
  10.8 42.9 %copy-start.2 = (f32[8,64,128]{2,1,0:T(8,128)S(1)}, f32[8,64,128]{2,1,0:T(8,128)}, u32[]{:S(2)}) copy-start(f32[8,64,128]{2,1,0:T(8,128)} %param.8) | copy-start | bytes 786436
  11.5 93.2 %reduce-scatter.3.cloned.1.call-start = ((), (), s32[]{:S(2)}) async-start(), calls=%async_computation.3 | async-start | bytes 393216 | tf_op jit(solution)/shard_map/reduce_scatter | solution.py:52
  57.5 58.8 %reduce-scatter.5.cloned.1.call-start = ((), (), s32[]{:S(2)}) async-start(), calls=%async_computation.5 | async-start | bytes 393216 | tf_op jit(solution)/shard_map/reduce_scatter | solution.py:59
  99.2 111.9 %all-reduce.3.cloned.1.call-start = ((), (), s32[]{:S(2)}) async-start(), calls=%async_computation.7 | async-start | bytes 3145728 | tf_op jit(solution)/shard_map/psum | solution.py:57
  118.2 93.0 %copy-start.7 = (f32[512,512]{1,0:T(8,128)S(1)}, f32[512,512]{1,0:T(8,128)}, u32[]{:S(2)}) copy-start(f32[512,512]{1,0:T(8,128)} %param.10) | copy-start | bytes 3145732
  119.6 101.8 %all-gather.8.cloned.1.call-start = ((), (), s32[]{:S(2)}) async-start(), calls=%async_computation.6 | async-start | bytes 1572864 | tf_op jit(solution)/shard_map/all_gather | solution.py:58
  213.0 8.4 %copy-start.5 = (f32[512,256]{1,0:T(8,128)S(1)}, f32[512,256]{1,0:T(8,128)}, u32[]{:S(2)}) copy-start(f32[512,256]{1,0:T(8,128)} %get-tuple-element.16) | copy-start | bytes 1572868
  221.5 2.3 copy-start.3
  221.5 2.3 copy-start.4
  223.8 2.7 %copy-start.1 = (f32[512,256]{1,0:T(8,128)}, f32[512,256]{1,0:T(8,128)S(1)}, u32[]{:S(2)}) copy-start(f32[512,256]{1,0:T(8,128)S(1)} %fusion) | copy-start | bytes 1572868
Sparse Core Ops, SparseCore 0:
  10.7 42.9 all-gather.3
  56.4 38.9 all-gather.5
  98.2 6.4 reduce-scatter.2
  107.4 8.8 reduce-scatter.4
  120.6 90.5 all-reduce.2
  213.2 8.2 all-gather.7
where the time goes:
time: 234 us; the launch traced here: 233 us
  waiting for transfers between devices  190 us (81%)
  matrix products  18.5 us (8%)
  between operations  14.2 us (6%)
  local copies, waits for them, and re-layouts  4.25 us (2%)
  other arithmetic  4.23 us (2%)
    psum x1, waiting for transfers between devices, on_device(): first_diagonal = corner_half - lax.psum(diagonal_partial, 'row')  91.4 us
    all_gather x1, waiting for transfers between devices, on_device(): lax.all_gather(first_piece, 'row', axis=0, tiled=True)  42.2 us
    all_gather x1, waiting for transfers between devices, on_device(): lax.all_gather(second_piece, 'row', axis=0, tiled=True)  37.9 us
    dot_general x6, matrix products, transposed_product(): lax.dot_general(left, right, (((0,), (0,)), ((), ())), precision=HIGH, pr...  14.3 us
    all_gather x1, waiting for transfers between devices, on_device(): diagonal_full = lax.all_gather(first_diagonal, 'col', axis=1, tiled=True)  6.88 us
    reduce_scatter x1, waiting for transfers between devices, on_device(): lax.psum_scatter(second_partial, 'col', scatter_dimension=1, tiled=True)  5.86 us
    reduce_scatter x1, waiting for transfers between devices, on_device(): lax.psum_scatter(first_partial, 'col', scatter_dimension=1, tiled=True)  5.48 us
  transfers between devices with their start and end apart: 6, of which 6 were waited for; matrix products, arithmetic and copies ran while one was open for 6% of the time, Pallas kernels for 0%

commit v1 on v0

--- a/solution.py
+++ b/solution.py
@@ -1,54 +1,50 @@
+import functools
+
 import jax
 import jax.numpy as jnp
 from jax import lax
+from jax.experimental import pallas as pl
+from jax.experimental.pallas import tpu as pltpu
 from jax.sharding import PartitionSpec as P
 
 HIGH = lax.Precision.HIGHEST
+F32, BF16 = jnp.float32, jnp.bfloat16
+NN = (((1,), (0,)), ((), ()))
+NT = (((1,), (1,)), ((), ()))
+TN = (((0,), (0,)), ((), ()))
+VMEM = pl.BlockSpec(memory_space=pltpu.VMEM)
+SMEM = pl.BlockSpec(memory_space=pltpu.SMEM)
+ANY = pl.BlockSpec(memory_space=pl.ANY)
 
 
 def product(left, right):
-    return jnp.dot(left, right, precision=HIGH, preferred_element_type=jnp.float32)
+    return jnp.dot(left, right, precision=HIGH, preferred_element_type=F32)
 
 
 def transposed_product(left, right):
-    return lax.dot_general(
-        left, right, (((0,), (0,)), ((), ())), precision=HIGH, preferred_element_type=jnp.float32
-    )
-
-
-def local_mask(ancestors, row_start, block_rows):
-    global_rows = row_start + jnp.arange(block_rows, dtype=jnp.int32)
-    return jnp.any(ancestors[:, None] == global_rows[None, :], axis=0).astype(jnp.float32)[:, None]
-
-
-def on_device(
-    known_inverse,
-    first_factor,
-    first_corner,
-    first_ancestors,
-    second_factor,
-    second_link,
-    second_corner,
-    second_ancestors,
-):
+    return lax.dot_general(left, right, TN, precision=HIGH, preferred_element_type=F32)
+
+
+def mask_of(ancestors, row_start, rows):
+    numbers = row_start + jnp.arange(rows, dtype=jnp.int32)
+    return jnp.any(ancestors[:, None] == numbers[None, :], axis=0).astype(F32)
+
+
+def reduce_plan(known_inverse, first_factor, first_corner, first_ancestors, second_factor, second_link, second_corner, second_ancestors):
     groups, share_rows, block_rows = known_inverse.shape
     half_width = second_corner.shape[1]
     col_index = lax.axis_index("col")
     row_start = lax.axis_index("row") * block_rows
-    first_mask = local_mask(first_ancestors, row_start, block_rows)
-    second_mask = local_mask(second_ancestors, row_start, block_rows)
+    first_mask = mask_of(first_ancestors, row_start, block_rows)[:, None]
+    second_mask = mask_of(second_ancestors, row_start, block_rows)[:, None]
     first_masked = first_factor * first_mask
     second_masked = second_factor * second_mask
     share_start = col_index * share_rows
     first_piece = lax.dynamic_slice_in_dim(first_masked, share_start, share_rows, 0)
     second_piece = lax.dynamic_slice_in_dim(second_masked, share_start, share_rows, 0)
     columns = known_inverse.reshape(groups * share_rows, block_rows)
-
-    def add_piece(piece):
-        return transposed_product(columns, piece)
-
-    first_partial = add_piece(lax.all_gather(first_piece, "row", axis=0, tiled=True))
-    second_partial = add_piece(lax.all_gather(second_piece, "row", axis=0, tiled=True))
+    first_partial = transposed_product(columns, lax.all_gather(first_piece, "row", axis=0, tiled=True))
+    second_partial = transposed_product(columns, lax.all_gather(second_piece, "row", axis=0, tiled=True))
     first_image = lax.psum_scatter(first_partial, "col", scatter_dimension=1, tiled=True)
     first_column = -(first_image * first_mask)
     first_full = lax.all_gather(first_column, "col", axis=1, tiled=True)
@@ -68,7 +64,228 @@
     return (first_column, first_diagonal, second_column, second_cross, second_diagonal)
 
 
+def dot(left, right, dims):
+    return lax.dot_general(left, right, dims, preferred_element_type=F32)
+
+
+def split(value):
+    high = value.astype(BF16)
+    return high, (value - high.astype(F32)).astype(BF16)
+
+
+def dot3(left, right, dims):
+    (lh, ll), (rh, rl) = left, right
+    return dot(lh, rh, dims) + (dot(lh, rl, dims) + dot(ll, rh, dims))
+
+
+def dot2(exact, right, dims, flip=False):
+    rh, rl = right
+    if flip:
+        return dot(rh, exact, dims) + dot(rl, exact, dims)
+    return dot(exact, rh, dims) + dot(exact, rl, dims)
+
+
+def slot_codes(mask):
+    block = mask.shape[1]
+    before = (lax.broadcasted_iota(jnp.int32, (block, block), 0) < lax.broadcasted_iota(jnp.int32, (block, block), 1)).astype(BF16)
+    rank = dot(mask.astype(BF16), before, NN)
+    return jnp.where(mask > 0, rank, -1.0).astype(jnp.int32)
+
+
+def picker(code_row, slots, offset=0):
+    block = code_row.shape[1]
+    at = lax.broadcasted_iota(jnp.int32, (slots, block), 0) - offset
+    return ((at == code_row) & (code_row >= 0)).astype(BF16)
+
+
+def prepare_kernel(cap, place, mask1, mask2, first, second, link, mine, theirs, out, code, m2, cols):
+    row, col = place[0], place[1]
+    groups, share, block = mine.shape
+    width = first.shape[1]
+    code[...] = slot_codes(mask1[...])
+    m2[...] = mask2[...]
+    pick = picker(code[pl.ds(row, 1), :], cap)
+    pick2 = (pick.astype(F32) * m2[pl.ds(row, 1), :]).astype(BF16)
+    first_c = dot2(pick, split(first[...]), NN)
+    second_c = dot2(pick2, split(second[...]), NN)
+    out[:, :width] = first_c
+    out[:, width : 2 * width] = second_c - dot3(split(first_c), split(link[...]), NN)
+    for g in range(groups):
+        base = g * block
+        cols[pl.ds(pl.multiple_of(base + col * share, share), share), :] = mine[g]
+        cols[pl.ds(pl.multiple_of(base + (1 - col) * share, share), share), :] = theirs[g]
+    half = dot2(pick, split(cols[...]), NT)
+    wide = out.shape[1] - 2 * width
+    total = jnp.zeros((cap, wide), F32)
+    for g in range(groups):
+        spread = picker(code[g : g + 1, :], wide, g * cap)
+        total += dot2(spread, split(half[:, g * block : (g + 1) * block]), NT, flip=True)
+    out[:, 2 * width :] = total
+
+
+def finish_kernel(cap, sources, *refs):
+    place, mask1, mask2 = refs[:3]
+    own = refs[3]
+    n = len(sources)
+    near, far = refs[4 : 4 + n], refs[4 + n : 4 + 2 * n]
+    corner1, corner2, cross0, diag0 = refs[4 + 2 * n : 8 + 2 * n]
+    outs = refs[8 + 2 * n : 13 + 2 * n]
+    ft, known, code, m2, c1, g1, c2, xx, g2, sems = refs[13 + 2 * n :]
+    row, col = place[0], place[1]
+    width = own.shape[1] - known.shape[1]
+    width //= 2
+    half_width = width // 2
+    half = cap // 2
+
+    code[...] = slot_codes(mask1[...])
+    m2[...] = mask2[...]
+
+    def put(value, start, rows):
+        at = pl.ds(pl.multiple_of(start, 8), rows)
+        ft[at, :] = value[:, : 2 * width]
+        known[at, :] = value[:, 2 * width :]
+
+    put(own[...], row * cap, cap)
+    for source, a, b in zip(sources, near, far):
+        base = source(row) * cap
+        put(a[...], base + col * half, half)
+        put(b[...], base + (1 - col) * half, half)
+
+    start = pl.multiple_of(col * half_width, half_width)
+    right_f = split(ft[:, pl.ds(start, half_width)])
+    right_t = split(ft[:, pl.ds(pl.multiple_of(width + start, half_width), half_width)])
+    k = split(known[...])
+    image_f = dot3(k, right_f, NN)
+    image_t = dot3(k, right_t, NN)
+    c1[...] = image_f
+    c2[...] = image_t
+    mine = pl.ds(pl.multiple_of(row * cap, 8), cap)
+    own_f, own_t = split(c1[mine, :]), split(c2[mine, :])
+    pick = picker(code[pl.ds(row, 1), :], cap)
+    pick2 = (pick.astype(F32) * m2[pl.ds(row, 1), :]).astype(BF16)
+    block = code.shape[1]
+    c1[:block, :] = -dot2(pick, own_f, TN)
+    c2[:block, :] = -dot2(pick2, own_t, TN)
+    copies = [
+        pltpu.make_async_copy(c1.at[:block], outs[0], sems.at[0]),
+        pltpu.make_async_copy(c2.at[:block], outs[2], sems.at[2]),
+    ]
+    for copy in copies:
+        copy.start()
+    image_f, image_t = split(image_f), split(image_t)
+    left_f = split(ft[:, :width])
+    left_t = split(ft[:, width:])
+    g1[...] = corner1[...] + dot3(left_f, image_f, TN)
+    copies.append(pltpu.make_async_copy(g1, outs[1], sems.at[1]))
+    copies[-1].start()
+    xx[...] = dot3(left_f, image_t, TN) - cross0[...]
+    copies.append(pltpu.make_async_copy(xx, outs[3], sems.at[3]))
+    copies[-1].start()
+    g2[...] = corner2[...] + (diag0[...] + dot3(left_t, image_t, TN))
+    copies.append(pltpu.make_async_copy(g2, outs[4], sems.at[4]))
+    copies[-1].start()
+    for copy in copies:
+        copy.wait()
+
+
+def gather_branch(cap, n, place, mask1, mask2, known_inverse, theirs, first_factor, second_factor, second_link, corner1, second_corner, cross0, diag0):
+    groups, share, block = known_inverse.shape
+    width = first_factor.shape[1]
+    half_width = second_corner.shape[1]
+    wide = -(-n * cap // 128) * 128
+    cost = pl.CostEstimate(flops=2 * cap * width * (width + n * block), bytes_accessed=4 * width * width * 2, transcendentals=0)
+    payload = pl.pallas_call(
+        functools.partial(prepare_kernel, cap),
+        out_shape=jax.ShapeDtypeStruct((cap, 2 * width + wide), F32),
+        in_specs=[SMEM] + [VMEM] * 7,
+        out_specs=VMEM,
+        scratch_shapes=[
+            pltpu.VMEM((n, block), jnp.int32),
+            pltpu.VMEM((n, block), F32),
+            pltpu.VMEM((n * block, block), F32),
+        ],
+        cost_estimate=cost,
+        name="prepare",
+    )(place, mask1, mask2, first_factor, second_factor, second_link, known_inverse, theirs)
+
+    half = cap // 2
+    ring = [(r, (r + 2) % n) for r in range(n)]
+    pair = [(r, r ^ 1) for r in range(n)]
+    swap = [(0, 1), (1, 0)]
+    own_half = lax.dynamic_slice_in_dim(payload, lax.axis_index("col") * half, half, 0)
+    along = [own_half]
+    sources, near = [], []
+    across = [lax.ppermute(own_half, "row", pair)]
+    for step in range(1, n // 2):
+        along.append(lax.ppermute(along[-1], "row", ring))
+        across.append(lax.ppermute(along[-1], "row", pair))
+    for step in range(n // 2):
+        if step:
+            near.append(along[step])
+            sources.append(lambda r, s=step: lax.rem(r - 2 * s + n, n))
+        near.append(across[step])
+        sources.append(lambda r, s=step: lax.rem(lax.rem(r, 2) * -2 + 1 + r - 2 * s + n, n))
+    far = [lax.ppermute(v, "col", swap) for v in near]
+
+    rows = wide
+    outs = (
+        jax.ShapeDtypeStruct((block, half_width), F32),
+        jax.ShapeDtypeStruct((width, half_width), F32),
+        jax.ShapeDtypeStruct((block, half_width), F32),
+        jax.ShapeDtypeStruct((width, half_width), F32),
+        jax.ShapeDtypeStruct((width, half_width), F32),
+    )
+    m = len(near)
+    cost = pl.CostEstimate(flops=2 * 3 * (rows * rows * width + 3 * width * rows * half_width), bytes_accessed=4 * rows * (2 * width + wide), transcendentals=0)
+    return pl.pallas_call(
+        functools.partial(finish_kernel, cap, sources),
+        out_shape=outs,
+        in_specs=[SMEM] + [VMEM] * (7 + 2 * m),
+        out_specs=[ANY] * 5,
+        scratch_shapes=[
+            pltpu.VMEM((rows, 2 * width), F32),
+            pltpu.VMEM((rows, wide), F32),
+            pltpu.VMEM((n, block), jnp.int32),
+            pltpu.VMEM((n, block), F32),
+            pltpu.VMEM((max(rows, block), half_width), F32),
+            pltpu.VMEM((width, half_width), F32),
+            pltpu.VMEM((max(rows, block), half_width), F32),
+            pltpu.VMEM((width, half_width), F32),
+            pltpu.VMEM((width, half_width), F32),
+            pltpu.SemaphoreType.DMA((5,)),
+        ],
+        compiler_params=pltpu.CompilerParams(vmem_limit_bytes=48 << 20),
+        cost_estimate=cost,
+        name="finish",
+    )(place, mask1, mask2, payload, *near, *far, corner1, second_corner, cross0, diag0)
+
+
+def gather_plan(n, known_inverse, first_factor, first_corner, first_ancestors, second_factor, second_link, second_corner, second_ancestors):
+    groups, share, block = known_inverse.shape
+    half_width = second_corner.shape[1]
+    row, col = lax.axis_index("row"), lax.axis_index("col")
+    place = jnp.stack([row, col]).astype(jnp.int32)
+    theirs = lax.ppermute(known_inverse, "col", [(0, 1), (1, 0)])
+    mask1 = mask_of(first_ancestors, 0, n * block).reshape(n, block)
+    mask2 = mask_of(second_ancestors, 0, n * block).reshape(n, block)
+    start = col * half_width
+    corner1 = lax.dynamic_slice_in_dim(first_corner, start, half_width, 1)
+    link_half = lax.dynamic_slice_in_dim(second_link, start, half_width, 1)
+    cross0 = product(first_corner, link_half)
+    diag0 = transposed_product(second_link, cross0)
+    return gather_branch(block, n, place, mask1, mask2, known_inverse, theirs, first_factor, second_factor, second_link, corner1, second_corner, cross0, diag0)
+
+
 def solution(mesh):
+    n = mesh.shape["row"]
+
+    def on_device(known_inverse, *rest):
+        groups, share, block = known_inverse.shape
+        width = rest[0].shape[1]
+        if n % 2 == 0 and mesh.shape["col"] == 2 and (n * block) ** 2 <= 12 * width**2:
+            return gather_plan(n, known_inverse, *rest)
+        return reduce_plan(known_inverse, *rest)
+
     return jax.shard_map(
         on_device,
         mesh=mesh,

time: 234 us -> 103 us (0.44)
  waiting for transfers between devices: 190 us -> 61.5 us
  Pallas kernels: 0 us -> 15.8 us
  between operations: 14.2 us -> 0.88 us
  matrix products: 18.5 us -> 7.43 us
  starting transfers between devices: 0.25 us -> 8.66 us
    psum x1 -> x0, waiting for transfers between devices: 91.4 us -> none  [on_device(): first_diagonal = corner_half - lax.psum(diagonal_partial, 'row')]
    all_gather x3 -> x0, waiting for transfers between devices: 87 us -> none  [the longest x1 42.2 us: on_device(): lax.all_gather(first_piece, 'row', axis=0, tiled=True)]
    ppermute x0 -> x15, waiting for transfers between devices: none -> 61.5 us  [the longest x3 40.8 us: gather_branch(): along.append(lax.ppermute(along[-1], 'row', ring))]
    pallas_call x0 -> x2, Pallas kernels: none -> 15.8 us  [the longest x1 11.1 us: gather_branch(): pl.pallas_call(functools.partial(finish_kernel, cap, sources), out_shape=...]
    reduce_scatter x2 -> x0, waiting for transfers between devices: 11.3 us -> none  [the longest x1 5.86 us: on_device(): lax.psum_scatter(second_partial, 'col', scatter_dimension=1, tiled=True)]
    dot_general x8 -> x2, matrix products: 18.5 us -> 7.43 us  [the longest x1 3.73 us: transposed_product(): lax.dot_general(left, right, TN, precision=HIGH, preferred_element_type=F32)]
    ppermute x0 -> x15, starting transfers between devices: none -> 8.66 us  [the longest x3 3.08 us: gather_branch(): across.append(lax.ppermute(along[-1], 'row', pair))]
  transfers between devices with their start and end apart: 6 -> 15, of which waited for: 6 -> 5; matrix products, arithmetic and copies ran while one was open for 6% -> 13% of each run, Pallas kernels for 0% -> 0%
where the time goes in v1:
time: 103 us
  waiting for transfers between devices  61.5 us (60%)
  Pallas kernels  15.8 us (15%)
  starting transfers between devices  8.66 us (8%)
  matrix products  7.43 us (7%)
  local copies, waits for them, and re-layouts  5.24 us (5%)
  other arithmetic  3.11 us (3%)
    ppermute x3, waiting for transfers between devices, gather_branch(): along.append(lax.ppermute(along[-1], 'row', ring))  40.8 us
    ppermute x3, waiting for transfers between devices, gather_branch(): across.append(lax.ppermute(along[-1], 'row', pair))  20.7 us
    pallas_call x1, Pallas kernels, gather_branch(): pl.pallas_call(functools.partial(finish_kernel, cap, sources), out_shape=...  11.1 us
    pallas_call x1, Pallas kernels, gather_branch(): pl.pallas_call(functools.partial(prepare_kernel, cap), out_shape=jax.Shap...  4.66 us
    dot_general x1, matrix products, transposed_product(): lax.dot_general(left, right, TN, precision=HIGH, preferred_element_type=F32)  3.73 us
    dot_general x1, matrix products, product(): return jnp.dot(left, right, precision=HIGH, preferred_element_type=F32)  3.7 us
    ppermute x3, starting transfers between devices, gather_branch(): across.append(lax.ppermute(along[-1], 'row', pair))  3.08 us
    ppermute x3, starting transfers between devices, gather_branch(): along.append(lax.ppermute(along[-1], 'row', ring))  2.71 us
  transfers between devices with their start and end apart: 15, of which 5 were waited for; matrix products, arithmetic and copies ran while one was open for 13% of the time, Pallas kernels for 0%

profile of v1, /device:TPU:0, one launch (start us, length us, event | category | flops | bytes accessed | tf_op | source)
XLA Modules:
  0.0 102.6 jit_solution(18374120436261457161)
XLA Ops:
  0.6 0.0 copy-start
  0.6 0.6 collective-permute-start
  1.2 1.0 %fusion = pred[1024]{0:T(1024)(128)(4,1)S(1)} fusion(s32[512]{0:T(512)} %param.11), kind=kLoop, calls=%fused_computation.1 | loop fusion | flops 1047552 | bytes 3072 | tf_op jit(solution)/shard_map/reduce_or | solution.py:30
  2.2 0.9 fusion.1
  3.1 0.6 pad_add_fusion.place.refs_0_
  3.7 0.6 convert_bitcast_fusion
  4.3 0.7 copy-done.5
  5.0 4.7 %prepare.1.refs_3_ = f32[128,2048]{1,0:T(8,128)} custom-call(s32[2]{0:T(128)} %pad_add_fusion.place.refs_0_, f32[8,128]{1,0:T(8,128)} %get-tuple-element.6.mask1.refs_1_, f32[8,128]{1,0:T(8,128)} %get-tuple-element.5.mask2.refs_2_, f32[128,512]{1,0:T(8,128)} %first.1, f32[128,512]{1,0:T(8,128)} %second.1, f32[512,512]{1,0:T(8,128)} %link.1, ...), custom_call_target="tpu_custom_call" | custom-call | flops 201326592 | bytes 2097152 | tf_op jit(solution)/shard_map/prepare/pallas_call | solution.py:197
  9.7 1.1 %constant_dynamic-slice_fusion.1 = f32[64,2048]{1,0:T(8,128)S(1)} fusion(f32[128,2048]{1,0:T(8,128)} %prepare.1.refs_3_, s32[]{:T(128)S(6)} %select_n.7), kind=kLoop, calls=%fused_computation.11 | loop fusion | bytes 1048580 | tf_op jit(solution)/shard_map/dynamic_slice | solution.py:215
  10.8 2.7 %collective-permute-start.2 = (f32[64,2048]{1,0:T(8,128)S(1)}, f32[64,2048]{1,0:T(8,128)S(1)}, u32[]{:S(2)}, u32[]{:S(2)}) collective-permute-start(f32[64,2048]{1,0:T(8,128)S(1)} %constant_dynamic-slice_fusion.1), channel_id=1, source_target_pairs={{0,4},{2,6},{4,8},{6,10},{8,12},{10,14},{12,0},{14,2},{1,5},{3,7},... | collective-permute-start | bytes 1572872 | tf_op jit(solution)/shard_map/ppermute | solution.py:220
  13.5 14.5 %collective-permute-done.2.refs_5_ = f32[64,2048]{1,0:T(8,128)S(1)} collective-permute-done((f32[64,2048]{1,0:T(8,128)S(1)}, f32[64,2048]{1,0:T(8,128)S(1)}, u32[]{:S(2)}, u32[]{:S(2)}) %collective-permute-start.2) | collective-permute-done | bytes 524320 | tf_op jit(solution)/shard_map/ppermute | solution.py:220
  28.0 0.0 collective-permute-start.4
  28.0 1.5 %collective-permute-start.1 = (f32[64,2048]{1,0:T(8,128)S(1)}, f32[64,2048]{1,0:T(8,128)S(1)}, u32[]{:S(2)}, u32[]{:S(2)}) collective-permute-start(f32[64,2048]{1,0:T(8,128)S(1)} %constant_dynamic-slice_fusion.1), channel_id=1, source_target_pairs={{0,2},{2,0},{4,6},{6,4},{8,10},{10,8},{12,14},{14,12},{1,3},{3,1},... | collective-permute-start | bytes 1572872 | tf_op jit(solution)/shard_map/ppermute | solution.py:218
  29.5 14.0 %collective-permute-done.4.refs_7_ = f32[64,2048]{1,0:T(8,128)S(1)} collective-permute-done((f32[64,2048]{1,0:T(8,128)S(1)}, f32[64,2048]{1,0:T(8,128)S(1)}, u32[]{:S(2)}, u32[]{:S(2)}) %collective-permute-start.4) | collective-permute-done | bytes 524320 | tf_op jit(solution)/shard_map/ppermute | solution.py:220
  43.5 0.0 collective-permute-start.6
  43.5 0.0 collective-permute-start.9
  43.5 1.3 %collective-permute-start.3 = (f32[64,2048]{1,0:T(8,128)S(1)}, f32[64,2048]{1,0:T(8,128)}, u32[]{:S(2)}, u32[]{:S(2)}) collective-permute-start(f32[64,2048]{1,0:T(8,128)S(1)} %collective-permute-done.2.refs_5_), channel_id=1, source_target_pairs={{0,2},{2,0},{4,6},{6,4},{8,10},{10,8},{12,14},{14,12},{1,3},{3,1},... | collective-permute-start | bytes 1572872 | tf_op jit(solution)/shard_map/ppermute | solution.py:221
  44.8 0.2 collective-permute-start.8
  45.0 0.8 collective-permute-start.5
  45.7 12.3 %collective-permute-done.6.refs_9_ = f32[64,2048]{1,0:T(8,128)S(1)} collective-permute-done((f32[64,2048]{1,0:T(8,128)S(1)}, f32[64,2048]{1,0:T(8,128)S(1)}, u32[]{:S(2)}, u32[]{:S(2)}) %collective-permute-start.6) | collective-permute-done | bytes 524320 | tf_op jit(solution)/shard_map/ppermute | solution.py:220
  58.1 1.1 %collective-permute-start.7 = (f32[64,2048]{1,0:T(8,128)S(1)}, f32[64,2048]{1,0:T(8,128)}, u32[]{:S(2)}, u32[]{:S(2)}) collective-permute-start(f32[64,2048]{1,0:T(8,128)S(1)} %collective-permute-done.6.refs_9_), channel_id=1, source_target_pairs={{0,2},{2,0},{4,6},{6,4},{8,10},{10,8},{12,14},{14,12},{1,3},{3,1},... | collective-permute-start | bytes 1572872 | tf_op jit(solution)/shard_map/ppermute | solution.py:221
  59.1 0.0 collective-permute-done.9.refs_12_
  59.1 0.5 collective-permute-start.10
  59.7 0.1 collective-permute-start.13
  59.7 9.9 %collective-permute-done.5.refs_8_ = f32[64,2048]{1,0:T(8,128)} collective-permute-done((f32[64,2048]{1,0:T(8,128)S(1)}, f32[64,2048]{1,0:T(8,128)}, u32[]{:S(2)}, u32[]{:S(2)}) %collective-permute-start.5) | collective-permute-done | bytes 524320 | tf_op jit(solution)/shard_map/ppermute | solution.py:221
  69.6 10.8 %collective-permute-done.7.refs_10_ = f32[64,2048]{1,0:T(8,128)} collective-permute-done((f32[64,2048]{1,0:T(8,128)S(1)}, f32[64,2048]{1,0:T(8,128)}, u32[]{:S(2)}, u32[]{:S(2)}) %collective-permute-start.7) | collective-permute-done | bytes 524320 | tf_op jit(solution)/shard_map/ppermute | solution.py:221
  80.4 3.7 %fusion.2 = f32[256,512]{1,0:T(8,128)} fusion(f32[512,512]{1,0:T(8,128)S(1)} %copy-done, f32[512,512]{1,0:T(8,128)} %link.1, s32[]{:T(128)S(6)} %select_n.8), kind=kOutput, calls=%fused_computation.5 | convolution fusion | flops 805306368 | bytes 2097156 | tf_op jit(solution)/shard_map/dot_general | solution.py:21
  84.1 2.0 %copy.15 = f32[256,512]{0,1:T(8,128)} copy(f32[256,512]{1,0:T(8,128)} %fusion.2) | data formatting | bytes 1048576 | tf_op jit(solution)/shard_map/dot_general | solution.py:21
  86.1 0.8 constant_dynamic-slice_fusion.refs_18_
  87.0 0.6 copy-done.4
  87.5 3.7 %convolution_bitcast_fusion.refs_21_ = f32[512,256]{1,0:T(8,128)} fusion(f32[256,512]{1,0:T(8,128)} %fusion.2, f32[512,512]{1,0:T(8,128)S(1)} %copy-done.4), kind=kOutput, calls=%fused_computation.2 | convolution fusion | flops 805306368 | bytes 2097152 | tf_op jit(solution)/shard_map/dot_general | solution.py:25
  91.3 11.1 %finish.1 = (f32[128,256]{1,0:T(8,128)}, f32[512,256]{1,0:T(8,128)}, f32[128,256]{1,0:T(8,128)}, f32[512,256]{1,0:T(8,128)}, f32[512,256]{1,0:T(8,128)}) custom-call(s32[2]{0:T(128)S(1)} %copy-done.3, f32[8,128]{1,0:T(8,128)S(1)} %copy-done.2, f32[8,128]{1,0:T(8,128)S(1)} %copy-done.1, f32[128,2048]{1,0:T(8,128)} %prepare.1.refs_3_, ...), custom_call_target="tpu_custom_call" | custom-call | flops 5637144576 | bytes 8388608 | tf_op jit(solution)/shard_map/finish/pallas_call | solution.py:240
  (21 shorter events, 0.0 us)
Async XLA Ops:
  0.6 79.8 %copy-start = (f32[512,512]{1,0:T(8,128)S(1)}, f32[512,512]{1,0:T(8,128)}, u32[]{:S(2)}) copy-start(f32[512,512]{1,0:T(8,128)} %param.10) | copy-start | bytes 3145732
  0.6 3.7 %collective-permute-start = (f32[8,64,128]{2,1,0:T(8,128)}, f32[8,64,128]{2,1,0:T(8,128)S(1)}, u32[]{:S(2)}, u32[]{:S(2)}) collective-permute-start(f32[8,64,128]{2,1,0:T(8,128)} %mine.1), channel_id=1, source_target_pairs={{0,1},{1,0},{2,3},{3,2},{4,5},{5,4},{6,7},{7,6},{8,9},{9,8},{10,11... | collective-permute-start | bytes 786440 | tf_op jit(solution)/shard_map/ppermute | solution.py:268
  4.3 0.7 copy-start.5
  10.8 17.2 %collective-permute-start.2 = (f32[64,2048]{1,0:T(8,128)S(1)}, f32[64,2048]{1,0:T(8,128)S(1)}, u32[]{:S(2)}, u32[]{:S(2)}) collective-permute-start(f32[64,2048]{1,0:T(8,128)S(1)} %constant_dynamic-slice_fusion.1), channel_id=1, source_target_pairs={{0,4},{2,6},{4,8},{6,10},{8,12},{10,14},{12,0},{14,2},{1,5},{3,7},... | collective-permute-start | bytes 1572872 | tf_op jit(solution)/shard_map/ppermute | solution.py:220
  28.0 15.5 %collective-permute-start.4 = (f32[64,2048]{1,0:T(8,128)S(1)}, f32[64,2048]{1,0:T(8,128)S(1)}, u32[]{:S(2)}, u32[]{:S(2)}) collective-permute-start(f32[64,2048]{1,0:T(8,128)S(1)} %collective-permute-done.2.refs_5_), channel_id=1, source_target_pairs={{0,4},{2,6},{4,8},{6,10},{8,12},{10,14},{12,0},{14,2},{1,5},{3,7},... | collective-permute-start | bytes 1572872 | tf_op jit(solution)/shard_map/ppermute | solution.py:220
  28.0 16.8 %collective-permute-start.1 = (f32[64,2048]{1,0:T(8,128)S(1)}, f32[64,2048]{1,0:T(8,128)S(1)}, u32[]{:S(2)}, u32[]{:S(2)}) collective-permute-start(f32[64,2048]{1,0:T(8,128)S(1)} %constant_dynamic-slice_fusion.1), channel_id=1, source_target_pairs={{0,2},{2,0},{4,6},{6,4},{8,10},{10,8},{12,14},{14,12},{1,3},{3,1},... | collective-permute-start | bytes 1572872 | tf_op jit(solution)/shard_map/ppermute | solution.py:218
  43.5 14.6 %collective-permute-start.6 = (f32[64,2048]{1,0:T(8,128)S(1)}, f32[64,2048]{1,0:T(8,128)S(1)}, u32[]{:S(2)}, u32[]{:S(2)}) collective-permute-start(f32[64,2048]{1,0:T(8,128)S(1)} %collective-permute-done.4.refs_7_), channel_id=1, source_target_pairs={{0,4},{2,6},{4,8},{6,10},{8,12},{10,14},{12,0},{14,2},{1,5},{3,7},... | collective-permute-start | bytes 1572872 | tf_op jit(solution)/shard_map/ppermute | solution.py:220
  43.5 15.7 %collective-permute-start.9 = (f32[64,2048]{1,0:T(8,128)S(1)}, f32[64,2048]{1,0:T(8,128)}, u32[]{:S(2)}, u32[]{:S(2)}) collective-permute-start(f32[64,2048]{1,0:T(8,128)S(1)} %collective-permute-done.2.refs_5_), channel_id=1, source_target_pairs={{0,1},{1,0},{2,3},{3,2},{4,5},{5,4},{6,7},{7,6},{8,9},{9,8},{10,11... | collective-permute-start | bytes 1572872 | tf_op jit(solution)/shard_map/ppermute | solution.py:228
  43.5 15.7 %collective-permute-start.3 = (f32[64,2048]{1,0:T(8,128)S(1)}, f32[64,2048]{1,0:T(8,128)}, u32[]{:S(2)}, u32[]{:S(2)}) collective-permute-start(f32[64,2048]{1,0:T(8,128)S(1)} %collective-permute-done.2.refs_5_), channel_id=1, source_target_pairs={{0,2},{2,0},{4,6},{6,4},{8,10},{10,8},{12,14},{14,12},{1,3},{3,1},... | collective-permute-start | bytes 1572872 | tf_op jit(solution)/shard_map/ppermute | solution.py:221
  44.8 14.9 %collective-permute-start.8 = (f32[64,2048]{1,0:T(8,128)S(1)}, f32[64,2048]{1,0:T(8,128)}, u32[]{:S(2)}, u32[]{:S(2)}) collective-permute-start(f32[64,2048]{1,0:T(8,128)S(1)} %collective-permute-done.1.refs_4_), channel_id=1, source_target_pairs={{0,1},{1,0},{2,3},{3,2},{4,5},{5,4},{6,7},{7,6},{8,9},{9,8},{10,11... | collective-permute-start | bytes 1572872 | tf_op jit(solution)/shard_map/ppermute | solution.py:228
  45.0 24.6 %collective-permute-start.5 = (f32[64,2048]{1,0:T(8,128)S(1)}, f32[64,2048]{1,0:T(8,128)}, u32[]{:S(2)}, u32[]{:S(2)}) collective-permute-start(f32[64,2048]{1,0:T(8,128)S(1)} %collective-permute-done.4.refs_7_), channel_id=1, source_target_pairs={{0,2},{2,0},{4,6},{6,4},{8,10},{10,8},{12,14},{14,12},{1,3},{3,1},... | collective-permute-start | bytes 1572872 | tf_op jit(solution)/shard_map/ppermute | solution.py:221
  58.1 22.3 %collective-permute-start.7 = (f32[64,2048]{1,0:T(8,128)S(1)}, f32[64,2048]{1,0:T(8,128)}, u32[]{:S(2)}, u32[]{:S(2)}) collective-permute-start(f32[64,2048]{1,0:T(8,128)S(1)} %collective-permute-done.6.refs_9_), channel_id=1, source_target_pairs={{0,2},{2,0},{4,6},{6,4},{8,10},{10,8},{12,14},{14,12},{1,3},{3,1},... | collective-permute-start | bytes 1572872 | tf_op jit(solution)/shard_map/ppermute | solution.py:221
  59.1 32.1 %collective-permute-start.11 = (f32[64,2048]{1,0:T(8,128)S(1)}, f32[64,2048]{1,0:T(8,128)}, u32[]{:S(2)}, u32[]{:S(2)}) collective-permute-start(f32[64,2048]{1,0:T(8,128)S(1)} %collective-permute-done.4.refs_7_), channel_id=1, source_target_pairs={{0,1},{1,0},{2,3},{3,2},{4,5},{5,4},{6,7},{7,6},{8,9},{9,8},{10,11... | collective-permute-start | bytes 1572872 | tf_op jit(solution)/shard_map/ppermute | solution.py:228
  59.1 32.1 %collective-permute-start.10 = (f32[64,2048]{1,0:T(8,128)}, f32[64,2048]{1,0:T(8,128)}, u32[]{:S(2)}, u32[]{:S(2)}) collective-permute-start(f32[64,2048]{1,0:T(8,128)} %collective-permute-done.3.refs_6_), channel_id=1, source_target_pairs={{0,1},{1,0},{2,3},{3,2},{4,5},{5,4},{6,7},{7,6},{8,9},{9,8},{10,11... | collective-permute-start | bytes 1572872 | tf_op jit(solution)/shard_map/ppermute | solution.py:228
  59.7 31.6 %collective-permute-start.13 = (f32[64,2048]{1,0:T(8,128)S(1)}, f32[64,2048]{1,0:T(8,128)}, u32[]{:S(2)}, u32[]{:S(2)}) collective-permute-start(f32[64,2048]{1,0:T(8,128)S(1)} %collective-permute-done.6.refs_9_), channel_id=1, source_target_pairs={{0,1},{1,0},{2,3},{3,2},{4,5},{5,4},{6,7},{7,6},{8,9},{9,8},{10,11... | collective-permute-start | bytes 1572872 | tf_op jit(solution)/shard_map/ppermute | solution.py:228
  69.6 21.7 %collective-permute-start.12 = (f32[64,2048]{1,0:T(8,128)}, f32[64,2048]{1,0:T(8,128)}, u32[]{:S(2)}, u32[]{:S(2)}) collective-permute-start(f32[64,2048]{1,0:T(8,128)} %collective-permute-done.5.refs_8_), channel_id=1, source_target_pairs={{0,1},{1,0},{2,3},{3,2},{4,5},{5,4},{6,7},{7,6},{8,9},{9,8},{10,11... | collective-permute-start | bytes 1572872 | tf_op jit(solution)/shard_map/ppermute | solution.py:228
  80.4 10.9 %collective-permute-start.14 = (f32[64,2048]{1,0:T(8,128)}, f32[64,2048]{1,0:T(8,128)}, u32[]{:S(2)}, u32[]{:S(2)}) collective-permute-start(f32[64,2048]{1,0:T(8,128)} %collective-permute-done.7.refs_10_), channel_id=1, source_target_pairs={{0,1},{1,0},{2,3},{3,2},{4,5},{5,4},{6,7},{7,6},{8,9},{9,8},{10,11... | collective-permute-start | bytes 1572872 | tf_op jit(solution)/shard_map/ppermute | solution.py:228
  86.1 1.4 %copy-start.4 = (f32[512,512]{1,0:T(8,128)S(1)}, f32[512,512]{1,0:T(8,128)}, u32[]{:S(2)}) copy-start(f32[512,512]{1,0:T(8,128)} %link.1) | copy-start | bytes 3145732
  87.5 3.8 %copy-start.1 = (f32[8,128]{1,0:T(8,128)S(1)}, f32[8,128]{1,0:T(8,128)}, u32[]{:S(2)}) copy-start(f32[8,128]{1,0:T(8,128)} %get-tuple-element.5.mask2.refs_2_) | copy-start | bytes 12292
  87.5 3.8 %copy-start.2 = (f32[8,128]{1,0:T(8,128)S(1)}, f32[8,128]{1,0:T(8,128)}, u32[]{:S(2)}) copy-start(f32[8,128]{1,0:T(8,128)} %get-tuple-element.6.mask1.refs_1_) | copy-start | bytes 12292
  87.5 3.8 %copy-start.3 = (s32[2]{0:T(128)S(1)}, s32[2]{0:T(128)}, u32[]{:S(2)}) copy-start(s32[2]{0:T(128)} %pad_add_fusion.place.refs_0_) | copy-start | bytes 28

commit v2 on v1

--- a/solution.py
+++ b/solution.py
@@ -6,6 +6,7 @@
 from jax.experimental import pallas as pl
 from jax.experimental.pallas import tpu as pltpu
 from jax.sharding import PartitionSpec as P
+
 
 HIGH = lax.Precision.HIGHEST
 F32, BF16 = jnp.float32, jnp.bfloat16
@@ -98,7 +99,7 @@
     return ((at == code_row) & (code_row >= 0)).astype(BF16)
 
 
-def prepare_kernel(cap, place, mask1, mask2, first, second, link, mine, theirs, out, code, m2, cols):
+def prepare_kernel(cap, place, mask1, mask2, first, second, link, mine, theirs, out, out_half, code, m2, cols):
     row, col = place[0], place[1]
     groups, share, block = mine.shape
     width = first.shape[1]
@@ -121,6 +122,8 @@
         spread = picker(code[g : g + 1, :], wide, g * cap)
         total += dot2(spread, split(half[:, g * block : (g + 1) * block]), NT, flip=True)
     out[:, 2 * width :] = total
+    half_cap = cap // 2
+    out_half[...] = out[pl.ds(pl.multiple_of(col * half_cap, 8), half_cap), :]
 
 
 def finish_kernel(cap, sources, *refs):
@@ -188,17 +191,27 @@
         copy.wait()
 
 
-def gather_branch(cap, n, place, mask1, mask2, known_inverse, theirs, first_factor, second_factor, second_link, corner1, second_corner, cross0, diag0):
-    groups, share, block = known_inverse.shape
+def side_kernel(place, corner, link, corner_half, cross0, diag0, link_half):
+    half_width = cross0.shape[1]
+    start = pl.multiple_of(place[1] * half_width, half_width)
+    corner_half[...] = corner[:, pl.ds(start, half_width)]
+    link_half[...] = link[:, pl.ds(start, half_width)]
+    value = dot3(split(corner[...]), split(link_half[...]), NN)
+    cross0[...] = value
+    diag0[...] = dot3(split(link[...]), split(value), TN)
+
+
+def gather_branch(cap, n, place, mask1, mask2, known_inverse, theirs, first_factor, second_factor, second_link, first_corner, second_corner):
+    _, _, block = known_inverse.shape
     width = first_factor.shape[1]
     half_width = second_corner.shape[1]
     wide = -(-n * cap // 128) * 128
     cost = pl.CostEstimate(flops=2 * cap * width * (width + n * block), bytes_accessed=4 * width * width * 2, transcendentals=0)
-    payload = pl.pallas_call(
+    payload, own_half = pl.pallas_call(
         functools.partial(prepare_kernel, cap),
-        out_shape=jax.ShapeDtypeStruct((cap, 2 * width + wide), F32),
+        out_shape=(jax.ShapeDtypeStruct((cap, 2 * width + wide), F32), jax.ShapeDtypeStruct((cap // 2, 2 * width + wide), F32)),
         in_specs=[SMEM] + [VMEM] * 7,
-        out_specs=VMEM,
+        out_specs=(VMEM, VMEM),
         scratch_shapes=[
             pltpu.VMEM((n, block), jnp.int32),
             pltpu.VMEM((n, block), F32),
@@ -208,24 +221,36 @@
         name="prepare",
     )(place, mask1, mask2, first_factor, second_factor, second_link, known_inverse, theirs)
 
-    half = cap // 2
     ring = [(r, (r + 2) % n) for r in range(n)]
     pair = [(r, r ^ 1) for r in range(n)]
     swap = [(0, 1), (1, 0)]
-    own_half = lax.dynamic_slice_in_dim(payload, lax.axis_index("col") * half, half, 0)
+
     along = [own_half]
     sources, near = [], []
     across = [lax.ppermute(own_half, "row", pair)]
-    for step in range(1, n // 2):
+    for _ in range(1, n // 2):
         along.append(lax.ppermute(along[-1], "row", ring))
         across.append(lax.ppermute(along[-1], "row", pair))
+    far = []
     for step in range(n // 2):
         if step:
             near.append(along[step])
+            far.append(lax.ppermute(along[step], "col", swap))
             sources.append(lambda r, s=step: lax.rem(r - 2 * s + n, n))
         near.append(across[step])
+        far.append(lax.ppermute(across[step], "col", swap))
         sources.append(lambda r, s=step: lax.rem(lax.rem(r, 2) * -2 + 1 + r - 2 * s + n, n))
-    far = [lax.ppermute(v, "col", swap) for v in near]
+
+    square = jax.ShapeDtypeStruct((width, half_width), F32)
+    corner_half, cross0, diag0 = pl.pallas_call(
+        side_kernel,
+        out_shape=(square, square, square),
+        in_specs=[SMEM] + [VMEM] * 2,
+        out_specs=(VMEM, VMEM, VMEM),
+        scratch_shapes=[pltpu.VMEM((width, half_width), F32)],
+        cost_estimate=pl.CostEstimate(flops=12 * width * width * half_width, bytes_accessed=20 * width * width, transcendentals=0),
+        name="side",
+    )(place, first_corner, second_link)
 
     rows = wide
     outs = (
@@ -257,30 +282,37 @@
         compiler_params=pltpu.CompilerParams(vmem_limit_bytes=48 << 20),
         cost_estimate=cost,
         name="finish",
-    )(place, mask1, mask2, payload, *near, *far, corner1, second_corner, cross0, diag0)
+    )(place, mask1, mask2, payload, *near, *far, corner_half, second_corner, cross0, diag0)
 
 
 def gather_plan(n, known_inverse, first_factor, first_corner, first_ancestors, second_factor, second_link, second_corner, second_ancestors):
-    groups, share, block = known_inverse.shape
-    half_width = second_corner.shape[1]
+    _, _, block = known_inverse.shape
     row, col = lax.axis_index("row"), lax.axis_index("col")
     place = jnp.stack([row, col]).astype(jnp.int32)
     theirs = lax.ppermute(known_inverse, "col", [(0, 1), (1, 0)])
     mask1 = mask_of(first_ancestors, 0, n * block).reshape(n, block)
     mask2 = mask_of(second_ancestors, 0, n * block).reshape(n, block)
-    start = col * half_width
-    corner1 = lax.dynamic_slice_in_dim(first_corner, start, half_width, 1)
-    link_half = lax.dynamic_slice_in_dim(second_link, start, half_width, 1)
-    cross0 = product(first_corner, link_half)
-    diag0 = transposed_product(second_link, cross0)
-    return gather_branch(block, n, place, mask1, mask2, known_inverse, theirs, first_factor, second_factor, second_link, corner1, second_corner, cross0, diag0)
+    mean = -(-first_ancestors.shape[0] // n)
+    cap = -(-mean * 5 // 64) * 16
+    operands = (place, mask1, mask2, known_inverse, theirs, first_factor, second_factor, second_link, first_corner, second_corner)
+
+    def branch(slots):
+        def run(*values):
+            return gather_branch(slots, n, *values)
+
+        return run
+
+    if cap >= block:
+        return branch(block)(*operands)
+    fits = jnp.max(jnp.sum(mask1, axis=1)) <= cap
+    return lax.cond(fits, branch(cap), branch(block), *operands)
 
 
 def solution(mesh):
     n = mesh.shape["row"]
 
     def on_device(known_inverse, *rest):
-        groups, share, block = known_inverse.shape
+        _, _, block = known_inverse.shape
         width = rest[0].shape[1]
         if n % 2 == 0 and mesh.shape["col"] == 2 and (n * block) ** 2 <= 12 * width**2:
             return gather_plan(n, known_inverse, *rest)

time: 103 us -> 66.2 us (0.64)
  waiting for transfers between devices: 61.5 us -> 34 us
  matrix products: 7.43 us -> 0 us
  local copies, waits for them, and re-layouts: 5.24 us -> 3.88 us
  Pallas kernels: 15.8 us -> 14.6 us
    ppermute x3, waiting for transfers between devices: 40.8 us -> 24.5 us  [gather_branch(): along.append(lax.ppermute(along[-1], 'row', ring))]
    ppermute x3, waiting for transfers between devices: 20.7 us -> 9.49 us  [gather_branch(): across.append(lax.ppermute(along[-1], 'row', pair))]
    dot_general x2 -> x0, matrix products: 7.43 us -> none  [the longest x1 3.73 us: transposed_product(): lax.dot_general(left, right, TN, precision=HIGH, preferred_element_type=F32)]
    pallas_call x1, Pallas kernels: 11.1 us -> 6.34 us  [gather_branch(): pl.pallas_call(functools.partial(finish_kernel, cap, sources), out_shape=...]
    cond x0 -> x18, local copies, waits for them, and re-layouts: none -> 3.77 us
    pallas_call x1 -> x2, Pallas kernels: 4.66 us -> 8.23 us  [the longest x1 4.34 us: gather_branch(): pl.pallas_call(side_kernel, out_shape=(square, square, square), in_specs=...]
    dot_general x1 -> x0, local copies, waits for them, and re-layouts: 2.03 us -> none  [product(): return jnp.dot(left, right, precision=HIGH, preferred_element_type=F32)]
    dynamic_slice x2 -> x0, local copies, waits for them, and re-layouts: 1.92 us -> none  [the longest x1 1.08 us: gather_branch(): lax.dynamic_slice_in_dim(payload, lax.axis_index('col') * half, half, 0)]
  transfers between devices with their start and end apart: 15 -> 15, of which waited for: 5 -> 5; matrix products, arithmetic and copies ran while one was open for 13% -> 3% of each run, Pallas kernels for 0% -> 7%
where the time goes in v2:
time: 66.2 us; the launch traced here: 65.8 us
  waiting for transfers between devices  34 us (51%)
  Pallas kernels  14.6 us (22%)
  starting transfers between devices  8.62 us (13%)
  local copies, waits for them, and re-layouts  3.88 us (6%)
  other arithmetic  2.66 us (4%)
  between operations  1.52 us (2%)
    ppermute x3, waiting for transfers between devices, gather_branch(): along.append(lax.ppermute(along[-1], 'row', ring))  24.5 us
    ppermute x3, waiting for transfers between devices, gather_branch(): across.append(lax.ppermute(along[-1], 'row', pair))  9.49 us
    pallas_call x1, Pallas kernels, gather_branch(): pl.pallas_call(functools.partial(finish_kernel, cap, sources), out_shape=...  6.34 us
    pallas_call x1, Pallas kernels, gather_branch(): pl.pallas_call(side_kernel, out_shape=(square, square, square), in_specs=...  4.34 us
    pallas_call x1, Pallas kernels, gather_branch(): pl.pallas_call(functools.partial(prepare_kernel, cap), out_shape=(jax.Sha...  3.89 us
    cond x18, local copies, waits for them, and re-layouts  3.77 us
    ppermute x3, starting transfers between devices, gather_branch(): across.append(lax.ppermute(along[-1], 'row', pair))  3.09 us
    ppermute x3, starting transfers between devices, gather_branch(): along.append(lax.ppermute(along[-1], 'row', ring))  2.66 us
  transfers between devices with their start and end apart: 15, of which 5 were waited for; matrix products, arithmetic and copies ran while one was open for 3% of the time, Pallas kernels for 7%

profile of v2, /device:TPU:0, one launch (start us, length us, event | category | flops | bytes accessed | tf_op | source)
XLA Modules:
  0.0 65.8 jit_solution(8101831967525105960)
XLA Ops:
  0.7 0.6 collective-permute-start.28
  1.2 1.0 %fusion = pred[1024]{0:T(1024)(128)(4,1)S(1)} fusion(s32[512]{0:T(512)} %param.13), kind=kLoop, calls=%fused_computation.5 | loop fusion | flops 1047552 | bytes 3072 | tf_op jit(solution)/shard_map/reduce_or | solution.py:31
  2.2 0.1 fusion.1
  2.4 0.1 pad_add_fusion
  2.4 0.6 reduce_max.9
  3.7 0.1 eq.30
  3.9 61.7 %conditional.1 = ((f32[128,256]{1,0:T(8,128)}, f32[512,256]{1,0:T(8,128)}, f32[128,256]{1,0:T(8,128)}, f32[512,256]{1,0:T(8,128)}, f32[512,256]{1,0:T(8,128)})) conditional(s32[]{:T(128)} %convert_element_type.19, (s32[2]{0:T(128)S(1)}, f32[8,128]{1,0:T(8,128)S(1)}, s32[256]{0:T(256)S(1)}, f32[128,512]{1,0:T(8,128)}, f32[128,512]{1,0:T(8,128)}, ...), branch_computations={%region_4.0_spmd, %region_5.0_spmd} | conditional | flops 6644301824 | bytes 57695996 | solution.py:308
  4.1 0.0 copy-start.16
  4.1 0.2 compare_reduce_fusion.1
  4.3 0.6 convert_bitcast_fusion.1.mask2.refs_2_
  4.9 0.3 copy-done.12
  5.2 0.3 copy-done.14
  5.5 0.1 copy-done.16
  5.6 3.9 %prepare.3 = (f32[80,1664]{1,0:T(8,128)}, f32[40,1664]{1,0:T(8,128)}) custom-call(s32[2]{0:T(128)S(1)} %get-tuple-element.55.place.refs_0_, f32[8,128]{1,0:T(8,128)S(1)} %get-tuple-element.56.mask1.refs_1_, f32[8,128]{1,0:T(8,128)} %convert_bitcast_fusion.1.mask2.refs_2_, f32[128,512]{1,0:T(8,128)S(1)} %copy-done.12, f32[128,512]{1,0:T(8,128)S(1)} %copy-done.14, ...), custom_call_target="tpu_custom_call" | custom-call | flops 125829120 | bytes 2097152 | tf_op jit(solution)/shard_map/cond/branch_1_fun/prepare/pallas_call | solution.py:210
  9.5 2.7 %collective-permute-start.15 = (f32[40,1664]{1,0:T(8,128)}, f32[40,1664]{1,0:T(8,128)S(1)}, u32[]{:S(2)}, u32[]{:S(2)}) collective-permute-start(f32[40,1664]{1,0:T(8,128)} %get-tuple-element.64), channel_id=1, source_target_pairs={{0,4},{2,6},{4,8},{6,10},{8,12},{10,14},{12,0},{14,2},{1,5},{3,7},... | collective-permute-start | bytes 798728 | tf_op jit(solution)/shard_map/cond/branch_1_fun/ppermute | solution.py:232
  12.1 9.2 %collective-permute-done.15.refs_5_ = f32[40,1664]{1,0:T(8,128)S(1)} collective-permute-done((f32[40,1664]{1,0:T(8,128)}, f32[40,1664]{1,0:T(8,128)S(1)}, u32[]{:S(2)}, u32[]{:S(2)}) %collective-permute-start.15) | collective-permute-done | bytes 266272 | tf_op jit(solution)/shard_map/cond/branch_1_fun/ppermute | solution.py:232
  21.3 1.5 %collective-permute-start.14 = (f32[40,1664]{1,0:T(8,128)}, f32[40,1664]{1,0:T(8,128)S(1)}, u32[]{:S(2)}, u32[]{:S(2)}) collective-permute-start(f32[40,1664]{1,0:T(8,128)} %get-tuple-element.64), channel_id=1, source_target_pairs={{0,2},{2,0},{4,6},{6,4},{8,10},{10,8},{12,14},{14,12},{1,3},{3,1},... | collective-permute-start | bytes 798728 | tf_op jit(solution)/shard_map/cond/branch_1_fun/ppermute | solution.py:230
  22.8 8.4 %collective-permute-done.17.refs_7_ = f32[40,1664]{1,0:T(8,128)S(1)} collective-permute-done((f32[40,1664]{1,0:T(8,128)S(1)}, f32[40,1664]{1,0:T(8,128)S(1)}, u32[]{:S(2)}, u32[]{:S(2)}) %collective-permute-start.17) | collective-permute-done | bytes 266272 | tf_op jit(solution)/shard_map/cond/branch_1_fun/ppermute | solution.py:232
  31.3 1.3 %collective-permute-start.16 = (f32[40,1664]{1,0:T(8,128)S(1)}, f32[40,1664]{1,0:T(8,128)S(1)}, u32[]{:S(2)}, u32[]{:S(2)}) collective-permute-start(f32[40,1664]{1,0:T(8,128)S(1)} %collective-permute-done.15.refs_5_), channel_id=1, source_target_pairs={{0,2},{2,0},{4,6},{6,4},{8,10},{10,8},{12,14},{14,12},{1,3},{3,1},... | collective-permute-start | bytes 798728 | tf_op jit(solution)/shard_map/cond/branch_1_fun/ppermute | solution.py:233
  32.5 0.2 collective-permute-start.21
  32.8 0.7 %collective-permute-start.18 = (f32[40,1664]{1,0:T(8,128)S(1)}, f32[40,1664]{1,0:T(8,128)S(1)}, u32[]{:S(2)}, u32[]{:S(2)}) collective-permute-start(f32[40,1664]{1,0:T(8,128)S(1)} %collective-permute-done.17.refs_7_), channel_id=1, source_target_pairs={{0,2},{2,0},{4,6},{6,4},{8,10},{10,8},{12,14},{14,12},{1,3},{3,1},... | collective-permute-start | bytes 798728 | tf_op jit(solution)/shard_map/cond/branch_1_fun/ppermute | solution.py:233
  33.5 6.8 %collective-permute-done.19.refs_9_ = f32[40,1664]{1,0:T(8,128)S(1)} collective-permute-done((f32[40,1664]{1,0:T(8,128)S(1)}, f32[40,1664]{1,0:T(8,128)S(1)}, u32[]{:S(2)}, u32[]{:S(2)}) %collective-permute-start.19) | collective-permute-done | bytes 266272 | tf_op jit(solution)/shard_map/cond/branch_1_fun/ppermute | solution.py:232
  40.3 1.1 %collective-permute-start.20 = (f32[40,1664]{1,0:T(8,128)S(1)}, f32[40,1664]{1,0:T(8,128)S(1)}, u32[]{:S(2)}, u32[]{:S(2)}) collective-permute-start(f32[40,1664]{1,0:T(8,128)S(1)} %collective-permute-done.19.refs_9_), channel_id=1, source_target_pairs={{0,2},{2,0},{4,6},{6,4},{8,10},{10,8},{12,14},{14,12},{1,3},{3,1},... | collective-permute-start | bytes 798728 | tf_op jit(solution)/shard_map/cond/branch_1_fun/ppermute | solution.py:233
  41.4 0.5 collective-permute-start.23
  41.9 0.1 collective-permute-start.26
  42.0 4.2 %collective-permute-done.18.refs_8_ = f32[40,1664]{1,0:T(8,128)S(1)} collective-permute-done((f32[40,1664]{1,0:T(8,128)S(1)}, f32[40,1664]{1,0:T(8,128)S(1)}, u32[]{:S(2)}, u32[]{:S(2)}) %collective-permute-start.18) | collective-permute-done | bytes 266272 | tf_op jit(solution)/shard_map/cond/branch_1_fun/ppermute | solution.py:233
  46.2 5.2 %collective-permute-done.20.refs_10_ = f32[40,1664]{1,0:T(8,128)S(1)} collective-permute-done((f32[40,1664]{1,0:T(8,128)S(1)}, f32[40,1664]{1,0:T(8,128)S(1)}, u32[]{:S(2)}, u32[]{:S(2)}) %collective-permute-start.20) | collective-permute-done | bytes 266272 | tf_op jit(solution)/shard_map/cond/branch_1_fun/ppermute | solution.py:233
  51.5 4.3 %side.3 = (f32[512,256]{1,0:T(8,128)}, f32[512,256]{1,0:T(8,128)}, f32[512,256]{1,0:T(8,128)}) custom-call(s32[2]{0:T(128)S(1)} %get-tuple-element.55.place.refs_0_, f32[512,512]{1,0:T(8,128)} %get-tuple-element.111.corner, f32[512,512]{1,0:T(8,128)} %copy-done.10), custom_call_target="tpu_custom_call" | custom-call | flops 805306368 | bytes 5242880 | tf_op jit(solution)/shard_map/cond/branch_1_fun/side/pallas_call | solution.py:245
  55.9 1.0 %copy-done.5 = f32[512,256]{1,0:T(8,128)S(1)} copy-done((f32[512,256]{1,0:T(8,128)S(1)}, f32[512,256]{1,0:T(8,128)}, u32[]{:S(2)}) %copy-start.5) | copy-done | bytes 524312 | tf_op jit(solution)/shard_map/cond
  56.9 1.0 %copy-done.6 = f32[512,256]{1,0:T(8,128)S(1)} copy-done((f32[512,256]{1,0:T(8,128)S(1)}, f32[512,256]{1,0:T(8,128)}, u32[]{:S(2)}) %copy-start.6) | copy-done | bytes 524312 | tf_op jit(solution)/shard_map/cond
  58.0 1.0 %copy-done.7 = f32[512,256]{1,0:T(8,128)S(1)} copy-done((f32[512,256]{1,0:T(8,128)S(1)}, f32[512,256]{1,0:T(8,128)}, u32[]{:S(2)}) %copy-start.7) | copy-done | bytes 524312 | tf_op jit(solution)/shard_map/cond
  59.0 6.3 %finish.3 = (f32[128,256]{1,0:T(8,128)}, f32[512,256]{1,0:T(8,128)}, f32[128,256]{1,0:T(8,128)}, f32[512,256]{1,0:T(8,128)}, f32[512,256]{1,0:T(8,128)}) custom-call(s32[2]{0:T(128)S(1)} %get-tuple-element.55.place.refs_0_, f32[8,128]{1,0:T(8,128)S(1)} %get-tuple-element.56.mask1.refs_1_, f32[8,128]{1,0:T(8,128)S(1)} %copy-done.1, f32[80,1664]{1,0:T(8,128)S(1)} %copy-done.2, ...), custom_call_target="tpu_custom_call" | custom-call | flops 2768240640 | bytes 4259840 | tf_op jit(solution)/shard_map/cond/branch_1_fun/finish/pallas_call | solution.py:265
  (32 shorter events, 0.1 us)
Async XLA Ops:
  0.6 3.2 %copy-start.17 = (s32[256]{0:T(256)S(1)}, s32[256]{0:T(256)}, u32[]{:S(2)}) copy-start(s32[256]{0:T(256)} %param.17) | copy-start | bytes 3076
  0.6 3.2 %copy-start.8 = (f32[512,512]{1,0:T(8,128)S(1)}, f32[512,512]{1,0:T(8,128)}, u32[]{:S(2)}) copy-start(f32[512,512]{1,0:T(8,128)} %param.15) | copy-start | bytes 3145732
  0.7 3.1 %collective-permute-start.28 = (f32[8,64,128]{2,1,0:T(8,128)}, f32[8,64,128]{2,1,0:T(8,128)}, u32[]{:S(2)}, u32[]{:S(2)}) collective-permute-start(f32[8,64,128]{2,1,0:T(8,128)} %param.10), channel_id=1, source_target_pairs={{0,1},{1,0},{2,3},{3,2},{4,5},{5,4},{6,7},{7,6},{8,9},{9,8},{10,11... | collective-permute-start | bytes 786440 | tf_op jit(solution)/shard_map/ppermute | solution.py:292
  4.1 5.4 %copy-start.10 = (f32[512,512]{1,0:T(8,128)}, f32[512,512]{1,0:T(8,128)S(1)}, u32[]{:S(2)}) copy-start(f32[512,512]{1,0:T(8,128)S(1)} %get-tuple-element.109.link) | copy-start | bytes 3145732 | tf_op jit(solution)/shard_map/cond
  4.1 1.1 %copy-start.12 = (f32[128,512]{1,0:T(8,128)S(1)}, f32[128,512]{1,0:T(8,128)}, u32[]{:S(2)}) copy-start(f32[128,512]{1,0:T(8,128)} %get-tuple-element.105.first) | copy-start | bytes 786436 | tf_op jit(solution)/shard_map/cond
  4.1 1.4 %copy-start.14 = (f32[128,512]{1,0:T(8,128)S(1)}, f32[128,512]{1,0:T(8,128)}, u32[]{:S(2)}) copy-start(f32[128,512]{1,0:T(8,128)} %get-tuple-element.107.second) | copy-start | bytes 786436 | tf_op jit(solution)/shard_map/cond
  4.1 1.5 %copy-start.16 = (f32[8,64,128]{2,1,0:T(8,128)S(1)}, f32[8,64,128]{2,1,0:T(8,128)}, u32[]{:S(2)}) copy-start(f32[8,64,128]{2,1,0:T(8,128)} %get-tuple-element.61.mine) | copy-start | bytes 786436 | tf_op jit(solution)/shard_map/cond
  9.5 11.9 %collective-permute-start.15 = (f32[40,1664]{1,0:T(8,128)}, f32[40,1664]{1,0:T(8,128)S(1)}, u32[]{:S(2)}, u32[]{:S(2)}) collective-permute-start(f32[40,1664]{1,0:T(8,128)} %get-tuple-element.64), channel_id=1, source_target_pairs={{0,4},{2,6},{4,8},{6,10},{8,12},{10,14},{12,0},{14,2},{1,5},{3,7},... | collective-permute-start | bytes 798728 | tf_op jit(solution)/shard_map/cond/branch_1_fun/ppermute | solution.py:232
  21.3 9.9 %collective-permute-start.17 = (f32[40,1664]{1,0:T(8,128)S(1)}, f32[40,1664]{1,0:T(8,128)S(1)}, u32[]{:S(2)}, u32[]{:S(2)}) collective-permute-start(f32[40,1664]{1,0:T(8,128)S(1)} %collective-permute-done.15.refs_5_), channel_id=1, source_target_pairs={{0,4},{2,6},{4,8},{6,10},{8,12},{10,14},{12,0},{14,2},{1,5},{3,7},... | collective-permute-start | bytes 798728 | tf_op jit(solution)/shard_map/cond/branch_1_fun/ppermute | solution.py:232
  21.3 11.2 %collective-permute-start.14 = (f32[40,1664]{1,0:T(8,128)}, f32[40,1664]{1,0:T(8,128)S(1)}, u32[]{:S(2)}, u32[]{:S(2)}) collective-permute-start(f32[40,1664]{1,0:T(8,128)} %get-tuple-element.64), channel_id=1, source_target_pairs={{0,2},{2,0},{4,6},{6,4},{8,10},{10,8},{12,14},{14,12},{1,3},{3,1},... | collective-permute-start | bytes 798728 | tf_op jit(solution)/shard_map/cond/branch_1_fun/ppermute | solution.py:230
  31.2 9.1 %collective-permute-start.19 = (f32[40,1664]{1,0:T(8,128)S(1)}, f32[40,1664]{1,0:T(8,128)S(1)}, u32[]{:S(2)}, u32[]{:S(2)}) collective-permute-start(f32[40,1664]{1,0:T(8,128)S(1)} %collective-permute-done.17.refs_7_), channel_id=1, source_target_pairs={{0,4},{2,6},{4,8},{6,10},{8,12},{10,14},{12,0},{14,2},{1,5},{3,7},... | collective-permute-start | bytes 798728 | tf_op jit(solution)/shard_map/cond/branch_1_fun/ppermute | solution.py:232
  31.3 10.1 %collective-permute-start.22 = (f32[40,1664]{1,0:T(8,128)S(1)}, f32[40,1664]{1,0:T(8,128)S(1)}, u32[]{:S(2)}, u32[]{:S(2)}) collective-permute-start(f32[40,1664]{1,0:T(8,128)S(1)} %collective-permute-done.15.refs_5_), channel_id=1, source_target_pairs={{0,1},{1,0},{2,3},{3,2},{4,5},{5,4},{6,7},{7,6},{8,9},{9,8},{10,11... | collective-permute-start | bytes 798728 | tf_op jit(solution)/shard_map/cond/branch_1_fun/ppermute | solution.py:238
  31.3 10.1 %collective-permute-start.16 = (f32[40,1664]{1,0:T(8,128)S(1)}, f32[40,1664]{1,0:T(8,128)S(1)}, u32[]{:S(2)}, u32[]{:S(2)}) collective-permute-start(f32[40,1664]{1,0:T(8,128)S(1)} %collective-permute-done.15.refs_5_), channel_id=1, source_target_pairs={{0,2},{2,0},{4,6},{6,4},{8,10},{10,8},{12,14},{14,12},{1,3},{3,1},... | collective-permute-start | bytes 798728 | tf_op jit(solution)/shard_map/cond/branch_1_fun/ppermute | solution.py:233
  32.5 9.4 %collective-permute-start.21 = (f32[40,1664]{1,0:T(8,128)S(1)}, f32[40,1664]{1,0:T(8,128)S(1)}, u32[]{:S(2)}, u32[]{:S(2)}) collective-permute-start(f32[40,1664]{1,0:T(8,128)S(1)} %collective-permute-done.14.refs_4_), channel_id=1, source_target_pairs={{0,1},{1,0},{2,3},{3,2},{4,5},{5,4},{6,7},{7,6},{8,9},{9,8},{10,11... | collective-permute-start | bytes 798728 | tf_op jit(solution)/shard_map/cond/branch_1_fun/ppermute | solution.py:241
  32.8 13.5 %collective-permute-start.18 = (f32[40,1664]{1,0:T(8,128)S(1)}, f32[40,1664]{1,0:T(8,128)S(1)}, u32[]{:S(2)}, u32[]{:S(2)}) collective-permute-start(f32[40,1664]{1,0:T(8,128)S(1)} %collective-permute-done.17.refs_7_), channel_id=1, source_target_pairs={{0,2},{2,0},{4,6},{6,4},{8,10},{10,8},{12,14},{14,12},{1,3},{3,1},... | collective-permute-start | bytes 798728 | tf_op jit(solution)/shard_map/cond/branch_1_fun/ppermute | solution.py:233
  40.3 11.1 %collective-permute-start.20 = (f32[40,1664]{1,0:T(8,128)S(1)}, f32[40,1664]{1,0:T(8,128)S(1)}, u32[]{:S(2)}, u32[]{:S(2)}) collective-permute-start(f32[40,1664]{1,0:T(8,128)S(1)} %collective-permute-done.19.refs_9_), channel_id=1, source_target_pairs={{0,2},{2,0},{4,6},{6,4},{8,10},{10,8},{12,14},{14,12},{1,3},{3,1},... | collective-permute-start | bytes 798728 | tf_op jit(solution)/shard_map/cond/branch_1_fun/ppermute | solution.py:233
  41.4 14.4 %collective-permute-start.24 = (f32[40,1664]{1,0:T(8,128)S(1)}, f32[40,1664]{1,0:T(8,128)S(1)}, u32[]{:S(2)}, u32[]{:S(2)}) collective-permute-start(f32[40,1664]{1,0:T(8,128)S(1)} %collective-permute-done.17.refs_7_), channel_id=1, source_target_pairs={{0,1},{1,0},{2,3},{3,2},{4,5},{5,4},{6,7},{7,6},{8,9},{9,8},{10,11... | collective-permute-start | bytes 798728 | tf_op jit(solution)/shard_map/cond/branch_1_fun/ppermute | solution.py:238
  41.4 14.4 %collective-permute-start.23 = (f32[40,1664]{1,0:T(8,128)S(1)}, f32[40,1664]{1,0:T(8,128)S(1)}, u32[]{:S(2)}, u32[]{:S(2)}) collective-permute-start(f32[40,1664]{1,0:T(8,128)S(1)} %collective-permute-done.16.refs_6_), channel_id=1, source_target_pairs={{0,1},{1,0},{2,3},{3,2},{4,5},{5,4},{6,7},{7,6},{8,9},{9,8},{10,11... | collective-permute-start | bytes 798728 | tf_op jit(solution)/shard_map/cond/branch_1_fun/ppermute | solution.py:241
  41.9 13.9 %collective-permute-start.26 = (f32[40,1664]{1,0:T(8,128)S(1)}, f32[40,1664]{1,0:T(8,128)}, u32[]{:S(2)}, u32[]{:S(2)}) collective-permute-start(f32[40,1664]{1,0:T(8,128)S(1)} %collective-permute-done.19.refs_9_), channel_id=1, source_target_pairs={{0,1},{1,0},{2,3},{3,2},{4,5},{5,4},{6,7},{7,6},{8,9},{9,8},{10,11... | collective-permute-start | bytes 798728 | tf_op jit(solution)/shard_map/cond/branch_1_fun/ppermute | solution.py:238
  46.2 9.6 %collective-permute-start.25 = (f32[40,1664]{1,0:T(8,128)S(1)}, f32[40,1664]{1,0:T(8,128)}, u32[]{:S(2)}, u32[]{:S(2)}) collective-permute-start(f32[40,1664]{1,0:T(8,128)S(1)} %collective-permute-done.18.refs_8_), channel_id=1, source_target_pairs={{0,1},{1,0},{2,3},{3,2},{4,5},{5,4},{6,7},{7,6},{8,9},{9,8},{10,11... | collective-permute-start | bytes 798728 | tf_op jit(solution)/shard_map/cond/branch_1_fun/ppermute | solution.py:241
  51.5 4.4 %collective-permute-start.27 = (f32[40,1664]{1,0:T(8,128)S(1)}, f32[40,1664]{1,0:T(8,128)}, u32[]{:S(2)}, u32[]{:S(2)}) collective-permute-start(f32[40,1664]{1,0:T(8,128)S(1)} %collective-permute-done.20.refs_10_), channel_id=1, source_target_pairs={{0,1},{1,0},{2,3},{3,2},{4,5},{5,4},{6,7},{7,6},{8,9},{9,8},{10,11... | collective-permute-start | bytes 798728 | tf_op jit(solution)/shard_map/cond/branch_1_fun/ppermute | solution.py:241
  51.5 4.4 %copy-start.1 = (f32[8,128]{1,0:T(8,128)S(1)}, f32[8,128]{1,0:T(8,128)}, u32[]{:S(2)}) copy-start(f32[8,128]{1,0:T(8,128)} %convert_bitcast_fusion.1.mask2.refs_2_) | copy-start | bytes 12292 | tf_op jit(solution)/shard_map/cond
  51.5 4.4 %copy-start.2 = (f32[80,1664]{1,0:T(8,128)S(1)}, f32[80,1664]{1,0:T(8,128)}, u32[]{:S(2)}) copy-start(f32[80,1664]{1,0:T(8,128)} %get-tuple-element.63.refs_3_) | copy-start | bytes 1597444 | tf_op jit(solution)/shard_map/cond
  55.9 1.0 %copy-start.5 = (f32[512,256]{1,0:T(8,128)S(1)}, f32[512,256]{1,0:T(8,128)}, u32[]{:S(2)}) copy-start(f32[512,256]{1,0:T(8,128)} %get-tuple-element.66.refs_18_) | copy-start | bytes 1572868 | tf_op jit(solution)/shard_map/cond
  56.9 1.0 %copy-start.6 = (f32[512,256]{1,0:T(8,128)S(1)}, f32[512,256]{1,0:T(8,128)}, u32[]{:S(2)}) copy-start(f32[512,256]{1,0:T(8,128)} %get-tuple-element.68.refs_20_) | copy-start | bytes 1572868 | tf_op jit(solution)/shard_map/cond
  58.0 1.0 %copy-start.7 = (f32[512,256]{1,0:T(8,128)S(1)}, f32[512,256]{1,0:T(8,128)}, u32[]{:S(2)}) copy-start(f32[512,256]{1,0:T(8,128)} %get-tuple-element.69.refs_21_) | copy-start | bytes 1572868 | tf_op jit(solution)/shard_map/cond

commit v3 on v0

v3 whole, which is shorter than its diff:
```python
import functools

import jax
import jax.numpy as jnp
from jax import lax
from jax.experimental import pallas as pl
from jax.experimental.pallas import tpu as pltpu
from jax.sharding import PartitionSpec as P


HIGH = lax.Precision.HIGHEST
F32, BF16 = jnp.float32, jnp.bfloat16
LANES = 128
NN = (((1,), (0,)), ((), ()))
NT = (((1,), (1,)), ((), ()))
TN = (((0,), (0,)), ((), ()))
VMEM = pl.BlockSpec(memory_space=pltpu.VMEM)
SMEM = pl.BlockSpec(memory_space=pltpu.SMEM)
ANY = pl.BlockSpec(memory_space=pl.ANY)


def product(left, right):
    return jnp.dot(left, right, precision=HIGH, preferred_element_type=F32)


def transposed_product(left, right):
    return lax.dot_general(left, right, TN, precision=HIGH, preferred_element_type=F32)


def mask_of(ancestors, row_start, rows):
    numbers = row_start + jnp.arange(rows, dtype=jnp.int32)
    return jnp.any(ancestors[:, None] == numbers[None, :], axis=0).astype(F32)


def reduce_plan(known_inverse, first_factor, first_corner, first_ancestors, second_factor, second_link, second_corner, second_ancestors):
    groups, share_rows, block_rows = known_inverse.shape
    half_width = second_corner.shape[1]
    col_index = lax.axis_index("col")
    row_start = lax.axis_index("row") * block_rows
    first_mask = mask_of(first_ancestors, row_start, block_rows)[:, None]
    second_mask = mask_of(second_ancestors, row_start, block_rows)[:, None]
    first_masked = first_factor * first_mask
    second_masked = second_factor * second_mask
    share_start = col_index * share_rows
    first_piece = lax.dynamic_slice_in_dim(first_masked, share_start, share_rows, 0)
    second_piece = lax.dynamic_slice_in_dim(second_masked, share_start, share_rows, 0)
    columns = known_inverse.reshape(groups * share_rows, block_rows)
    first_partial = transposed_product(columns, lax.all_gather(first_piece, "row", axis=0, tiled=True))
    second_partial = transposed_product(columns, lax.all_gather(second_piece, "row", axis=0, tiled=True))
    first_image = lax.psum_scatter(first_partial, "col", scatter_dimension=1, tiled=True)
    first_column = -(first_image * first_mask)
    first_full = lax.all_gather(first_column, "col", axis=1, tiled=True)
    diagonal_partial = transposed_product(first_masked, first_column)
    corner_half = lax.dynamic_slice_in_dim(first_corner, col_index * half_width, half_width, 1)
    first_diagonal = corner_half - lax.psum(diagonal_partial, "row")
    diagonal_full = lax.all_gather(first_diagonal, "col", axis=1, tiled=True)
    second_image = lax.psum_scatter(second_partial, "col", scatter_dimension=1, tiled=True)
    link_half = lax.dynamic_slice_in_dim(second_link, col_index * half_width, half_width, 1)
    second_column = -((second_image + product(first_full, link_half)) * second_mask)
    second_half = lax.dynamic_slice_in_dim(second_masked, col_index * half_width, half_width, 1)
    cross_partial = transposed_product(first_full, second_half)
    closing_partial = transposed_product(second_masked, second_column)
    cross_total, closing_total = lax.psum((cross_partial, closing_partial), "row")
    second_cross = -(cross_total + product(diagonal_full, link_half))
    second_diagonal = second_corner - closing_total - transposed_product(second_link, second_cross)
    return (first_column, first_diagonal, second_column, second_cross, second_diagonal)


def dot(left, right, dims):
    return lax.dot_general(left, right, dims, preferred_element_type=F32)


def split(value):
    high = value.astype(BF16)
    return high, (value - high.astype(F32)).astype(BF16)


def dot3(left, right, dims):
    (lh, ll), (rh, rl) = left, right
    return dot(lh, rh, dims) + (dot(lh, rl, dims) + dot(ll, rh, dims))


def dot2(exact, right, dims, flip=False):
    rh, rl = right
    if flip:
        return dot(rh, exact, dims) + dot(rl, exact, dims)
    return dot(exact, rh, dims) + dot(exact, rl, dims)


def slot_codes(mask):
    block = mask.shape[1]
    before = (lax.broadcasted_iota(jnp.int32, (block, block), 0) < lax.broadcasted_iota(jnp.int32, (block, block), 1)).astype(BF16)
    rank = dot(mask.astype(BF16), before, NN)
    return jnp.where(mask > 0, rank, -1.0).astype(jnp.int32)


def marks(ancestors, n, block):
    count = ancestors.shape[1]
    group = lax.div(ancestors, block)
    inside = ancestors - group * block
    groups = (lax.broadcasted_iota(jnp.int32, (n, count), 0) == group).astype(BF16)
    insides = (lax.broadcasted_iota(jnp.int32, (block, count), 0) == inside).astype(BF16)
    return dot(groups, insides, NT)


def picker(code_row, slots, offset=0):
    block = code_row.shape[1]
    at = lax.broadcasted_iota(jnp.int32, (slots, block), 0) - offset
    return ((at == code_row) & (code_row >= 0)).astype(BF16)


def rows_at(start, size, step=8):
    return pl.ds(pl.multiple_of(start, step), size)


def factors_kernel(cap, n, anc1, anc2, first, second, link, out, code, m2, most):
    row = lax.axis_index("row")
    block, width = first.shape
    mask1 = marks(anc1[...], n, block)
    code[...] = slot_codes(mask1)
    m2[...] = marks(anc2[...], n, block)
    most[0, 0] = jnp.max(jnp.sum(mask1, axis=1, keepdims=True)).astype(jnp.int32)
    pick = picker(code[pl.ds(row, 1), :], cap)
    pick2 = (pick.astype(F32) * m2[pl.ds(row, 1), :]).astype(BF16)
    first_c = dot2(pick, split(first[...]), NN)
    out[:, :width] = first_c
    out[:, width:] = dot2(pick2, split(second[...]), NN) - dot3(split(first_c), split(link[...]), NN)


def place_of(row, n):
    return jnp.where(lax.rem(row, 2) == 0, lax.div(row, 2), n - 1 - lax.div(row, 2))


def row_of(place, n):
    return jnp.where(place < n // 2, 2 * place, 2 * (n - 1 - place) + 1)


def chunks_of(lanes):
    return -(-lanes // LANES)


def arrivals_of(n):
    return [0] + [sign * k for k in range(1, n // 2) for sign in (-1, 1)] + [n // 2]


def payload_kernel(cap, n, counts, code, factors, mine, theirs, own, up, down, cols, images, own_ud):
    row, col = lax.axis_index("row"), lax.axis_index("col")
    groups, share, block = mine.shape
    both, half = factors.shape[1], cap // 2
    for g in range(groups):
        base = g * block
        cols[rows_at(base + col * share, share), :] = mine[g]
        cols[rows_at(base + (1 - col) * share, share), :] = theirs[g]
    pick = picker(code[pl.ds(row, 1), :], cap)
    images[...] = dot2(pick, split(cols[...]), NT)
    arrivals = arrivals_of(n)
    place = place_of(row, n)
    own_ud[...] = jnp.zeros(own_ud.shape, F32)
    for d in range(n):
        g = row_of(lax.rem(place + d, n), n)
        spread = picker(code[pl.ds(g, 1), :], cap)
        image = images[:, pl.ds(pl.multiple_of(g * block, block), block)]
        value = dot2(spread, split(image), NT, flip=True)
        x = arrivals.index(d if d <= n // 2 else d - n)
        own[:, x * cap : (x + 1) * cap] = value
        for way, slot in ((0, (n - d) % n), (1, d)):
            if slot < counts[way]:
                own_ud[way, :, slot * cap : (slot + 1) * cap] = value
    mine_rows = rows_at(col * half, half)
    for way, out in ((0, up), (1, down)):
        for c in range(both // LANES):
            out[c * half : (c + 1) * half, :] = factors[mine_rows, c * LANES : (c + 1) * LANES]
        for c in range(chunks_of(counts[way] * cap)):
            at = both // LANES + c
            out[at * half : (at + 1) * half, :] = own_ud[way, mine_rows, c * LANES : (c + 1) * LANES]


def side_kernel(corner, link, cross0, diag0, link_half):
    half_width = cross0.shape[1]
    start = pl.multiple_of(lax.axis_index("col") * half_width, half_width)
    link_half[...] = link[:, pl.ds(start, half_width)]
    value = dot3(split(corner[...]), split(link_half[...]), NN)
    cross0[...] = value
    diag0[...] = dot3(split(link[...]), split(value), TN)


def assemble(cap, flat, blk, k):
    col = lax.axis_index("col")
    half = cap // 2
    for value, side in zip(flat, (col, 1 - col)):
        for c in range(value.shape[0] // half):
            blk[rows_at(k * cap + side * half, half), c * LANES : (c + 1) * LANES] = value[c * half : (c + 1) * half, :]


def columns(both, half_width):
    start = lax.axis_index("col") * half_width
    f_at = pl.ds(pl.multiple_of(start, half_width), half_width)
    t_at = pl.ds(pl.multiple_of(both // 2 + start, half_width), half_width)
    return f_at, t_at


def pairs(size, values, lh, ll, rh, rl):
    both, half_width = lh.shape[1], rh.shape[1] // 2
    width = both // 2
    lh[size:, :], ll[size:, :] = split(values)
    f_at, t_at = columns(both, half_width)
    for left, right in ((lh, rh), (ll, rl)):
        for lanes, at in ((slice(0, half_width), f_at), (slice(half_width, 2 * half_width), t_at)):
            right[:size, lanes] = left[size:, at]
            right[size:, lanes] = left[:size, at]
    cross = dot3((lh[:, :width], ll[:, :width]), (rh[...], rl[...]), TN)
    close = dot3((lh[:, width:], ll[:, width:]), (rh[:, half_width:], rl[:, half_width:]), TN)
    return cross, close


def ahead(pieces, slots):
    lanes = slice(slots[0] * LANES, (slots[-1] + 1) * LANES)
    total = None
    for fth, ftl, kh, kl in pieces:
        value = dot3((kh[:, lanes], kl[:, lanes]), (fth[...], ftl[...]), TN)
        total = value if total is None else total + value
    return total


def update_kernel(cap, n, k, *refs):
    arrivals = arrivals_of(n)
    fresh, final = k == 1, k == n // 2 - 1
    if fresh:
        (factors, own), refs = refs[:2], refs[2:]
        old = ()
    else:
        old_v, old_ab, old_ee = refs[:3]
        refs = refs[3:]
        old = [refs[4 * m : 4 * m + 4] for m in range(k - 1)]
        refs = refs[4 * (k - 1) :]
        if final:
            own, refs = refs[0], refs[1:]
    up, down, refs = refs[:2], refs[2:4], refs[4:]
    fth, ftl, kh, kl, ab, ee, v_next, *refs = refs
    if final:
        image, *refs = refs
    blk, middle, lh, ll, rh, rl = refs
    both = fth.shape[1]
    news = ([0] if fresh else []) + [2 * k - 1, 2 * k]
    size = cap * len(news)
    if fresh:
        blk[:cap, :both] = factors[...]
    base = len(news) - 2
    assemble(cap, up, blk, base)
    assemble(cap, down, blk, base + 1)
    middle[...] = jnp.zeros(middle.shape, F32)
    kh[...] = jnp.zeros(kh.shape, BF16)
    kl[...] = jnp.zeros(kl.shape, BF16)
    for a, x in enumerate(news):
        rows = slice(a * cap, (a + 1) * cap)
        for y in range(x, n):
            if x == 0:
                value = own[:, y * cap : (y + 1) * cap]
            else:
                way = -1 if arrivals[x] < 0 else 1
                slot = (way * (arrivals[y] - arrivals[x])) % n
                if slot >= n - 2 * k + (1 if way < 0 or slot == 0 else 0):
                    continue
                value = blk[rows, both + slot * cap : both + (slot + 1) * cap]
            if y in news:
                b = news.index(y)
                middle[rows, b * cap : (b + 1) * cap] = value * 0.5 if y == x else value
            else:
                kh[rows, y * LANES : y * LANES + cap], kl[rows, y * LANES : y * LANES + cap] = split(value)
    sh, sl = split(blk[:, :both])
    fth[...], ftl[...] = sh, sl
    lh[:size, :], ll[:size, :] = sh, sl
    values = dot3(split(middle[...]), (sh, sl), NN)
    if not fresh:
        values = values + jnp.concatenate([old_v[:cap, :], old_v[LANES : LANES + cap, :]], axis=0)
    cross, close = pairs(size, values, lh, ll, rh, rl)
    if fresh:
        ab[...], ee[...] = cross, close
    else:
        ab[...] = old_ab[...] + cross
        ee[...] = old_ee[...] + close
    pieces = [*old, (fth, ftl, kh, kl)]
    v_next[...] = ahead(pieces, [2 * k + 1] if final else [2 * k + 1, 2 * k + 2])
    if final:
        f_at, t_at = columns(both, ee.shape[1])
        start = 0
        total_f = total_t = None
        for ph, pl_, _, _ in pieces:
            stop = start + ph.shape[0]
            part = split(own[:, start:stop])
            value_f = dot3(part, (ph[:, f_at], pl_[:, f_at]), NN)
            value_t = dot3(part, (ph[:, t_at], pl_[:, t_at]), NN)
            total_f = value_f if total_f is None else total_f + value_f
            total_t = value_t if total_t is None else total_t + value_t
            start = stop
        image[:, : ee.shape[1]] = total_f
        image[:, ee.shape[1] :] = total_t


def last_kernel(cap, n, up, down, up_far, down_far, old_v, old_ab, old_ee, image, own, code, m2, corner1, corner2, cross0, diag0, *refs):
    c1, g1, c2, xx, g2, flat, flat_far, blk, lh, ll, rh, rl, c1_v, g1_v, c2_v, xx_v, g2_v, corner1_v, corner2_v, cross0_v, diag0_v, sems = refs
    row, col = lax.axis_index("row"), lax.axis_index("col")
    both, half_width = lh.shape[1], old_ee.shape[1]
    half_at = pl.ds(pl.multiple_of(col * half_width, half_width), half_width)
    loads = [
        pltpu.make_async_copy(corner1.at[:, half_at], corner1_v, sems.at[5]),
        pltpu.make_async_copy(corner2, corner2_v, sems.at[6]),
        pltpu.make_async_copy(cross0, cross0_v, sems.at[7]),
        pltpu.make_async_copy(diag0, diag0_v, sems.at[8]),
    ]
    for load in loads:
        load.start()
    cut = up.shape[0]
    flat[:cut, :], flat[cut:, :] = up[...], down[...]
    flat_far[:cut, :], flat_far[cut:, :] = up_far[...], down_far[...]
    assemble(cap, (flat, flat_far), blk, 0)
    sh, sl = split(blk[:, :both])
    lh[:cap, :], ll[:cap, :] = sh, sl
    values = dot3(split(blk[:, both : both + cap] * 0.5), (sh, sl), NN) + old_v[:cap, :]
    cross, close = pairs(cap, values, lh, ll, rh, rl)
    for load in loads:
        load.wait()
    copies = []

    def send(value, ref, out):
        ref[...] = value
        copies.append(pltpu.make_async_copy(ref, out, sems.at[len(copies)]))
        copies[-1].start()

    send(corner1_v[...] + (old_ab[:, :half_width] + cross[:, :half_width]), g1_v, g1)
    send(old_ab[:, half_width:] + cross[:, half_width:] - cross0_v[...], xx_v, xx)
    send(corner2_v[...] + (diag0_v[...] + (old_ee[...] + close)), g2_v, g2)
    k = split(own[:, (n - 1) * cap :])
    pick = picker(code[pl.ds(row, 1), :], cap)
    pick2 = (pick.astype(F32) * m2[pl.ds(row, 1), :]).astype(BF16)
    f_at, t_at = columns(both, half_width)
    image_f = image[:, :half_width] + dot3(k, (lh[:cap, f_at], ll[:cap, f_at]), NN)
    send(-dot2(pick, split(image_f), TN), c1_v, c1)
    image_t = image[:, half_width:] + dot3(k, (lh[:cap, t_at], ll[:cap, t_at]), NN)
    send(-dot2(pick2, split(image_t), TN), c2_v, c2)
    for copy in copies:
        copy.wait()


def call_factors(cap, n, anc1, anc2, first_factor, second_factor, second_link):
    block, width = first_factor.shape
    return pl.pallas_call(
        functools.partial(factors_kernel, cap, n),
        out_shape=(
            jax.ShapeDtypeStruct((cap, 2 * width), F32),
            jax.ShapeDtypeStruct((n, block), jnp.int32),
            jax.ShapeDtypeStruct((n, block), F32),
            jax.ShapeDtypeStruct((1, 1), jnp.int32),
        ),
        in_specs=[VMEM] * 5,
        out_specs=(VMEM, VMEM, VMEM, SMEM),
        cost_estimate=pl.CostEstimate(flops=6 * cap * width * width, bytes_accessed=4 * width * (2 * block + width), transcendentals=0),
        name="factors",
    )(anc1, anc2, first_factor, second_factor, second_link)


def call_payload(cap, n, code, factors, mine, theirs):
    _, _, block = mine.shape
    both, half = factors.shape[1], cap // 2
    counts = (n - 1, n - 2)
    flats = [jax.ShapeDtypeStruct(((both // LANES + chunks_of(count * cap)) * half, LANES), F32) for count in counts]
    return pl.pallas_call(
        functools.partial(payload_kernel, cap, n, counts),
        out_shape=(jax.ShapeDtypeStruct((cap, n * cap), F32), *flats),
        in_specs=[VMEM] * 4,
        out_specs=(VMEM,) * 3,
        scratch_shapes=[
            pltpu.VMEM((n * block, block), F32),
            pltpu.VMEM((cap, n * block), F32),
            pltpu.VMEM((2, cap, chunks_of(counts[0] * cap) * LANES), F32),
        ],
        cost_estimate=pl.CostEstimate(flops=8 * cap * block * n * block, bytes_accessed=8 * n * block * block, transcendentals=0),
        name="payload",
    )(code, factors, mine, theirs)


def gather_branch(cap, n, factors, code, m2, own, own_up, own_down, second_link, first_corner, second_corner):
    block = code.shape[1]
    width = second_link.shape[0]
    half_width = second_corner.shape[1]
    half, both = cap // 2, 2 * width
    square = jax.ShapeDtypeStruct((width, half_width), F32)
    tall = jax.ShapeDtypeStruct((block, half_width), F32)

    order = [*range(0, n, 2), *range(n - 1, 0, -2)]
    ups = [(order[k], order[(k + 1) % n]) for k in range(n)]
    downs = [(b, a) for a, b in ups]
    swap = [(0, 1), (1, 0)]

    def scratch_of(blocks):
        size = cap * blocks
        return [
            pltpu.VMEM((2 * size, both), BF16),
            pltpu.VMEM((2 * size, both), BF16),
            pltpu.VMEM((2 * size, 2 * half_width), BF16),
            pltpu.VMEM((2 * size, 2 * half_width), BF16),
        ]

    params = pltpu.CompilerParams(vmem_limit_bytes=40 << 20)
    cross0, diag0 = pl.pallas_call(
        side_kernel,
        out_shape=(square, square),
        in_specs=[VMEM] * 2,
        out_specs=(VMEM, VMEM),
        scratch_shapes=[pltpu.VMEM((width, half_width), F32)],
        cost_estimate=pl.CostEstimate(flops=12 * width * width * half_width, bytes_accessed=20 * width * width, transcendentals=0),
        name="side",
    )(first_corner, second_link)

    def flat_rows(count):
        return (both // LANES + chunks_of(count * cap)) * half

    up, down = own_up, own_down
    pieces, state, image = [], (), ()
    for k in range(1, n // 2):
        up = lax.ppermute(up[: flat_rows(n + 1 - 2 * k)], "row", ups)
        down = lax.ppermute(down[: flat_rows(n - 2 * k)], "row", downs)
        up_far, down_far = lax.ppermute(up, "col", swap), lax.ppermute(down, "col", swap)
        fresh, final = k == 1, k == n // 2 - 1
        blocks = 3 if fresh else 2
        size = blocks * cap
        ins = [factors, own] if fresh else [*state, *(array for piece in pieces for array in piece)]
        if final and not fresh:
            ins.append(own)
        ins += [up, up_far, down, down_far]
        half_piece = jax.ShapeDtypeStruct((size, both), BF16)
        outs = [half_piece, half_piece] + [jax.ShapeDtypeStruct((size, n * LANES), BF16)] * 2
        outs += [jax.ShapeDtypeStruct((width, 2 * half_width), F32), square]
        outs += [jax.ShapeDtypeStruct(((1 if final else 2) * LANES, both), F32)]
        if final:
            outs += [jax.ShapeDtypeStruct((cap, 2 * half_width), F32)]
        results = pl.pallas_call(
            functools.partial(update_kernel, cap, n, k),
            out_shape=tuple(outs),
            in_specs=[VMEM] * len(ins),
            out_specs=(VMEM,) * len(outs),
            scratch_shapes=[pltpu.VMEM((size, both + chunks_of((n - 1) * cap) * LANES), F32), pltpu.VMEM((size, size), F32)] + scratch_of(blocks),
            compiler_params=params,
            cost_estimate=pl.CostEstimate(flops=6 * size * width * (4 * size + 6 * half_width), bytes_accessed=4 * size * width * 8, transcendentals=0),
        )(*ins)
        pieces.append(results[:4])
        ab, ee, v_next = results[4:7]
        state = (v_next, ab, ee)
        image = results[7:]
    rows = flat_rows(1)
    cut = -(-rows // 16) * 8
    k = n // 2
    up = lax.ppermute(up[:cut], "row", ups)
    down = lax.ppermute(down[cut:rows], "row", downs)
    up_far, down_far = lax.ppermute(up, "col", swap), lax.ppermute(down, "col", swap)
    return pl.pallas_call(
        functools.partial(last_kernel, cap, n),
        out_shape=(tall, square, tall, square, square),
        in_specs=[VMEM] * 11 + [ANY] * 4,
        out_specs=(ANY,) * 5,
        scratch_shapes=[pltpu.VMEM((rows, LANES), F32)] * 2
        + [pltpu.VMEM((cap, both + chunks_of(cap) * LANES), F32)]
        + scratch_of(1)
        + [pltpu.VMEM(shape.shape, F32) for shape in (tall, square, tall, square, square)]
        + [pltpu.VMEM(square.shape, F32)] * 4
        + [pltpu.SemaphoreType.DMA((9,))],
        compiler_params=params,
        cost_estimate=pl.CostEstimate(flops=6 * cap * width * (2 * width + 6 * half_width), bytes_accessed=4 * width * width * 5, transcendentals=0),
        name="last",
    )(up, down, up_far, down_far, *state, *image, own, code, m2, first_corner, second_corner, cross0, diag0)


def gather_plan(n, known_inverse, first_factor, first_corner, first_ancestors, second_factor, second_link, second_corner, second_ancestors):
    _, _, block = known_inverse.shape
    theirs = lax.ppermute(known_inverse, "col", [(0, 1), (1, 0)])
    anc1, anc2 = first_ancestors[None, :], second_ancestors[None, :]
    mean = -(-first_ancestors.shape[0] // n)
    cap = min(-(-mean * 5 // 64) * 16, block)
    factors, code, m2, most = call_factors(cap, n, anc1, anc2, first_factor, second_factor, second_link)
    own = call_payload(cap, n, code, factors, known_inverse, theirs)

    def compact(own, factors, code, m2, known_inverse, theirs, anc1, anc2, first_factor, second_factor, second_link, first_corner, second_corner):
        return gather_branch(cap, n, factors, code, m2, *own, second_link, first_corner, second_corner)

    def general(own, factors, code, m2, known_inverse, theirs, anc1, anc2, first_factor, second_factor, second_link, first_corner, second_corner):
        factors, code, m2, _ = call_factors(block, n, anc1, anc2, first_factor, second_factor, second_link)
        own = call_payload(block, n, code, factors, known_inverse, theirs)
        return gather_branch(block, n, factors, code, m2, *own, second_link, first_corner, second_corner)

    operands = (own, factors, code, m2, known_inverse, theirs, anc1, anc2, first_factor, second_factor, second_link, first_corner, second_corner)
    if cap == block:
        return compact(*operands)
    return lax.cond(most[0, 0] <= cap, compact, general, *operands)


def solution(mesh):
    n = mesh.shape["row"]

    def on_device(known_inverse, *rest):
        _, _, block = known_inverse.shape
        width = rest[0].shape[1]
        if n % 2 == 0 and n > 4 and block % LANES == 0 and mesh.shape["col"] == 2 and (n * block) ** 2 <= 12 * width**2:
            return gather_plan(n, known_inverse, *rest)
        return reduce_plan(known_inverse, *rest)

    return jax.shard_map(
        on_device,
        mesh=mesh,
        in_specs=(
            P("pole", "col", "row"),
            P(("pole", "row"), None),
            P("pole", None),
            P("pole"),
            P(("pole", "row"), None),
            P("pole", None),
            P("pole", "col"),
            P("pole"),
        ),
        out_specs=(
            P(("pole", "row"), "col"),
            P("pole", "col"),
            P(("pole", "row"), "col"),
            P("pole", "col"),
            P("pole", "col"),
        ),
        check_vma=False,
    )
```

time: 234 us -> 52 us (0.22)
  waiting for transfers between devices: 190 us -> 14.1 us
  Pallas kernels: 0 us -> 22.1 us
  matrix products: 18.5 us -> 0 us
  between operations: 14.2 us -> 1.51 us
  starting transfers between devices: 0.25 us -> 11 us
  other arithmetic: 4.23 us -> 0 us
    psum x1 -> x0, waiting for transfers between devices: 91.4 us -> none  [on_device(): first_diagonal = corner_half - lax.psum(diagonal_partial, 'row')]
    all_gather x3 -> x0, waiting for transfers between devices: 87 us -> none  [the longest x1 42.2 us: on_device(): lax.all_gather(first_piece, 'row', axis=0, tiled=True)]
    pallas_call x0 -> x7, Pallas kernels: none -> 22.1 us  [the longest x3 10.8 us: gather_branch(): pl.pallas_call(functools.partial(update_kernel, cap, n, k), out_shape=tup...]
    dot_general x8 -> x0, matrix products: 18.5 us -> none  [the longest x6 14.3 us: transposed_product(): lax.dot_general(left, right, (((0,), (0,)), ((), ())), precision=HIGH, pr...]
    ppermute x0 -> x17, waiting for transfers between devices: none -> 14.1 us  [the longest x3 7.22 us: gather_branch(): up = lax.ppermute(up[:flat_rows(n + 1 - 2 * k)], 'row', ups)]
    reduce_scatter x2 -> x0, waiting for transfers between devices: 11.3 us -> none  [the longest x1 5.86 us: on_device(): lax.psum_scatter(second_partial, 'col', scatter_dimension=1, tiled=True)]
    ppermute x0 -> x17, starting transfers between devices: none -> 11 us  [the longest x3 5.99 us: gather_branch(): up = lax.ppermute(up[:flat_rows(n + 1 - 2 * k)], 'row', ups)]
  transfers between devices with their start and end apart: 6 -> 17, of which waited for: 6 -> 3; matrix products, arithmetic and copies ran while one was open for 6% -> 3% of each run, Pallas kernels for 0% -> 33%
where the time goes in v3:
time: 52 us; the launch traced here: 51.8 us
  Pallas kernels  22.1 us (42%)
  waiting for transfers between devices  14.1 us (27%)
  starting transfers between devices  11 us (21%)
  local copies, waits for them, and re-layouts  2.9 us (6%)
  between operations  1.51 us (3%)
    pallas_call x3, Pallas kernels, gather_branch(): pl.pallas_call(functools.partial(update_kernel, cap, n, k), out_shape=tup...  10.8 us
    ppermute x3, waiting for transfers between devices, gather_branch(): up = lax.ppermute(up[:flat_rows(n + 1 - 2 * k)], 'row', ups)  7.22 us
    ppermute x3, waiting for transfers between devices, gather_branch(): down = lax.ppermute(down[:flat_rows(n - 2 * k)], 'row', downs)  6.07 us
    ppermute x3, starting transfers between devices, gather_branch(): up = lax.ppermute(up[:flat_rows(n + 1 - 2 * k)], 'row', ups)  5.99 us
    pallas_call x1, Pallas kernels, gather_branch(): pl.pallas_call(side_kernel, out_shape=(square, square), in_specs=[VMEM] *...  3.86 us
    pallas_call x1, Pallas kernels, gather_branch(): pl.pallas_call(functools.partial(last_kernel, cap, n), out_shape=(tall, s...  3.49 us
    pallas_call x1, Pallas kernels, call_factors(): pl.pallas_call(functools.partial(factors_kernel, cap, n), out_shape=(jax....  2.3 us
    pallas_call x1, Pallas kernels, call_payload(): pl.pallas_call(functools.partial(payload_kernel, cap, n, counts), out_sha...  1.68 us
  transfers between devices with their start and end apart: 17, of which 3 were waited for; matrix products, arithmetic and copies ran while one was open for 3% of the time, Pallas kernels for 33%

profile of v3, /device:TPU:0, one launch (start us, length us, event | category | flops | bytes accessed | tf_op | source)
XLA Modules:
  0.0 51.8 jit_solution(15836597304523472223)
XLA Ops:
  0.6 0.6 %collective-permute-start.32 = (f32[8,64,128]{2,1,0:T(8,128)}, f32[8,64,128]{2,1,0:T(8,128)S(1)}, u32[]{:S(2)}, u32[]{:S(2)}) collective-permute-start(f32[8,64,128]{2,1,0:T(8,128)} %mine.1), channel_id=1, source_target_pairs={{0,1},{1,0},{2,3},{3,2},{4,5},{5,4},{6,7},{7,6},{8,9},{9,8},{10,11... | collective-permute-start | bytes 786440 | tf_op jit(solution)/shard_map/ppermute | solution.py:475
  1.2 0.1 copy-done.18
  1.3 0.6 %copy-done.19 = s32[256]{0:T(256)S(1)} copy-done((s32[256]{0:T(256)S(1)}, s32[256]{0:T(256)}, u32[]{:S(2)}) %copy-start.19) | copy-done | bytes 1048
  1.9 2.3 %factors.3 = (f32[80,1024]{1,0:T(8,128)S(1)}, s32[8,128]{1,0:T(8,128)S(1)}, f32[8,128]{1,0:T(8,128)S(1)}, s32[1,1]{1,0:T(1,128)}) custom-call(s32[1,512]{1,0:T(1,128)S(1)} %bitcast.3, s32[1,256]{1,0:T(1,128)S(1)} %bitcast.5, f32[128,512]{1,0:T(8,128)} %first.1, f32[128,512]{1,0:T(8,128)} %second.1, f32[512,512]{1,0:T(8,128)} %link.1), custom_call_target="tpu_custom_call" | custom-call | flops 125829120 | bytes 1572864 | tf_op jit(solution)/shard_map/factors/pallas_call | solution.py:347
  4.9 0.0 copy-start.14
  4.9 1.7 %payload.3 = (f32[80,640]{1,0:T(8,128)}, f32[520,128]{1,0:T(8,128)}, f32[480,128]{1,0:T(8,128)}) custom-call(s32[8,128]{1,0:T(8,128)S(1)} %get-tuple-element.113.code, f32[80,1024]{1,0:T(8,128)S(1)} %get-tuple-element.114.factors, f32[8,64,128]{2,1,0:T(8,128)S(1)} %copy-done.13, f32[8,64,128]{2,1,0:T(8,128)S(1)} %collective-permute-done.32.theirs), custom_call_target="tpu_custom_call" | custom-call | flops 83886080 | bytes 1048576 | tf_op jit(solution)/shard_map/payload/pallas_call | solution.py:367
  6.6 45.0 %conditional.1 = ((f32[128,256]{1,0:T(8,128)}, f32[512,256]{1,0:T(8,128)}, f32[128,256]{1,0:T(8,128)}, f32[512,256]{1,0:T(8,128)}, f32[512,256]{1,0:T(8,128)})) conditional(s32[]{:T(128)} %bitcast.2, (s32[1,512]{1,0:T(1,128)S(1)}, s32[1,256]{1,0:T(1,128)S(1)}, f32[128,512]{1,0:T(8,128)S(1)}, f32[128,512]{1,0:T(8,128)S(1)}, f32[512,512]{1,0:T(8,128)}, ...), branch_computations={%region_0.0_spmd, %region_1.0_spmd} | conditional | flops 9797894144 | bytes 68125544 | solution.py:493
  6.6 0.7 %copy-done.17 = f32[80,1024]{1,0:T(8,128)} copy-done((f32[80,1024]{1,0:T(8,128)}, f32[80,1024]{1,0:T(8,128)S(1)}, u32[]{:S(2)}) %copy-start.17) | copy-done | bytes 327704 | tf_op jit(solution)/shard_map/cond
  7.3 2.6 %collective-permute-start.16 = (f32[520,128]{1,0:T(8,128)}, f32[520,128]{1,0:T(8,128)S(1)}, u32[]{:S(2)}, u32[]{:S(2)}) collective-permute-start(f32[520,128]{1,0:T(8,128)} %get-tuple-element.71), channel_id=1, source_target_pairs={{0,4},{4,8},{8,12},{12,14},{14,10},{10,6},{6,2},{2,0},{1,5},{5,9},... | collective-permute-start | bytes 798728 | tf_op jit(solution)/shard_map/cond/branch_1_fun/ppermute | solution.py:421
  9.9 7.2 %collective-permute-done.16.refs_2_ = f32[520,128]{1,0:T(8,128)S(1)} collective-permute-done((f32[520,128]{1,0:T(8,128)}, f32[520,128]{1,0:T(8,128)S(1)}, u32[]{:S(2)}, u32[]{:S(2)}) %collective-permute-start.16) | collective-permute-done | bytes 266272 | tf_op jit(solution)/shard_map/cond/branch_1_fun/ppermute | solution.py:421
  17.1 1.9 %collective-permute-start.17 = (f32[480,128]{1,0:T(8,128)S(1)}, f32[480,128]{1,0:T(8,128)S(1)}, u32[]{:S(2)}, u32[]{:S(2)}) collective-permute-start(f32[480,128]{1,0:T(8,128)S(1)} %slice.42), channel_id=1, source_target_pairs={{0,4},{4,8},{8,12},{12,14},{14,10},{10,6},{6,2},{2,0},{1,5},{5,9},... | collective-permute-start | bytes 737288 | tf_op jit(solution)/shard_map/cond/branch_1_fun/ppermute | solution.py:421
  19.0 0.3 collective-permute-start.21
  19.2 0.5 collective-permute-start.26
  19.7 6.1 %collective-permute-done.21.refs_9_ = f32[440,128]{1,0:T(8,128)S(1)} collective-permute-done((f32[440,128]{1,0:T(8,128)S(1)}, f32[440,128]{1,0:T(8,128)S(1)}, u32[]{:S(2)}, u32[]{:S(2)}) %collective-permute-start.21) | collective-permute-done | bytes 225312 | tf_op jit(solution)/shard_map/cond/branch_1_fun/ppermute | solution.py:422
  25.8 0.7 %slice.46 = f32[400,128]{1,0:T(8,128)} slice(f32[440,128]{1,0:T(8,128)S(1)} %collective-permute-done.21.refs_9_), slice={[0:400], [0:128]} | slice | bytes 409600 | tf_op jit(solution)/shard_map/cond/branch_1_fun/slice | solution.py:422
  26.5 0.5 collective-permute-start.22
  27.0 0.7 %slice.43 = f32[400,128]{1,0:T(8,128)} slice(f32[480,128]{1,0:T(8,128)S(1)} %collective-permute-done.17.refs_7_), slice={[0:400], [0:128]} | slice | bytes 409600 | tf_op jit(solution)/shard_map/cond/branch_1_fun/slice | solution.py:421
  27.7 1.5 %collective-permute-start.18 = (f32[400,128]{1,0:T(8,128)}, f32[400,128]{1,0:T(8,128)S(1)}, u32[]{:S(2)}, u32[]{:S(2)}) collective-permute-start(f32[400,128]{1,0:T(8,128)} %slice.43), channel_id=1, source_target_pairs={{0,4},{4,8},{8,12},{12,14},{14,10},{10,6},{6,2},{2,0},{1,5},{5,9},... | collective-permute-start | bytes 614408 | tf_op jit(solution)/shard_map/cond/branch_1_fun/ppermute | solution.py:421
  29.2 0.5 collective-permute-start.28
  29.7 3.9 %side.3 = (f32[512,256]{1,0:T(8,128)}, f32[512,256]{1,0:T(8,128)}) custom-call(f32[512,512]{1,0:T(8,128)} %get-tuple-element.95.corner.corner1, f32[512,512]{1,0:T(8,128)S(1)} %copy-done.8), custom_call_target="tpu_custom_call" | custom-call | flops 805306368 | bytes 5242880 | tf_op jit(solution)/shard_map/cond/branch_1_fun/side/pallas_call | solution.py:405
  33.6 0.0 collective-permute-start.31
  33.6 0.0 collective-permute-done.18.refs_12_
  33.7 0.5 collective-permute-start.30
  34.1 4.0 %branch_1_fun.3 = (bf16[240,1024]{1,0:T(8,128)(2,1)S(1)}, bf16[240,1024]{1,0:T(8,128)(2,1)S(1)}, bf16[240,1024]{1,0:T(8,128)(2,1)S(1)}, bf16[240,1024]{1,0:T(8,1...) custom-call(f32[80,1024]{1,0:T(8,128)} %copy-done.17, ...), custom_call_target="tpu_custom_call" | custom-call | flops 1840250880 | bytes 3932160 | tf_op jit(solution)/shard_map/cond/branch_1_fun/pallas_call | solution.py:437
  38.1 1.1 %collective-permute-start.23 = (f32[176,128]{1,0:T(8,128)S(1)}, f32[176,128]{1,0:T(8,128)S(1)}, u32[]{:S(2)}, u32[]{:S(2)}) collective-permute-start(f32[176,128]{1,0:T(8,128)S(1)} %slice.47), channel_id=1, source_target_pairs={{4,0},{8,4},{12,8},{14,12},{10,14},{6,10},{2,6},{0,2},{5,1},{9,5},... | collective-permute-start | bytes 270344 | tf_op jit(solution)/shard_map/cond/branch_1_fun/ppermute | solution.py:454
  39.2 1.1 %collective-permute-start.19 = (f32[184,128]{1,0:T(8,128)S(1)}, f32[184,128]{1,0:T(8,128)S(1)}, u32[]{:S(2)}, u32[]{:S(2)}) collective-permute-start(f32[184,128]{1,0:T(8,128)S(1)} %slice.44), channel_id=1, source_target_pairs={{0,4},{4,8},{8,12},{12,14},{14,10},{10,6},{6,2},{2,0},{1,5},{5,9},... | collective-permute-start | bytes 282632 | tf_op jit(solution)/shard_map/cond/branch_1_fun/ppermute | solution.py:453
  40.3 3.0 %branch_1_fun.4 = (bf16[160,1024]{1,0:T(8,128)(2,1)S(1)}, bf16[160,1024]{1,0:T(8,128)(2,1)S(1)}, bf16[160,1024]{1,0:T(8,128)(2,1)S(1)}, bf16[160,1024]{1,0:T(8,1...) custom-call(f32[256,1024]{1,0:T(8,128)S(1)} %get-tuple-element.75.refs_0_, ...), custom_call_target="tpu_custom_call" | custom-call | flops 1069547520 | bytes 2621440 | tf_op jit(solution)/shard_map/cond/branch_1_fun/pallas_call | solution.py:437
  43.2 0.1 collective-permute-start.25
  43.3 0.8 %collective-permute-done.19.up = f32[184,128]{1,0:T(8,128)S(1)} collective-permute-done((f32[184,128]{1,0:T(8,128)S(1)}, f32[184,128]{1,0:T(8,128)S(1)}, u32[]{:S(2)}, u32[]{:S(2)}) %collective-permute-start.19) | collective-permute-done | bytes 94240 | tf_op jit(solution)/shard_map/cond/branch_1_fun/ppermute | solution.py:453
  44.1 0.0 copy-start.4
  44.2 3.9 %branch_1_fun.5 = (bf16[160,1024]{1,0:T(8,128)(2,1)}, bf16[160,1024]{1,0:T(8,128)(2,1)}, bf16[160,1024]{1,0:T(8,128)(2,1)}, bf16[160,1024]{1,0:T(8,128)(2,1)}, f...) custom-call(f32[256,1024]{1,0:T(8,128)S(1)} %get-tuple-element.82.refs_0_, ...), custom_call_target="tpu_custom_call" | custom-call | flops 1069547520 | bytes 2621440 | tf_op jit(solution)/shard_map/cond/branch_1_fun/pallas_call | solution.py:437
  48.1 3.5 %last.3 = (f32[128,256]{1,0:T(8,128)}, f32[512,256]{1,0:T(8,128)}, f32[128,256]{1,0:T(8,128)}, f32[512,256]{1,0:T(8,128)}, f32[512,256]{1,0:T(8,128)}) custom-call(f32[184,128]{1,0:T(8,128)S(1)} %collective-permute-done.19.up, f32[176,128]{1,0:T(8,128)S(1)} %collective-permute-done.23.down, f32[184,128]{1,0:T(8,128)S(1)} %collective-permute-done.24.up_far, ...), custom_call_target="tpu_custom_call" | custom-call | flops 629145600 | bytes 5242880 | tf_op jit(solution)/shard_map/cond/branch_1_fun/last/pallas_call | solution.py:456
  (40 shorter events, 0.1 us)
Async XLA Ops:
  0.6 0.7 %copy-start.18 = (s32[512]{0:T(512)S(1)}, s32[512]{0:T(512)}, u32[]{:S(2)}) copy-start(s32[512]{0:T(512)} %param.13) | copy-start | bytes 6148
  0.6 4.2 %collective-permute-start.32 = (f32[8,64,128]{2,1,0:T(8,128)}, f32[8,64,128]{2,1,0:T(8,128)S(1)}, u32[]{:S(2)}, u32[]{:S(2)}) collective-permute-start(f32[8,64,128]{2,1,0:T(8,128)} %mine.1), channel_id=1, source_target_pairs={{0,1},{1,0},{2,3},{3,2},{4,5},{5,4},{6,7},{7,6},{8,9},{9,8},{10,11... | collective-permute-start | bytes 786440 | tf_op jit(solution)/shard_map/ppermute | solution.py:475
  1.2 0.7 %copy-start.19 = (s32[256]{0:T(256)S(1)}, s32[256]{0:T(256)}, u32[]{:S(2)}) copy-start(s32[256]{0:T(256)} %param.17) | copy-start | bytes 3076
  1.9 3.0 %copy-start.13 = (f32[8,64,128]{2,1,0:T(8,128)S(1)}, f32[8,64,128]{2,1,0:T(8,128)}, u32[]{:S(2)}) copy-start(f32[8,64,128]{2,1,0:T(8,128)} %mine.1) | copy-start | bytes 786436
  4.9 1.7 %copy-start.14 = (f32[128,512]{1,0:T(8,128)S(1)}, f32[128,512]{1,0:T(8,128)}, u32[]{:S(2)}) copy-start(f32[128,512]{1,0:T(8,128)} %first.1) | copy-start | bytes 786436
  4.9 1.7 %copy-start.15 = (f32[128,512]{1,0:T(8,128)S(1)}, f32[128,512]{1,0:T(8,128)}, u32[]{:S(2)}) copy-start(f32[128,512]{1,0:T(8,128)} %second.1) | copy-start | bytes 786436
  6.6 0.7 %copy-start.17 = (f32[80,1024]{1,0:T(8,128)}, f32[80,1024]{1,0:T(8,128)S(1)}, u32[]{:S(2)}) copy-start(f32[80,1024]{1,0:T(8,128)S(1)} %get-tuple-element.73.refs_0_) | copy-start | bytes 983044 | tf_op jit(solution)/shard_map/cond
  7.3 22.5 %copy-start.8 = (f32[512,512]{1,0:T(8,128)S(1)}, f32[512,512]{1,0:T(8,128)}, u32[]{:S(2)}) copy-start(f32[512,512]{1,0:T(8,128)} %get-tuple-element.97.link) | copy-start | bytes 3145732 | tf_op jit(solution)/shard_map/cond
  7.3 9.8 %collective-permute-start.16 = (f32[520,128]{1,0:T(8,128)}, f32[520,128]{1,0:T(8,128)S(1)}, u32[]{:S(2)}, u32[]{:S(2)}) collective-permute-start(f32[520,128]{1,0:T(8,128)} %get-tuple-element.71), channel_id=1, source_target_pairs={{0,4},{4,8},{8,12},{12,14},{14,10},{10,6},{6,2},{2,0},{1,5},{5,9},... | collective-permute-start | bytes 798728 | tf_op jit(solution)/shard_map/cond/branch_1_fun/ppermute | solution.py:421
  9.9 9.1 %collective-permute-start.20 = (f32[480,128]{1,0:T(8,128)}, f32[480,128]{1,0:T(8,128)S(1)}, u32[]{:S(2)}, u32[]{:S(2)}) collective-permute-start(f32[480,128]{1,0:T(8,128)} %get-tuple-element.72), channel_id=1, source_target_pairs={{4,0},{8,4},{12,8},{14,12},{10,14},{6,10},{2,6},{0,2},{5,1},{9,5},... | collective-permute-start | bytes 737288 | tf_op jit(solution)/shard_map/cond/branch_1_fun/ppermute | solution.py:422
  17.1 9.9 %collective-permute-start.17 = (f32[480,128]{1,0:T(8,128)S(1)}, f32[480,128]{1,0:T(8,128)S(1)}, u32[]{:S(2)}, u32[]{:S(2)}) collective-permute-start(f32[480,128]{1,0:T(8,128)S(1)} %slice.42), channel_id=1, source_target_pairs={{0,4},{4,8},{8,12},{12,14},{14,10},{10,6},{6,2},{2,0},{1,5},{5,9},... | collective-permute-start | bytes 737288 | tf_op jit(solution)/shard_map/cond/branch_1_fun/ppermute | solution.py:421
  19.0 6.8 %collective-permute-start.21 = (f32[440,128]{1,0:T(8,128)S(1)}, f32[440,128]{1,0:T(8,128)S(1)}, u32[]{:S(2)}, u32[]{:S(2)}) collective-permute-start(f32[440,128]{1,0:T(8,128)S(1)} %slice.45), channel_id=1, source_target_pairs={{4,0},{8,4},{12,8},{14,12},{10,14},{6,10},{2,6},{0,2},{5,1},{9,5},... | collective-permute-start | bytes 675848 | tf_op jit(solution)/shard_map/cond/branch_1_fun/ppermute | solution.py:422
  19.2 10.0 %collective-permute-start.27 = (f32[480,128]{1,0:T(8,128)S(1)}, f32[480,128]{1,0:T(8,128)S(1)}, u32[]{:S(2)}, u32[]{:S(2)}) collective-permute-start(f32[480,128]{1,0:T(8,128)S(1)} %collective-permute-done.20.refs_4_), channel_id=1, source_target_pairs={{0,1},{1,0},{2,3},{3,2},{4,5},{5,4},{6,7},{7,6},{8,9},{9,8},{10,11... | collective-permute-start | bytes 737288 | tf_op jit(solution)/shard_map/cond/branch_1_fun/ppermute | solution.py:423
  19.2 14.9 %collective-permute-start.26 = (f32[520,128]{1,0:T(8,128)S(1)}, f32[520,128]{1,0:T(8,128)S(1)}, u32[]{:S(2)}, u32[]{:S(2)}) collective-permute-start(f32[520,128]{1,0:T(8,128)S(1)} %collective-permute-done.16.refs_2_), channel_id=1, source_target_pairs={{0,1},{1,0},{2,3},{3,2},{4,5},{5,4},{6,7},{7,6},{8,9},{9,8},{10,11... | collective-permute-start | bytes 798728 | tf_op jit(solution)/shard_map/cond/branch_1_fun/ppermute | solution.py:423
  26.5 7.1 %collective-permute-start.22 = (f32[400,128]{1,0:T(8,128)}, f32[400,128]{1,0:T(8,128)S(1)}, u32[]{:S(2)}, u32[]{:S(2)}) collective-permute-start(f32[400,128]{1,0:T(8,128)} %slice.46), channel_id=1, source_target_pairs={{4,0},{8,4},{12,8},{14,12},{10,14},{6,10},{2,6},{0,2},{5,1},{9,5},... | collective-permute-start | bytes 614408 | tf_op jit(solution)/shard_map/cond/branch_1_fun/ppermute | solution.py:422
  27.7 6.0 %collective-permute-start.18 = (f32[400,128]{1,0:T(8,128)}, f32[400,128]{1,0:T(8,128)S(1)}, u32[]{:S(2)}, u32[]{:S(2)}) collective-permute-start(f32[400,128]{1,0:T(8,128)} %slice.43), channel_id=1, source_target_pairs={{0,4},{4,8},{8,12},{12,14},{14,10},{10,6},{6,2},{2,0},{1,5},{5,9},... | collective-permute-start | bytes 614408 | tf_op jit(solution)/shard_map/cond/branch_1_fun/ppermute | solution.py:421
  29.2 10.0 %collective-permute-start.29 = (f32[440,128]{1,0:T(8,128)S(1)}, f32[440,128]{1,0:T(8,128)S(1)}, u32[]{:S(2)}, u32[]{:S(2)}) collective-permute-start(f32[440,128]{1,0:T(8,128)S(1)} %collective-permute-done.21.refs_9_), channel_id=1, source_target_pairs={{0,1},{1,0},{2,3},{3,2},{4,5},{5,4},{6,7},{7,6},{8,9},{9,8},{10,11... | collective-permute-start | bytes 675848 | tf_op jit(solution)/shard_map/cond/branch_1_fun/ppermute | solution.py:423
  29.2 11.0 %collective-permute-start.28 = (f32[480,128]{1,0:T(8,128)S(1)}, f32[480,128]{1,0:T(8,128)S(1)}, u32[]{:S(2)}, u32[]{:S(2)}) collective-permute-start(f32[480,128]{1,0:T(8,128)S(1)} %collective-permute-done.17.refs_7_), channel_id=1, source_target_pairs={{0,1},{1,0},{2,3},{3,2},{4,5},{5,4},{6,7},{7,6},{8,9},{9,8},{10,11... | collective-permute-start | bytes 737288 | tf_op jit(solution)/shard_map/cond/branch_1_fun/ppermute | solution.py:423
  33.6 10.5 %collective-permute-start.31 = (f32[400,128]{1,0:T(8,128)S(1)}, f32[400,128]{1,0:T(8,128)S(1)}, u32[]{:S(2)}, u32[]{:S(2)}) collective-permute-start(f32[400,128]{1,0:T(8,128)S(1)} %collective-permute-done.22.refs_14_), channel_id=1, source_target_pairs={{0,1},{1,0},{2,3},{3,2},{4,5},{5,4},{6,7},{7,6},{8,9},{9,8},{10,11... | collective-permute-start | bytes 614408 | tf_op jit(solution)/shard_map/cond/branch_1_fun/ppermute | solution.py:423
  33.7 10.4 %collective-permute-start.30 = (f32[400,128]{1,0:T(8,128)S(1)}, f32[400,128]{1,0:T(8,128)S(1)}, u32[]{:S(2)}, u32[]{:S(2)}) collective-permute-start(f32[400,128]{1,0:T(8,128)S(1)} %collective-permute-done.18.refs_12_), channel_id=1, source_target_pairs={{0,1},{1,0},{2,3},{3,2},{4,5},{5,4},{6,7},{7,6},{8,9},{9,8},{10,11... | collective-permute-start | bytes 614408 | tf_op jit(solution)/shard_map/cond/branch_1_fun/ppermute | solution.py:423
  38.1 5.1 %collective-permute-start.23 = (f32[176,128]{1,0:T(8,128)S(1)}, f32[176,128]{1,0:T(8,128)S(1)}, u32[]{:S(2)}, u32[]{:S(2)}) collective-permute-start(f32[176,128]{1,0:T(8,128)S(1)} %slice.47), channel_id=1, source_target_pairs={{4,0},{8,4},{12,8},{14,12},{10,14},{6,10},{2,6},{0,2},{5,1},{9,5},... | collective-permute-start | bytes 270344 | tf_op jit(solution)/shard_map/cond/branch_1_fun/ppermute | solution.py:454
  39.2 4.9 %collective-permute-start.19 = (f32[184,128]{1,0:T(8,128)S(1)}, f32[184,128]{1,0:T(8,128)S(1)}, u32[]{:S(2)}, u32[]{:S(2)}) collective-permute-start(f32[184,128]{1,0:T(8,128)S(1)} %slice.44), channel_id=1, source_target_pairs={{0,4},{4,8},{8,12},{12,14},{14,10},{10,6},{6,2},{2,0},{1,5},{5,9},... | collective-permute-start | bytes 282632 | tf_op jit(solution)/shard_map/cond/branch_1_fun/ppermute | solution.py:453
  40.3 3.8 %copy-start.16 = (f32[80,640]{1,0:T(8,128)S(1)}, f32[80,640]{1,0:T(8,128)}, u32[]{:S(2)}) copy-start(f32[80,640]{1,0:T(8,128)} %get-tuple-element.74.refs_1_.refs_11_.own) | copy-start | bytes 614404 | tf_op jit(solution)/shard_map/cond
  43.2 4.8 %collective-permute-start.25 = (f32[176,128]{1,0:T(8,128)S(1)}, f32[176,128]{1,0:T(8,128)S(1)}, u32[]{:S(2)}, u32[]{:S(2)}) collective-permute-start(f32[176,128]{1,0:T(8,128)S(1)} %collective-permute-done.23.down), channel_id=1, source_target_pairs={{0,1},{1,0},{2,3},{3,2},{4,5},{5,4},{6,7},{7,6},{8,9},{9,8},{10,11... | collective-permute-start | bytes 270344 | tf_op jit(solution)/shard_map/cond/branch_1_fun/ppermute | solution.py:455
  44.1 3.9 %collective-permute-start.24 = (f32[184,128]{1,0:T(8,128)S(1)}, f32[184,128]{1,0:T(8,128)S(1)}, u32[]{:S(2)}, u32[]{:S(2)}) collective-permute-start(f32[184,128]{1,0:T(8,128)S(1)} %collective-permute-done.19.up), channel_id=1, source_target_pairs={{0,1},{1,0},{2,3},{3,2},{4,5},{5,4},{6,7},{7,6},{8,9},{9,8},{10,11... | collective-permute-start | bytes 282632 | tf_op jit(solution)/shard_map/cond/branch_1_fun/ppermute | solution.py:455
  44.1 3.9 %copy-start.4 = (f32[512,256]{1,0:T(8,128)S(1)}, f32[512,256]{1,0:T(8,128)}, u32[]{:S(2)}) copy-start(f32[512,256]{1,0:T(8,128)} %get-tuple-element.98.cross0) | copy-start | bytes 1572868 | tf_op jit(solution)/shard_map/cond
  44.1 3.9 %copy-start.5 = (f32[512,256]{1,0:T(8,128)S(1)}, f32[512,256]{1,0:T(8,128)}, u32[]{:S(2)}) copy-start(f32[512,256]{1,0:T(8,128)} %get-tuple-element.99.diag0) | copy-start | bytes 1572868 | tf_op jit(solution)/shard_map/cond
  44.1 3.9 %copy-start.10 = (f32[512,512]{1,0:T(8,128)S(1)}, f32[512,512]{1,0:T(8,128)}, u32[]{:S(2)}) copy-start(f32[512,512]{1,0:T(8,128)} %get-tuple-element.95.corner.corner1) | copy-start | bytes 3145732 | tf_op jit(solution)/shard_map/cond
  44.2 3.9 %copy-start.12 = (f32[512,256]{1,0:T(8,128)S(1)}, f32[512,256]{1,0:T(8,128)}, u32[]{:S(2)}) copy-start(f32[512,256]{1,0:T(8,128)} %get-tuple-element.96.corner2) | copy-start | bytes 1572868 | tf_op jit(solution)/shard_map/cond

commit v4 on v3

--- a/solution.py
+++ b/solution.py
@@ -113,18 +113,32 @@
     return pl.ds(pl.multiple_of(start, step), size)
 
 
-def factors_kernel(cap, n, anc1, anc2, first, second, link, out, code, m2, most):
+def fetch(pairs, sems):
+    copies = [pltpu.make_async_copy(source, target, sems.at[k]) for k, (source, target) in enumerate(pairs)]
+    for copy in copies:
+        copy.start()
+    return copies
+
+
+def factors_kernel(cap, n, anc1_h, anc2_h, first_h, second_h, link_h, out, code, m2, most, anc1, anc2, first, second, link, sems):
+    loads = fetch(((anc1_h, anc1), (anc2_h, anc2), (first_h, first), (second_h, second), (link_h, link)), sems)
     row = lax.axis_index("row")
     block, width = first.shape
+    loads[0].wait()
     mask1 = marks(anc1[...], n, block)
     code[...] = slot_codes(mask1)
+    most[...] = jnp.broadcast_to(jnp.max(jnp.sum(mask1, axis=1, keepdims=True), axis=0, keepdims=True), most.shape)
+    loads[1].wait()
     m2[...] = marks(anc2[...], n, block)
-    most[0, 0] = jnp.max(jnp.sum(mask1, axis=1, keepdims=True)).astype(jnp.int32)
     pick = picker(code[pl.ds(row, 1), :], cap)
     pick2 = (pick.astype(F32) * m2[pl.ds(row, 1), :]).astype(BF16)
+    loads[2].wait()
     first_c = dot2(pick, split(first[...]), NN)
     out[:, :width] = first_c
-    out[:, width:] = dot2(pick2, split(second[...]), NN) - dot3(split(first_c), split(link[...]), NN)
+    loads[3].wait()
+    second_c = dot2(pick2, split(second[...]), NN)
+    loads[4].wait()
+    out[:, width:] = second_c - dot3(split(first_c), split(link[...]), NN)
 
 
 def place_of(row, n):
@@ -143,29 +157,33 @@
     return [0] + [sign * k for k in range(1, n // 2) for sign in (-1, 1)] + [n // 2]
 
 
-def payload_kernel(cap, n, counts, code, factors, mine, theirs, own, up, down, cols, images, own_ud):
+def payload_kernel(cap, n, counts, code, factors, mine_h, theirs, own, up, down, cols, images, own_ud, spreads, mine, sems):
+    loads = fetch(((mine_h, mine),), sems)
     row, col = lax.axis_index("row"), lax.axis_index("col")
     groups, share, block = mine.shape
     both, half = factors.shape[1], cap // 2
     for g in range(groups):
-        base = g * block
-        cols[rows_at(base + col * share, share), :] = mine[g]
-        cols[rows_at(base + (1 - col) * share, share), :] = theirs[g]
+        cols[rows_at(g * block + (1 - col) * share, share), :] = theirs[g]
+        spreads[g * cap : (g + 1) * cap, :] = picker(code[g : g + 1, :], cap)
+    own_ud[...] = jnp.zeros(own_ud.shape, F32)
     pick = picker(code[pl.ds(row, 1), :], cap)
+    loads[0].wait()
+    for g in range(groups):
+        cols[rows_at(g * block + col * share, share), :] = mine[g]
     images[...] = dot2(pick, split(cols[...]), NT)
     arrivals = arrivals_of(n)
     place = place_of(row, n)
-    own_ud[...] = jnp.zeros(own_ud.shape, F32)
     for d in range(n):
         g = row_of(lax.rem(place + d, n), n)
-        spread = picker(code[pl.ds(g, 1), :], cap)
+        spread = spreads[rows_at(g * cap, cap, 16), :]
         image = images[:, pl.ds(pl.multiple_of(g * block, block), block)]
         value = dot2(spread, split(image), NT, flip=True)
         x = arrivals.index(d if d <= n // 2 else d - n)
-        own[:, x * cap : (x + 1) * cap] = value
+        own[:, both + x * cap : both + (x + 1) * cap] = value
         for way, slot in ((0, (n - d) % n), (1, d)):
             if slot < counts[way]:
                 own_ud[way, :, slot * cap : (slot + 1) * cap] = value
+    own[:, :both] = factors[...]
     mine_rows = rows_at(col * half, half)
     for way, out in ((0, up), (1, down)):
         for c in range(both // LANES):
@@ -213,38 +231,21 @@
     return cross, close
 
 
-def ahead(pieces, slots):
-    lanes = slice(slots[0] * LANES, (slots[-1] + 1) * LANES)
-    total = None
-    for fth, ftl, kh, kl in pieces:
-        value = dot3((kh[:, lanes], kl[:, lanes]), (fth[...], ftl[...]), TN)
-        total = value if total is None else total + value
-    return total
-
-
 def update_kernel(cap, n, k, *refs):
     arrivals = arrivals_of(n)
-    fresh, final = k == 1, k == n // 2 - 1
+    fresh = k == 1
     if fresh:
-        (factors, own), refs = refs[:2], refs[2:]
-        old = ()
+        own, refs = refs[0], refs[1:]
     else:
-        old_v, old_ab, old_ee = refs[:3]
-        refs = refs[3:]
-        old = [refs[4 * m : 4 * m + 4] for m in range(k - 1)]
-        refs = refs[4 * (k - 1) :]
-        if final:
-            own, refs = refs[0], refs[1:]
-    up, down, refs = refs[:2], refs[2:4], refs[4:]
-    fth, ftl, kh, kl, ab, ee, v_next, *refs = refs
-    if final:
-        image, *refs = refs
-    blk, middle, lh, ll, rh, rl = refs
-    both = fth.shape[1]
+        (old_v, old_ab, old_ee, old_image, own), refs = refs[:5], refs[5:]
+    up, down = refs[:2], refs[2:4]
+    v_next, ab, ee, image, blk, middle, fth, ftl, kh, kl, lh, ll, rh, rl = refs[4:]
+    both, half_width = fth.shape[1], ee.shape[1]
     news = ([0] if fresh else []) + [2 * k - 1, 2 * k]
+    later = news[-1] + 1
     size = cap * len(news)
     if fresh:
-        blk[:cap, :both] = factors[...]
+        blk[:cap, :both] = own[:, :both]
     base = len(news) - 2
     assemble(cap, up, blk, base)
     assemble(cap, down, blk, base + 1)
@@ -255,7 +256,7 @@
         rows = slice(a * cap, (a + 1) * cap)
         for y in range(x, n):
             if x == 0:
-                value = own[:, y * cap : (y + 1) * cap]
+                value = own[:, both + y * cap : both + (y + 1) * cap]
             else:
                 way = -1 if arrivals[x] < 0 else 1
                 slot = (way * (arrivals[y] - arrivals[x])) % n
@@ -266,7 +267,8 @@
                 b = news.index(y)
                 middle[rows, b * cap : (b + 1) * cap] = value * 0.5 if y == x else value
             else:
-                kh[rows, y * LANES : y * LANES + cap], kl[rows, y * LANES : y * LANES + cap] = split(value)
+                lanes = slice((y - later) * LANES, (y - later) * LANES + cap)
+                kh[rows, lanes], kl[rows, lanes] = split(value)
     sh, sl = split(blk[:, :both])
     fth[...], ftl[...] = sh, sl
     lh[:size, :], ll[:size, :] = sh, sl
@@ -274,27 +276,20 @@
     if not fresh:
         values = values + jnp.concatenate([old_v[:cap, :], old_v[LANES : LANES + cap, :]], axis=0)
     cross, close = pairs(size, values, lh, ll, rh, rl)
+    to_come = dot3((kh[...], kl[...]), (sh, sl), TN)
+    part = split(own[:, both + news[0] * cap : both + later * cap])
+    f_at, t_at = columns(both, half_width)
+    image_f = dot3(part, (fth[:, f_at], ftl[:, f_at]), NN)
+    image_t = dot3(part, (fth[:, t_at], ftl[:, t_at]), NN)
     if fresh:
-        ab[...], ee[...] = cross, close
+        ab[...], ee[...], v_next[...] = cross, close, to_come
+        image[:, :half_width], image[:, half_width:] = image_f, image_t
     else:
         ab[...] = old_ab[...] + cross
         ee[...] = old_ee[...] + close
-    pieces = [*old, (fth, ftl, kh, kl)]
-    v_next[...] = ahead(pieces, [2 * k + 1] if final else [2 * k + 1, 2 * k + 2])
-    if final:
-        f_at, t_at = columns(both, ee.shape[1])
-        start = 0
-        total_f = total_t = None
-        for ph, pl_, _, _ in pieces:
-            stop = start + ph.shape[0]
-            part = split(own[:, start:stop])
-            value_f = dot3(part, (ph[:, f_at], pl_[:, f_at]), NN)
-            value_t = dot3(part, (ph[:, t_at], pl_[:, t_at]), NN)
-            total_f = value_f if total_f is None else total_f + value_f
-            total_t = value_t if total_t is None else total_t + value_t
-            start = stop
-        image[:, : ee.shape[1]] = total_f
-        image[:, ee.shape[1] :] = total_t
+        v_next[...] = old_v[2 * LANES :, :] + to_come
+        image[:, :half_width] = old_image[:, :half_width] + image_f
+        image[:, half_width:] = old_image[:, half_width:] + image_t
 
 
 def last_kernel(cap, n, up, down, up_far, down_far, old_v, old_ab, old_ee, image, own, code, m2, corner1, corner2, cross0, diag0, *refs):
@@ -330,7 +325,7 @@
     send(corner1_v[...] + (old_ab[:, :half_width] + cross[:, :half_width]), g1_v, g1)
     send(old_ab[:, half_width:] + cross[:, half_width:] - cross0_v[...], xx_v, xx)
     send(corner2_v[...] + (diag0_v[...] + (old_ee[...] + close)), g2_v, g2)
-    k = split(own[:, (n - 1) * cap :])
+    k = split(own[:, both + (n - 1) * cap :])
     pick = picker(code[pl.ds(row, 1), :], cap)
     pick2 = (pick.astype(F32) * m2[pl.ds(row, 1), :]).astype(BF16)
     f_at, t_at = columns(both, half_width)
@@ -350,10 +345,11 @@
             jax.ShapeDtypeStruct((cap, 2 * width), F32),
             jax.ShapeDtypeStruct((n, block), jnp.int32),
             jax.ShapeDtypeStruct((n, block), F32),
-            jax.ShapeDtypeStruct((1, 1), jnp.int32),
+            jax.ShapeDtypeStruct((1, LANES), F32),
         ),
-        in_specs=[VMEM] * 5,
-        out_specs=(VMEM, VMEM, VMEM, SMEM),
+        in_specs=[ANY] * 5,
+        out_specs=(VMEM,) * 4,
+        scratch_shapes=[pltpu.VMEM(v.shape, v.dtype) for v in (anc1, anc2, first_factor, second_factor, second_link)] + [pltpu.SemaphoreType.DMA((5,))],
         cost_estimate=pl.CostEstimate(flops=6 * cap * width * width, bytes_accessed=4 * width * (2 * block + width), transcendentals=0),
         name="factors",
     )(anc1, anc2, first_factor, second_factor, second_link)
@@ -366,20 +362,23 @@
     flats = [jax.ShapeDtypeStruct(((both // LANES + chunks_of(count * cap)) * half, LANES), F32) for count in counts]
     return pl.pallas_call(
         functools.partial(payload_kernel, cap, n, counts),
-        out_shape=(jax.ShapeDtypeStruct((cap, n * cap), F32), *flats),
-        in_specs=[VMEM] * 4,
+        out_shape=(jax.ShapeDtypeStruct((cap, both + n * cap), F32), *flats),
+        in_specs=[VMEM, VMEM, ANY, VMEM],
         out_specs=(VMEM,) * 3,
         scratch_shapes=[
             pltpu.VMEM((n * block, block), F32),
             pltpu.VMEM((cap, n * block), F32),
             pltpu.VMEM((2, cap, chunks_of(counts[0] * cap) * LANES), F32),
+            pltpu.VMEM((n * cap, block), BF16),
+            pltpu.VMEM(mine.shape, F32),
+            pltpu.SemaphoreType.DMA((1,)),
         ],
         cost_estimate=pl.CostEstimate(flops=8 * cap * block * n * block, bytes_accessed=8 * n * block * block, transcendentals=0),
         name="payload",
     )(code, factors, mine, theirs)
 
 
-def gather_branch(cap, n, factors, code, m2, own, own_up, own_down, second_link, first_corner, second_corner):
+def gather_branch(cap, n, code, m2, own, own_up, own_down, second_link, first_corner, second_corner):
     block = code.shape[1]
     width = second_link.shape[0]
     half_width = second_corner.shape[1]
@@ -416,39 +415,35 @@
         return (both // LANES + chunks_of(count * cap)) * half
 
     up, down = own_up, own_down
-    pieces, state, image = [], (), ()
+    state = ()
     for k in range(1, n // 2):
         up = lax.ppermute(up[: flat_rows(n + 1 - 2 * k)], "row", ups)
         down = lax.ppermute(down[: flat_rows(n - 2 * k)], "row", downs)
         up_far, down_far = lax.ppermute(up, "col", swap), lax.ppermute(down, "col", swap)
-        fresh, final = k == 1, k == n // 2 - 1
-        blocks = 3 if fresh else 2
+        blocks = 3 if k == 1 else 2
         size = blocks * cap
-        ins = [factors, own] if fresh else [*state, *(array for piece in pieces for array in piece)]
-        if final and not fresh:
-            ins.append(own)
-        ins += [up, up_far, down, down_far]
-        half_piece = jax.ShapeDtypeStruct((size, both), BF16)
-        outs = [half_piece, half_piece] + [jax.ShapeDtypeStruct((size, n * LANES), BF16)] * 2
-        outs += [jax.ShapeDtypeStruct((width, 2 * half_width), F32), square]
-        outs += [jax.ShapeDtypeStruct(((1 if final else 2) * LANES, both), F32)]
-        if final:
-            outs += [jax.ShapeDtypeStruct((cap, 2 * half_width), F32)]
-        results = pl.pallas_call(
+        later = (n - 1 - 2 * k) * LANES
+        ins = [*state, own, up, up_far, down, down_far]
+        outs = [jax.ShapeDtypeStruct(shape, F32) for shape in ((later, both), (width, 2 * half_width), (width, half_width), (cap, 2 * half_width))]
+        state = pl.pallas_call(
             functools.partial(update_kernel, cap, n, k),
             out_shape=tuple(outs),
             in_specs=[VMEM] * len(ins),
             out_specs=(VMEM,) * len(outs),
-            scratch_shapes=[pltpu.VMEM((size, both + chunks_of((n - 1) * cap) * LANES), F32), pltpu.VMEM((size, size), F32)] + scratch_of(blocks),
+            scratch_shapes=[
+                pltpu.VMEM((size, both + chunks_of((n - 1) * cap) * LANES), F32),
+                pltpu.VMEM((size, size), F32),
+                pltpu.VMEM((size, both), BF16),
+                pltpu.VMEM((size, both), BF16),
+                pltpu.VMEM((size, later), BF16),
+                pltpu.VMEM((size, later), BF16),
+            ]
+            + scratch_of(blocks),
             compiler_params=params,
-            cost_estimate=pl.CostEstimate(flops=6 * size * width * (4 * size + 6 * half_width), bytes_accessed=4 * size * width * 8, transcendentals=0),
+            cost_estimate=pl.CostEstimate(flops=6 * size * width * (2 * size + 2 * later + 6 * half_width), bytes_accessed=4 * size * width * 8, transcendentals=0),
         )(*ins)
-        pieces.append(results[:4])
-        ab, ee, v_next = results[4:7]
-        state = (v_next, ab, ee)
-        image = results[7:]
     rows = flat_rows(1)
-    cut = -(-rows // 16) * 8
+    cut = 3 * rows // 40 * 8
     k = n // 2
     up = lax.ppermute(up[:cut], "row", ups)
     down = lax.ppermute(down[cut:rows], "row", downs)
@@ -467,7 +462,7 @@
         compiler_params=params,
         cost_estimate=pl.CostEstimate(flops=6 * cap * width * (2 * width + 6 * half_width), bytes_accessed=4 * width * width * 5, transcendentals=0),
         name="last",
-    )(up, down, up_far, down_far, *state, *image, own, code, m2, first_corner, second_corner, cross0, diag0)
+    )(up, down, up_far, down_far, *state, own, code, m2, first_corner, second_corner, cross0, diag0)
 
 
 def gather_plan(n, known_inverse, first_factor, first_corner, first_ancestors, second_factor, second_link, second_corner, second_ancestors):
@@ -479,15 +474,15 @@
     factors, code, m2, most = call_factors(cap, n, anc1, anc2, first_factor, second_factor, second_link)
     own = call_payload(cap, n, code, factors, known_inverse, theirs)
 
-    def compact(own, factors, code, m2, known_inverse, theirs, anc1, anc2, first_factor, second_factor, second_link, first_corner, second_corner):
-        return gather_branch(cap, n, factors, code, m2, *own, second_link, first_corner, second_corner)
-
-    def general(own, factors, code, m2, known_inverse, theirs, anc1, anc2, first_factor, second_factor, second_link, first_corner, second_corner):
+    def compact(own, code, m2, known_inverse, theirs, anc1, anc2, first_factor, second_factor, second_link, first_corner, second_corner):
+        return gather_branch(cap, n, code, m2, *own, second_link, first_corner, second_corner)
+
+    def general(own, code, m2, known_inverse, theirs, anc1, anc2, first_factor, second_factor, second_link, first_corner, second_corner):
         factors, code, m2, _ = call_factors(block, n, anc1, anc2, first_factor, second_factor, second_link)
         own = call_payload(block, n, code, factors, known_inverse, theirs)
-        return gather_branch(block, n, factors, code, m2, *own, second_link, first_corner, second_corner)
-
-    operands = (own, factors, code, m2, known_inverse, theirs, anc1, anc2, first_factor, second_factor, second_link, first_corner, second_corner)
+        return gather_branch(block, n, code, m2, *own, second_link, first_corner, second_corner)
+
+    operands = (own, code, m2, known_inverse, theirs, anc1, anc2, first_factor, second_factor, second_link, first_corner, second_corner)
     if cap == block:
         return compact(*operands)
     return lax.cond(most[0, 0] <= cap, compact, general, *operands)

time: 52 us -> 52.2 us (level)
  local copies, waits for them, and re-layouts: 2.9 us -> 0.1 us
  waiting for transfers between devices: 14.1 us -> 15.4 us
  Pallas kernels: 22.1 us -> 23 us
  loops' own time: 0.15 us -> 0.72 us
    ppermute x3, waiting for transfers between devices: 6.07 us -> 15.3 us  [gather_branch(): down = lax.ppermute(down[:flat_rows(n - 2 * k)], 'row', downs)]
    ppermute x3, waiting for transfers between devices: 7.22 us -> 0.09 us  [gather_branch(): up = lax.ppermute(up[:flat_rows(n + 1 - 2 * k)], 'row', ups)]
    ppermute x3, starting transfers between devices: 0.74 us -> 5.67 us  [gather_branch(): down = lax.ppermute(down[:flat_rows(n - 2 * k)], 'row', downs)]
    ppermute x3, starting transfers between devices: 5.99 us -> 1.34 us  [gather_branch(): up = lax.ppermute(up[:flat_rows(n + 1 - 2 * k)], 'row', ups)]
    pallas_call x1, Pallas kernels: 1.68 us -> 3.69 us  [call_payload(): pl.pallas_call(functools.partial(payload_kernel, cap, n, counts), out_sha...]
    pallas_call x3, Pallas kernels: 10.8 us -> 8.89 us  [gather_branch(): pl.pallas_call(functools.partial(update_kernel, cap, n, k), out_shape=tup...]
    ppermute x4, starting transfers between devices: 1.48 us -> 0.09 us  [gather_branch(): lax.ppermute(up, 'col', swap)]
    ppermute x4, starting transfers between devices: 0.08 us -> 1.41 us  [gather_branch(): lax.ppermute(down, 'col', swap)]
  transfers between devices with their start and end apart: 17 -> 17, of which waited for: 3 -> 4; matrix products, arithmetic and copies ran while one was open for 3% -> 0% of each run, Pallas kernels for 33% -> 30%
where the time goes in v4:
time: 52.2 us; the launch traced here: 52 us
  Pallas kernels  23 us (44%)
  waiting for transfers between devices  15.4 us (30%)
  starting transfers between devices  11.2 us (21%)
  between operations  1.52 us (3%)
  loops' own time  0.72 us (1%)
    ppermute x3, waiting for transfers between devices, gather_branch(): down = lax.ppermute(down[:flat_rows(n - 2 * k)], 'row', downs)  15.3 us
    pallas_call x3, Pallas kernels, gather_branch(): pl.pallas_call(functools.partial(update_kernel, cap, n, k), out_shape=tup...  8.89 us
    ppermute x3, starting transfers between devices, gather_branch(): down = lax.ppermute(down[:flat_rows(n - 2 * k)], 'row', downs)  5.67 us
    pallas_call x1, Pallas kernels, gather_branch(): pl.pallas_call(side_kernel, out_shape=(square, square), in_specs=[VMEM] *...  4.16 us
    pallas_call x1, Pallas kernels, call_payload(): pl.pallas_call(functools.partial(payload_kernel, cap, n, counts), out_sha...  3.69 us
    pallas_call x1, Pallas kernels, gather_branch(): pl.pallas_call(functools.partial(last_kernel, cap, n), out_shape=(tall, s...  3.49 us
    pallas_call x1, Pallas kernels, call_factors(): pl.pallas_call(functools.partial(factors_kernel, cap, n), out_shape=(jax....  2.76 us
    ppermute x4, starting transfers between devices, gather_branch(): lax.ppermute(down, 'col', swap)  1.41 us
  transfers between devices with their start and end apart: 17, of which 4 were waited for; matrix products, arithmetic and copies ran while one was open for 0% of the time, Pallas kernels for 30%

profile of v4, /device:TPU:0, one launch (start us, length us, event | category | flops | bytes accessed | tf_op | source)
XLA Modules:
  0.0 52.0 jit_solution(17092957094720697994)
XLA Ops:
  0.6 0.6 %collective-permute-start.32 = (f32[8,64,128]{2,1,0:T(8,128)}, f32[8,64,128]{2,1,0:T(8,128)S(1)}, u32[]{:S(2)}, u32[]{:S(2)}) collective-permute-start(f32[8,64,128]{2,1,0:T(8,128)} %mine_h.1), channel_id=1, source_target_pairs={{0,1},{1,0},{2,3},{3,2},{4,5},{5,4},{6,7},{7,6},{8,9},{9,8},{10,11... | collective-permute-start | bytes 786440 | tf_op jit(solution)/shard_map/ppermute | solution.py:470
  1.2 2.8 %factors.3 = (f32[80,1024]{1,0:T(8,128)}, s32[8,128]{1,0:T(8,128)S(1)}, f32[8,128]{1,0:T(8,128)S(1)}, f32[1,128]{1,0:T(1,128)}) custom-call(s32[1,512]{1,0:T(1,128)} %bitcast.4, s32[1,256]{1,0:T(1,128)} %bitcast.6, f32[128,512]{1,0:T(8,128)} %first_h.1, f32[128,512]{1,0:T(8,128)} %second_h.1, f32[512,512]{1,0:T(8,128)} %link_h.1), custom_call_target="tpu_custom_call" | custom-call | flops 125829120 | bytes 1572864 | tf_op jit(solution)/shard_map/factors/pallas_call | solution.py:342
  4.6 3.7 %payload.3 = (f32[80,1664]{1,0:T(8,128)}, f32[520,128]{1,0:T(8,128)}, f32[480,128]{1,0:T(8,128)}) custom-call(s32[8,128]{1,0:T(8,128)S(1)} %get-tuple-element.98.code, f32[80,1024]{1,0:T(8,128)} %get-tuple-element.99.factors, f32[8,64,128]{2,1,0:T(8,128)} %mine_h.1, f32[8,64,128]{2,1,0:T(8,128)S(1)} %collective-permute-done.32.theirs), custom_call_target="tpu_custom_call" | custom-call | flops 83886080 | bytes 1048576 | tf_op jit(solution)/shard_map/payload/pallas_call | solution.py:363
  8.3 43.4 %conditional.1 = ((f32[128,256]{1,0:T(8,128)}, f32[512,256]{1,0:T(8,128)}, f32[128,256]{1,0:T(8,128)}, f32[512,256]{1,0:T(8,128)}, f32[512,256]{1,0:T(8,128)})) conditional(s32[]{:T(128)} %bitcast.2, (s32[1,512]{1,0:T(1,128)}, s32[1,256]{1,0:T(1,128)}, f32[128,512]{1,0:T(8,128)}, f32[128,512]{1,0:T(8,128)}, f32[512,512]{1,0:T(8,128)}, ...), branch_computations={%region_0.0_spmd, %region_1.0_spmd} | conditional | flops 10401873920 | bytes 68125512 | solution.py:488
  8.6 2.5 %collective-permute-start.20 = (f32[480,128]{1,0:T(8,128)}, f32[480,128]{1,0:T(8,128)S(1)}, u32[]{:S(2)}, u32[]{:S(2)}) collective-permute-start(f32[480,128]{1,0:T(8,128)} %get-tuple-element.64), channel_id=1, source_target_pairs={{4,0},{8,4},{12,8},{14,12},{10,14},{6,10},{2,6},{0,2},{5,1},{9,5},... | collective-permute-start | bytes 737288 | tf_op jit(solution)/shard_map/cond/branch_1_fun/ppermute | solution.py:421
  11.1 0.1 collective-permute-start.16
  11.3 6.8 %collective-permute-done.20.refs_3_ = f32[480,128]{1,0:T(8,128)S(1)} collective-permute-done((f32[480,128]{1,0:T(8,128)}, f32[480,128]{1,0:T(8,128)S(1)}, u32[]{:S(2)}, u32[]{:S(2)}) %collective-permute-start.20) | collective-permute-done | bytes 245792 | tf_op jit(solution)/shard_map/cond/branch_1_fun/ppermute | solution.py:421
  18.0 1.7 %collective-permute-start.21 = (f32[440,128]{1,0:T(8,128)S(1)}, f32[440,128]{1,0:T(8,128)S(1)}, u32[]{:S(2)}, u32[]{:S(2)}) collective-permute-start(f32[440,128]{1,0:T(8,128)S(1)} %slice.49), channel_id=1, source_target_pairs={{4,0},{8,4},{12,8},{14,12},{10,14},{6,10},{2,6},{0,2},{5,1},{9,5},... | collective-permute-start | bytes 675848 | tf_op jit(solution)/shard_map/cond/branch_1_fun/ppermute | solution.py:421
  19.7 0.1 collective-permute-done.16.refs_1_
  19.9 0.5 collective-permute-start.17
  20.3 5.1 %collective-permute-done.21.refs_7_ = f32[440,128]{1,0:T(8,128)S(1)} collective-permute-done((f32[440,128]{1,0:T(8,128)S(1)}, f32[440,128]{1,0:T(8,128)S(1)}, u32[]{:S(2)}, u32[]{:S(2)}) %collective-permute-start.21) | collective-permute-done | bytes 225312 | tf_op jit(solution)/shard_map/cond/branch_1_fun/ppermute | solution.py:421
  25.4 1.4 %collective-permute-start.22 = (f32[400,128]{1,0:T(8,128)S(1)}, f32[400,128]{1,0:T(8,128)S(1)}, u32[]{:S(2)}, u32[]{:S(2)}) collective-permute-start(f32[400,128]{1,0:T(8,128)S(1)} %slice.50), channel_id=1, source_target_pairs={{4,0},{8,4},{12,8},{14,12},{10,14},{6,10},{2,6},{0,2},{5,1},{9,5},... | collective-permute-start | bytes 614408 | tf_op jit(solution)/shard_map/cond/branch_1_fun/ppermute | solution.py:421
  26.9 0.5 collective-permute-start.27
  27.4 0.0 collective-permute-start.29
  27.4 0.0 collective-permute-done.17.refs_5_
  27.4 0.7 %collective-permute-start.18 = (f32[400,128]{1,0:T(8,128)S(1)}, f32[400,128]{1,0:T(8,128)S(1)}, u32[]{:S(2)}, u32[]{:S(2)}) collective-permute-start(f32[400,128]{1,0:T(8,128)S(1)} %slice.47), channel_id=1, source_target_pairs={{0,4},{4,8},{8,12},{12,14},{14,10},{10,6},{6,2},{2,0},{1,5},{5,9},... | collective-permute-start | bytes 614408 | tf_op jit(solution)/shard_map/cond/branch_1_fun/ppermute | solution.py:420
  28.1 3.4 %collective-permute-done.22.refs_7_ = f32[400,128]{1,0:T(8,128)S(1)} collective-permute-done((f32[400,128]{1,0:T(8,128)S(1)}, f32[400,128]{1,0:T(8,128)S(1)}, u32[]{:S(2)}, u32[]{:S(2)}) %collective-permute-start.22) | collective-permute-done | bytes 204832 | tf_op jit(solution)/shard_map/cond/branch_1_fun/ppermute | solution.py:421
  31.5 4.2 %side.3 = (f32[512,256]{1,0:T(8,128)}, f32[512,256]{1,0:T(8,128)}) custom-call(f32[512,512]{1,0:T(8,128)} %get-tuple-element.80.corner.corner1, f32[512,512]{1,0:T(8,128)} %get-tuple-element.82.link), custom_call_target="tpu_custom_call" | custom-call | flops 805306368 | bytes 5242880 | tf_op jit(solution)/shard_map/cond/branch_1_fun/side/pallas_call | solution.py:404
  35.7 1.1 %collective-permute-start.23 = (f32[144,128]{1,0:T(8,128)S(1)}, f32[144,128]{1,0:T(8,128)S(1)}, u32[]{:S(2)}, u32[]{:S(2)}) collective-permute-start(f32[144,128]{1,0:T(8,128)S(1)} %slice.51), channel_id=1, source_target_pairs={{4,0},{8,4},{12,8},{14,12},{10,14},{6,10},{2,6},{0,2},{5,1},{9,5},... | collective-permute-start | bytes 221192 | tf_op jit(solution)/shard_map/cond/branch_1_fun/ppermute | solution.py:449
  36.9 0.3 collective-permute-start.31
  37.2 1.0 %collective-permute-start.19 = (f32[216,128]{1,0:T(8,128)S(1)}, f32[216,128]{1,0:T(8,128)S(1)}, u32[]{:S(2)}, u32[]{:S(2)}) collective-permute-start(f32[216,128]{1,0:T(8,128)S(1)} %slice.48), channel_id=1, source_target_pairs={{0,4},{4,8},{8,12},{12,14},{14,10},{10,6},{6,2},{2,0},{1,5},{5,9},... | collective-permute-start | bytes 331784 | tf_op jit(solution)/shard_map/cond/branch_1_fun/ppermute | solution.py:448
  38.2 3.6 %branch_1_fun.3 = (f32[640,1024]{1,0:T(8,128)S(1)}, f32[512,512]{1,0:T(8,128)S(1)}, f32[512,256]{1,0:T(8,128)S(1)}, f32[80,512]{1,0:T(8,128)S(1)}) custom-call(f32[80,1664]{1,0:T(8,128)S(1)} %copy-done.7, f32[520,128]{1,0:T(8,128)S(1)} %collective-permute-done.16.refs_1_, f32[520,128]{1,0:T(8,128)S(1)} %collective-permute-done.26.refs_2_, ...), custom_call_target="tpu_custom_call" | custom-call | flops 2430074880 | bytes 3932160 | tf_op jit(solution)/shard_map/cond/branch_1_fun/pallas_call | solution.py:428
  41.9 0.6 %collective-permute-start.25 = (f32[144,128]{1,0:T(8,128)S(1)}, f32[144,128]{1,0:T(8,128)S(1)}, u32[]{:S(2)}, u32[]{:S(2)}) collective-permute-start(f32[144,128]{1,0:T(8,128)S(1)} %collective-permute-done.23.down), channel_id=1, source_target_pairs={{0,1},{1,0},{2,3},{3,2},{4,5},{5,4},{6,7},{7,6},{8,9},{9,8},{10,11... | collective-permute-start | bytes 221192 | tf_op jit(solution)/shard_map/cond/branch_1_fun/ppermute | solution.py:450
  42.5 0.0 collective-permute-done.19.up
  42.5 0.1 collective-permute-start.24
  42.6 2.9 %branch_1_fun.4 = (f32[384,1024]{1,0:T(8,128)S(1)}, f32[512,512]{1,0:T(8,128)S(1)}, f32[512,256]{1,0:T(8,128)S(1)}, f32[80,512]{1,0:T(8,128)S(1)}) custom-call(f32[640,1024]{1,0:T(8,128)S(1)} %get-tuple-element.66.refs_0_, f32[512,512]{1,0:T(8,128)S(1)} %get-tuple-element.67.refs_1_, f32[512,256]{1,0:T(8,128)S(1)} %get-tuple-element.68.refs_2_, ...), custom_call_target="tpu_custom_call" | custom-call | flops 1289748480 | bytes 2621440 | tf_op jit(solution)/shard_map/cond/branch_1_fun/pallas_call | solution.py:428
  45.5 0.0 copy-start.3
  45.5 0.0 copy-start.4
  45.5 0.0 copy-start.9
  45.5 0.0 copy-start.11
  45.5 2.4 %branch_1_fun.5 = (f32[128,1024]{1,0:T(8,128)S(1)}, f32[512,512]{1,0:T(8,128)S(1)}, f32[512,256]{1,0:T(8,128)S(1)}, f32[80,512]{1,0:T(8,128)S(1)}) custom-call(f32[384,1024]{1,0:T(8,128)S(1)} %get-tuple-element.70.refs_0_, f32[512,512]{1,0:T(8,128)S(1)} %get-tuple-element.71.refs_1_, f32[512,256]{1,0:T(8,128)S(1)} %get-tuple-element.72.refs_2_, ...), custom_call_target="tpu_custom_call" | custom-call | flops 1038090240 | bytes 2621440 | tf_op jit(solution)/shard_map/cond/branch_1_fun/pallas_call | solution.py:428
  48.0 3.5 %last.3 = (f32[128,256]{1,0:T(8,128)}, f32[512,256]{1,0:T(8,128)}, f32[128,256]{1,0:T(8,128)}, f32[512,256]{1,0:T(8,128)}, f32[512,256]{1,0:T(8,128)}) custom-call(f32[216,128]{1,0:T(8,128)S(1)} %collective-permute-done.19.up, f32[144,128]{1,0:T(8,128)S(1)} %collective-permute-done.23.down, f32[216,128]{1,0:T(8,128)S(1)} %collective-permute-done.24.up_far, ...), custom_call_target="tpu_custom_call" | custom-call | flops 629145600 | bytes 5242880 | tf_op jit(solution)/shard_map/cond/branch_1_fun/last/pallas_call | solution.py:451
  (26 shorter events, 0.1 us)
Async XLA Ops:
  0.6 4.0 %collective-permute-start.32 = (f32[8,64,128]{2,1,0:T(8,128)}, f32[8,64,128]{2,1,0:T(8,128)S(1)}, u32[]{:S(2)}, u32[]{:S(2)}) collective-permute-start(f32[8,64,128]{2,1,0:T(8,128)} %mine_h.1), channel_id=1, source_target_pairs={{0,1},{1,0},{2,3},{3,2},{4,5},{5,4},{6,7},{7,6},{8,9},{9,8},{10,11... | collective-permute-start | bytes 786440 | tf_op jit(solution)/shard_map/ppermute | solution.py:470
  8.6 29.7 %copy-start.7 = (f32[80,1664]{1,0:T(8,128)S(1)}, f32[80,1664]{1,0:T(8,128)}, u32[]{:S(2)}) copy-start(f32[80,1664]{1,0:T(8,128)} %get-tuple-element.65.refs_0_.refs_4_.own) | copy-start | bytes 1597444 | tf_op jit(solution)/shard_map/cond
  8.6 9.5 %collective-permute-start.20 = (f32[480,128]{1,0:T(8,128)}, f32[480,128]{1,0:T(8,128)S(1)}, u32[]{:S(2)}, u32[]{:S(2)}) collective-permute-start(f32[480,128]{1,0:T(8,128)} %get-tuple-element.64), channel_id=1, source_target_pairs={{4,0},{8,4},{12,8},{14,12},{10,14},{6,10},{2,6},{0,2},{5,1},{9,5},... | collective-permute-start | bytes 737288 | tf_op jit(solution)/shard_map/cond/branch_1_fun/ppermute | solution.py:421
  11.1 8.7 %collective-permute-start.16 = (f32[520,128]{1,0:T(8,128)}, f32[520,128]{1,0:T(8,128)S(1)}, u32[]{:S(2)}, u32[]{:S(2)}) collective-permute-start(f32[520,128]{1,0:T(8,128)} %get-tuple-element.63), channel_id=1, source_target_pairs={{0,4},{4,8},{8,12},{12,14},{14,10},{10,6},{6,2},{2,0},{1,5},{5,9},... | collective-permute-start | bytes 798728 | tf_op jit(solution)/shard_map/cond/branch_1_fun/ppermute | solution.py:420
  18.0 7.4 %collective-permute-start.21 = (f32[440,128]{1,0:T(8,128)S(1)}, f32[440,128]{1,0:T(8,128)S(1)}, u32[]{:S(2)}, u32[]{:S(2)}) collective-permute-start(f32[440,128]{1,0:T(8,128)S(1)} %slice.49), channel_id=1, source_target_pairs={{4,0},{8,4},{12,8},{14,12},{10,14},{6,10},{2,6},{0,2},{5,1},{9,5},... | collective-permute-start | bytes 675848 | tf_op jit(solution)/shard_map/cond/branch_1_fun/ppermute | solution.py:421
  19.9 7.5 %collective-permute-start.17 = (f32[480,128]{1,0:T(8,128)S(1)}, f32[480,128]{1,0:T(8,128)S(1)}, u32[]{:S(2)}, u32[]{:S(2)}) collective-permute-start(f32[480,128]{1,0:T(8,128)S(1)} %slice.46), channel_id=1, source_target_pairs={{0,4},{4,8},{8,12},{12,14},{14,10},{10,6},{6,2},{2,0},{1,5},{5,9},... | collective-permute-start | bytes 737288 | tf_op jit(solution)/shard_map/cond/branch_1_fun/ppermute | solution.py:420
  25.4 6.1 %collective-permute-start.22 = (f32[400,128]{1,0:T(8,128)S(1)}, f32[400,128]{1,0:T(8,128)S(1)}, u32[]{:S(2)}, u32[]{:S(2)}) collective-permute-start(f32[400,128]{1,0:T(8,128)S(1)} %slice.50), channel_id=1, source_target_pairs={{4,0},{8,4},{12,8},{14,12},{10,14},{6,10},{2,6},{0,2},{5,1},{9,5},... | collective-permute-start | bytes 614408 | tf_op jit(solution)/shard_map/cond/branch_1_fun/ppermute | solution.py:421
  26.9 10.3 %collective-permute-start.26 = (f32[520,128]{1,0:T(8,128)S(1)}, f32[520,128]{1,0:T(8,128)S(1)}, u32[]{:S(2)}, u32[]{:S(2)}) collective-permute-start(f32[520,128]{1,0:T(8,128)S(1)} %collective-permute-done.16.refs_1_), channel_id=1, source_target_pairs={{0,1},{1,0},{2,3},{3,2},{4,5},{5,4},{6,7},{7,6},{8,9},{9,8},{10,11... | collective-permute-start | bytes 798728 | tf_op jit(solution)/shard_map/cond/branch_1_fun/ppermute | solution.py:422
  26.9 10.0 %collective-permute-start.27 = (f32[480,128]{1,0:T(8,128)S(1)}, f32[480,128]{1,0:T(8,128)S(1)}, u32[]{:S(2)}, u32[]{:S(2)}) collective-permute-start(f32[480,128]{1,0:T(8,128)S(1)} %collective-permute-done.20.refs_3_), channel_id=1, source_target_pairs={{0,1},{1,0},{2,3},{3,2},{4,5},{5,4},{6,7},{7,6},{8,9},{9,8},{10,11... | collective-permute-start | bytes 737288 | tf_op jit(solution)/shard_map/cond/branch_1_fun/ppermute | solution.py:422
  27.4 10.8 %collective-permute-start.29 = (f32[440,128]{1,0:T(8,128)S(1)}, f32[440,128]{1,0:T(8,128)S(1)}, u32[]{:S(2)}, u32[]{:S(2)}) collective-permute-start(f32[440,128]{1,0:T(8,128)S(1)} %collective-permute-done.21.refs_7_), channel_id=1, source_target_pairs={{0,1},{1,0},{2,3},{3,2},{4,5},{5,4},{6,7},{7,6},{8,9},{9,8},{10,11... | collective-permute-start | bytes 675848 | tf_op jit(solution)/shard_map/cond/branch_1_fun/ppermute | solution.py:422
  27.4 8.3 %collective-permute-start.18 = (f32[400,128]{1,0:T(8,128)S(1)}, f32[400,128]{1,0:T(8,128)S(1)}, u32[]{:S(2)}, u32[]{:S(2)}) collective-permute-start(f32[400,128]{1,0:T(8,128)S(1)} %slice.47), channel_id=1, source_target_pairs={{0,4},{4,8},{8,12},{12,14},{14,10},{10,6},{6,2},{2,0},{1,5},{5,9},... | collective-permute-start | bytes 614408 | tf_op jit(solution)/shard_map/cond/branch_1_fun/ppermute | solution.py:420
  31.5 11.0 %collective-permute-start.28 = (f32[480,128]{1,0:T(8,128)S(1)}, f32[480,128]{1,0:T(8,128)S(1)}, u32[]{:S(2)}, u32[]{:S(2)}) collective-permute-start(f32[480,128]{1,0:T(8,128)S(1)} %collective-permute-done.17.refs_5_), channel_id=1, source_target_pairs={{0,1},{1,0},{2,3},{3,2},{4,5},{5,4},{6,7},{7,6},{8,9},{9,8},{10,11... | collective-permute-start | bytes 737288 | tf_op jit(solution)/shard_map/cond/branch_1_fun/ppermute | solution.py:422
  35.7 6.2 %collective-permute-start.23 = (f32[144,128]{1,0:T(8,128)S(1)}, f32[144,128]{1,0:T(8,128)S(1)}, u32[]{:S(2)}, u32[]{:S(2)}) collective-permute-start(f32[144,128]{1,0:T(8,128)S(1)} %slice.51), channel_id=1, source_target_pairs={{4,0},{8,4},{12,8},{14,12},{10,14},{6,10},{2,6},{0,2},{5,1},{9,5},... | collective-permute-start | bytes 221192 | tf_op jit(solution)/shard_map/cond/branch_1_fun/ppermute | solution.py:449
  36.9 8.6 %collective-permute-start.31 = (f32[400,128]{1,0:T(8,128)S(1)}, f32[400,128]{1,0:T(8,128)S(1)}, u32[]{:S(2)}, u32[]{:S(2)}) collective-permute-start(f32[400,128]{1,0:T(8,128)S(1)} %collective-permute-done.22.refs_7_), channel_id=1, source_target_pairs={{0,1},{1,0},{2,3},{3,2},{4,5},{5,4},{6,7},{7,6},{8,9},{9,8},{10,11... | collective-permute-start | bytes 614408 | tf_op jit(solution)/shard_map/cond/branch_1_fun/ppermute | solution.py:422
  37.2 5.3 %collective-permute-start.19 = (f32[216,128]{1,0:T(8,128)S(1)}, f32[216,128]{1,0:T(8,128)S(1)}, u32[]{:S(2)}, u32[]{:S(2)}) collective-permute-start(f32[216,128]{1,0:T(8,128)S(1)} %slice.48), channel_id=1, source_target_pairs={{0,4},{4,8},{8,12},{12,14},{14,10},{10,6},{6,2},{2,0},{1,5},{5,9},... | collective-permute-start | bytes 331784 | tf_op jit(solution)/shard_map/cond/branch_1_fun/ppermute | solution.py:448
  38.2 7.3 %collective-permute-start.30 = (f32[400,128]{1,0:T(8,128)S(1)}, f32[400,128]{1,0:T(8,128)S(1)}, u32[]{:S(2)}, u32[]{:S(2)}) collective-permute-start(f32[400,128]{1,0:T(8,128)S(1)} %collective-permute-done.18.refs_5_), channel_id=1, source_target_pairs={{0,1},{1,0},{2,3},{3,2},{4,5},{5,4},{6,7},{7,6},{8,9},{9,8},{10,11... | collective-permute-start | bytes 614408 | tf_op jit(solution)/shard_map/cond/branch_1_fun/ppermute | solution.py:422
  41.9 6.0 %collective-permute-start.25 = (f32[144,128]{1,0:T(8,128)S(1)}, f32[144,128]{1,0:T(8,128)S(1)}, u32[]{:S(2)}, u32[]{:S(2)}) collective-permute-start(f32[144,128]{1,0:T(8,128)S(1)} %collective-permute-done.23.down), channel_id=1, source_target_pairs={{0,1},{1,0},{2,3},{3,2},{4,5},{5,4},{6,7},{7,6},{8,9},{9,8},{10,11... | collective-permute-start | bytes 221192 | tf_op jit(solution)/shard_map/cond/branch_1_fun/ppermute | solution.py:450
  42.5 5.4 %collective-permute-start.24 = (f32[216,128]{1,0:T(8,128)S(1)}, f32[216,128]{1,0:T(8,128)S(1)}, u32[]{:S(2)}, u32[]{:S(2)}) collective-permute-start(f32[216,128]{1,0:T(8,128)S(1)} %collective-permute-done.19.up), channel_id=1, source_target_pairs={{0,1},{1,0},{2,3},{3,2},{4,5},{5,4},{6,7},{7,6},{8,9},{9,8},{10,11... | collective-permute-start | bytes 331784 | tf_op jit(solution)/shard_map/cond/branch_1_fun/ppermute | solution.py:450
  45.5 2.5 %copy-start.3 = (f32[512,256]{1,0:T(8,128)S(1)}, f32[512,256]{1,0:T(8,128)}, u32[]{:S(2)}) copy-start(f32[512,256]{1,0:T(8,128)} %get-tuple-element.83.cross0) | copy-start | bytes 1572868 | tf_op jit(solution)/shard_map/cond
  45.5 2.5 %copy-start.4 = (f32[512,256]{1,0:T(8,128)S(1)}, f32[512,256]{1,0:T(8,128)}, u32[]{:S(2)}) copy-start(f32[512,256]{1,0:T(8,128)} %get-tuple-element.84.diag0) | copy-start | bytes 1572868 | tf_op jit(solution)/shard_map/cond
  45.5 2.5 %copy-start.9 = (f32[512,512]{1,0:T(8,128)S(1)}, f32[512,512]{1,0:T(8,128)}, u32[]{:S(2)}) copy-start(f32[512,512]{1,0:T(8,128)} %get-tuple-element.80.corner.corner1) | copy-start | bytes 3145732 | tf_op jit(solution)/shard_map/cond
  45.5 2.5 %copy-start.11 = (f32[512,256]{1,0:T(8,128)S(1)}, f32[512,256]{1,0:T(8,128)}, u32[]{:S(2)}) copy-start(f32[512,256]{1,0:T(8,128)} %get-tuple-element.81.corner2) | copy-start | bytes 1572868 | tf_op jit(solution)/shard_map/cond

commit v5 on v4

--- a/solution.py
+++ b/solution.py
@@ -11,6 +11,7 @@
 HIGH = lax.Precision.HIGHEST
 F32, BF16 = jnp.float32, jnp.bfloat16
 LANES = 128
+UNIT = 256
 NN = (((1,), (0,)), ((), ()))
 NT = (((1,), (1,)), ((), ()))
 TN = (((0,), (0,)), ((), ()))
@@ -75,16 +76,28 @@
     return high, (value - high.astype(F32)).astype(BF16)
 
 
+def passes(lefts, rights, dims):
+    (left_axis,), (right_axis,) = dims[0]
+    depth, count = lefts[0].shape[left_axis], len(lefts)
+    if -(-count * depth // UNIT) < count * -(-depth // UNIT):
+        return dot(jnp.concatenate(lefts, axis=left_axis), jnp.concatenate(rights, axis=right_axis), dims)
+    total = None
+    for left, right in zip(lefts, rights):
+        value = dot(left, right, dims)
+        total = value if total is None else total + value
+    return total
+
+
 def dot3(left, right, dims):
     (lh, ll), (rh, rl) = left, right
-    return dot(lh, rh, dims) + (dot(lh, rl, dims) + dot(ll, rh, dims))
+    return passes([lh, ll, lh], [rl, rh, rh], dims)
 
 
 def dot2(exact, right, dims, flip=False):
     rh, rl = right
     if flip:
-        return dot(rh, exact, dims) + dot(rl, exact, dims)
-    return dot(exact, rh, dims) + dot(exact, rl, dims)
+        return passes([rl, rh], [exact, exact], dims)
+    return passes([exact, exact], [rl, rh], dims)
 
 
 def slot_codes(mask):
@@ -120,25 +133,21 @@
     return copies
 
 
-def factors_kernel(cap, n, anc1_h, anc2_h, first_h, second_h, link_h, out, code, m2, most, anc1, anc2, first, second, link, sems):
-    loads = fetch(((anc1_h, anc1), (anc2_h, anc2), (first_h, first), (second_h, second), (link_h, link)), sems)
+def factors_kernel(caps, n, anc1_h, anc2_h, first_h, second_h, first_c, second_c, code1, code2, over, anc1, anc2, first, second, sems):
+    loads = fetch(((anc1_h, anc1), (anc2_h, anc2), (first_h, first), (second_h, second)), sems)
     row = lax.axis_index("row")
-    block, width = first.shape
-    loads[0].wait()
-    mask1 = marks(anc1[...], n, block)
-    code[...] = slot_codes(mask1)
-    most[...] = jnp.broadcast_to(jnp.max(jnp.sum(mask1, axis=1, keepdims=True), axis=0, keepdims=True), most.shape)
-    loads[1].wait()
-    m2[...] = marks(anc2[...], n, block)
-    pick = picker(code[pl.ds(row, 1), :], cap)
-    pick2 = (pick.astype(F32) * m2[pl.ds(row, 1), :]).astype(BF16)
-    loads[2].wait()
-    first_c = dot2(pick, split(first[...]), NN)
-    out[:, :width] = first_c
-    loads[3].wait()
-    second_c = dot2(pick2, split(second[...]), NN)
-    loads[4].wait()
-    out[:, width:] = second_c - dot3(split(first_c), split(link[...]), NN)
+    block = first.shape[0]
+    excess = jnp.zeros((1, 1), F32)
+    for load, ancestors, code, cap in zip(loads, (anc1, anc2), (code1, code2), caps):
+        load.wait()
+        mask = marks(ancestors[...], n, block)
+        code[...] = slot_codes(mask)
+        excess = jnp.maximum(excess, jnp.max(jnp.sum(mask, axis=1, keepdims=True), axis=0, keepdims=True) - cap)
+    over[...] = jnp.broadcast_to(excess, over.shape)
+    for load, source, code, cap, out in zip(loads[2:], (first, second), (code1, code2), caps, (first_c, second_c)):
+        pick = picker(code[pl.ds(row, 1), :], cap)
+        load.wait()
+        out[...] = dot2(pick, split(source[...]), NN)
 
 
 def place_of(row, n):
@@ -157,11 +166,12 @@
     return [0] + [sign * k for k in range(1, n // 2) for sign in (-1, 1)] + [n // 2]
 
 
-def payload_kernel(cap, n, counts, code, factors, mine_h, theirs, own, up, down, cols, images, own_ud, spreads, mine, sems):
+def payload_kernel(caps, n, counts, code, first_c, second_c, mine_h, theirs, own, up, down, cols, images, own_ud, spreads, mine, sems):
     loads = fetch(((mine_h, mine),), sems)
     row, col = lax.axis_index("row"), lax.axis_index("col")
     groups, share, block = mine.shape
-    both, half = factors.shape[1], cap // 2
+    cap, width = caps[0], first_c.shape[1]
+    half, half2 = caps[0] // 2, caps[1] // 2
     for g in range(groups):
         cols[rows_at(g * block + (1 - col) * share, share), :] = theirs[g]
         spreads[g * cap : (g + 1) * cap, :] = picker(code[g : g + 1, :], cap)
@@ -179,35 +189,69 @@
         image = images[:, pl.ds(pl.multiple_of(g * block, block), block)]
         value = dot2(spread, split(image), NT, flip=True)
         x = arrivals.index(d if d <= n // 2 else d - n)
-        own[:, both + x * cap : both + (x + 1) * cap] = value
+        own[:, width + x * cap : width + (x + 1) * cap] = value
         for way, slot in ((0, (n - d) % n), (1, d)):
             if slot < counts[way]:
                 own_ud[way, :, slot * cap : (slot + 1) * cap] = value
-    own[:, :both] = factors[...]
-    mine_rows = rows_at(col * half, half)
+    own[:, :width] = first_c[...]
+    mine_rows, mine_rows2 = rows_at(col * half, half), rows_at(col * half2, half2)
     for way, out in ((0, up), (1, down)):
-        for c in range(both // LANES):
-            out[c * half : (c + 1) * half, :] = factors[mine_rows, c * LANES : (c + 1) * LANES]
+        at = 0
+        for c in range(width // LANES):
+            out[at : at + half, :] = first_c[mine_rows, c * LANES : (c + 1) * LANES]
+            at += half
+        for c in range(width // LANES):
+            out[at : at + half2, :] = second_c[mine_rows2, c * LANES : (c + 1) * LANES]
+            at += half2
         for c in range(chunks_of(counts[way] * cap)):
-            at = both // LANES + c
-            out[at * half : (at + 1) * half, :] = own_ud[way, mine_rows, c * LANES : (c + 1) * LANES]
-
-
-def side_kernel(corner, link, cross0, diag0, link_half):
+            out[at : at + half, :] = own_ud[way, mine_rows, c * LANES : (c + 1) * LANES]
+            at += half
+
+
+def side_kernel(corner, link, cross0, diag0, link_h, link_l, link_half):
     half_width = cross0.shape[1]
     start = pl.multiple_of(lax.axis_index("col") * half_width, half_width)
     link_half[...] = link[:, pl.ds(start, half_width)]
+    link_h[...], link_l[...] = split(link[...])
     value = dot3(split(corner[...]), split(link_half[...]), NN)
     cross0[...] = value
-    diag0[...] = dot3(split(link[...]), split(value), TN)
-
-
-def assemble(cap, flat, blk, k):
+    diag0[...] = dot3((link_h[...], link_l[...]), split(value), TN)
+
+
+def assemble(caps, width, flat, blk, sblk, k):
     col = lax.axis_index("col")
-    half = cap // 2
+    half, half2 = caps[0] // 2, caps[1] // 2
     for value, side in zip(flat, (col, 1 - col)):
-        for c in range(value.shape[0] // half):
-            blk[rows_at(k * cap + side * half, half), c * LANES : (c + 1) * LANES] = value[c * half : (c + 1) * half, :]
+        rows, rows2 = rows_at(k * caps[0] + side * half, half), rows_at(k * caps[1] + side * half2, half2)
+        at = 0
+        for c in range(width // LANES):
+            blk[rows, c * LANES : (c + 1) * LANES] = value[at : at + half, :]
+            at += half
+        for c in range(width // LANES):
+            sblk[rows2, c * LANES : (c + 1) * LANES] = value[at : at + half2, :]
+            at += half2
+        for c in range((value.shape[0] - at) // half):
+            blk[rows, width + c * LANES : width + (c + 1) * LANES] = value[at : at + half, :]
+            at += half
+
+
+def source_row(distance, n):
+    return row_of(lax.rem(place_of(lax.axis_index("row"), n) + distance + n, n), n)
+
+
+def factors_of(caps, n, distances, blk, sblk, code1, code2, link, lh, ll):
+    cap, cap2 = caps
+    width = link[0].shape[0]
+    size = cap * len(distances)
+    first = split(blk[:, :width])
+    lh[:size, :width], ll[:size, :width] = first
+    image = dot3(first, (link[0][...], link[1][...]), NN)
+    for k, distance in enumerate(distances):
+        g = source_row(distance, n)
+        spread = dot(picker(code1[pl.ds(g, 1), :], cap), picker(code2[pl.ds(g, 1), :], cap2), NT).astype(BF16)
+        rows = slice(k * cap, (k + 1) * cap)
+        second = dot2(spread, split(sblk[k * cap2 : (k + 1) * cap2, :]), NN)
+        lh[rows, width:], ll[rows, width:] = split(second - image[rows, :])
 
 
 def columns(both, half_width):
@@ -231,24 +275,29 @@
     return cross, close
 
 
-def update_kernel(cap, n, k, *refs):
+def update_kernel(caps, n, k, *refs):
     arrivals = arrivals_of(n)
     fresh = k == 1
+    cap = caps[0]
+    (own, code1, code2, link_h, link_l), refs = refs[:5], refs[5:]
     if fresh:
-        own, refs = refs[0], refs[1:]
+        own_s, refs = refs[0], refs[1:]
     else:
-        (old_v, old_ab, old_ee, old_image, own), refs = refs[:5], refs[5:]
+        (old_v, old_ab, old_ee, old_image), refs = refs[:4], refs[4:]
     up, down = refs[:2], refs[2:4]
-    v_next, ab, ee, image, blk, middle, fth, ftl, kh, kl, lh, ll, rh, rl = refs[4:]
-    both, half_width = fth.shape[1], ee.shape[1]
+    v_next, ab, ee, image, blk, sblk, middle, kh, kl, lh, ll, rh, rl = refs[4:]
+    both, half_width = lh.shape[1], ee.shape[1]
+    width = both // 2
     news = ([0] if fresh else []) + [2 * k - 1, 2 * k]
     later = news[-1] + 1
     size = cap * len(news)
     if fresh:
-        blk[:cap, :both] = own[:, :both]
+        blk[:cap, :width] = own[:, :width]
+        sblk[: caps[1], :] = own_s[...]
     base = len(news) - 2
-    assemble(cap, up, blk, base)
-    assemble(cap, down, blk, base + 1)
+    assemble(caps, width, up, blk, sblk, base)
+    assemble(caps, width, down, blk, sblk, base + 1)
+    factors_of(caps, n, [arrivals[x] for x in news], blk, sblk, code1, code2, (link_h, link_l), lh, ll)
     middle[...] = jnp.zeros(middle.shape, F32)
     kh[...] = jnp.zeros(kh.shape, BF16)
     kl[...] = jnp.zeros(kl.shape, BF16)
@@ -256,31 +305,29 @@
         rows = slice(a * cap, (a + 1) * cap)
         for y in range(x, n):
             if x == 0:
-                value = own[:, both + y * cap : both + (y + 1) * cap]
+                value = own[:, width + y * cap : width + (y + 1) * cap]
             else:
                 way = -1 if arrivals[x] < 0 else 1
                 slot = (way * (arrivals[y] - arrivals[x])) % n
                 if slot >= n - 2 * k + (1 if way < 0 or slot == 0 else 0):
                     continue
-                value = blk[rows, both + slot * cap : both + (slot + 1) * cap]
+                value = blk[rows, width + slot * cap : width + (slot + 1) * cap]
             if y in news:
                 b = news.index(y)
                 middle[rows, b * cap : (b + 1) * cap] = value * 0.5 if y == x else value
             else:
                 lanes = slice((y - later) * LANES, (y - later) * LANES + cap)
                 kh[rows, lanes], kl[rows, lanes] = split(value)
-    sh, sl = split(blk[:, :both])
-    fth[...], ftl[...] = sh, sl
-    lh[:size, :], ll[:size, :] = sh, sl
+    sh, sl = lh[:size, :], ll[:size, :]
     values = dot3(split(middle[...]), (sh, sl), NN)
     if not fresh:
         values = values + jnp.concatenate([old_v[:cap, :], old_v[LANES : LANES + cap, :]], axis=0)
     cross, close = pairs(size, values, lh, ll, rh, rl)
     to_come = dot3((kh[...], kl[...]), (sh, sl), TN)
-    part = split(own[:, both + news[0] * cap : both + later * cap])
+    part = split(own[:, width + news[0] * cap : width + later * cap])
     f_at, t_at = columns(both, half_width)
-    image_f = dot3(part, (fth[:, f_at], ftl[:, f_at]), NN)
-    image_t = dot3(part, (fth[:, t_at], ftl[:, t_at]), NN)
+    image_f = dot3(part, (lh[:size, f_at], ll[:size, f_at]), NN)
+    image_t = dot3(part, (lh[:size, t_at], ll[:size, t_at]), NN)
     if fresh:
         ab[...], ee[...], v_next[...] = cross, close, to_come
         image[:, :half_width], image[:, half_width:] = image_f, image_t
@@ -292,8 +339,9 @@
         image[:, half_width:] = old_image[:, half_width:] + image_t
 
 
-def last_kernel(cap, n, up, down, up_far, down_far, old_v, old_ab, old_ee, image, own, code, m2, corner1, corner2, cross0, diag0, *refs):
-    c1, g1, c2, xx, g2, flat, flat_far, blk, lh, ll, rh, rl, c1_v, g1_v, c2_v, xx_v, g2_v, corner1_v, corner2_v, cross0_v, diag0_v, sems = refs
+def last_kernel(caps, n, up, down, up_far, down_far, old_v, old_ab, old_ee, image, own, code1, code2, link_h, link_l, corner1, corner2, cross0, diag0, *refs):
+    cap = caps[0]
+    c1, g1, c2, xx, g2, flat, flat_far, blk, sblk, lh, ll, rh, rl, c1_v, g1_v, c2_v, xx_v, g2_v, corner1_v, corner2_v, cross0_v, diag0_v, sems = refs
     row, col = lax.axis_index("row"), lax.axis_index("col")
     both, half_width = lh.shape[1], old_ee.shape[1]
     half_at = pl.ds(pl.multiple_of(col * half_width, half_width), half_width)
@@ -308,10 +356,10 @@
     cut = up.shape[0]
     flat[:cut, :], flat[cut:, :] = up[...], down[...]
     flat_far[:cut, :], flat_far[cut:, :] = up_far[...], down_far[...]
-    assemble(cap, (flat, flat_far), blk, 0)
-    sh, sl = split(blk[:, :both])
-    lh[:cap, :], ll[:cap, :] = sh, sl
-    values = dot3(split(blk[:, both : both + cap] * 0.5), (sh, sl), NN) + old_v[:cap, :]
+    width = both // 2
+    assemble(caps, width, (flat, flat_far), blk, sblk, 0)
+    factors_of(caps, n, [n // 2], blk, sblk, code1, code2, (link_h, link_l), lh, ll)
+    values = dot3(split(blk[:, width : width + cap] * 0.5), (lh[:cap, :], ll[:cap, :]), NN) + old_v[:cap, :]
     cross, close = pairs(cap, values, lh, ll, rh, rl)
     for load in loads:
         load.wait()
@@ -325,9 +373,9 @@
     send(corner1_v[...] + (old_ab[:, :half_width] + cross[:, :half_width]), g1_v, g1)
     send(old_ab[:, half_width:] + cross[:, half_width:] - cross0_v[...], xx_v, xx)
     send(corner2_v[...] + (diag0_v[...] + (old_ee[...] + close)), g2_v, g2)
-    k = split(own[:, both + (n - 1) * cap :])
-    pick = picker(code[pl.ds(row, 1), :], cap)
-    pick2 = (pick.astype(F32) * m2[pl.ds(row, 1), :]).astype(BF16)
+    k = split(own[:, width + (n - 1) * cap :])
+    pick = picker(code1[pl.ds(row, 1), :], cap)
+    pick2 = (pick.astype(F32) * (code2[pl.ds(row, 1), :] >= 0).astype(F32)).astype(BF16)
     f_at, t_at = columns(both, half_width)
     image_f = image[:, :half_width] + dot3(k, (lh[:cap, f_at], ll[:cap, f_at]), NN)
     send(-dot2(pick, split(image_f), TN), c1_v, c1)
@@ -337,33 +385,35 @@
         copy.wait()
 
 
-def call_factors(cap, n, anc1, anc2, first_factor, second_factor, second_link):
+def call_factors(caps, n, anc1, anc2, first_factor, second_factor):
     block, width = first_factor.shape
+    codes = jax.ShapeDtypeStruct((n, block), jnp.int32)
     return pl.pallas_call(
-        functools.partial(factors_kernel, cap, n),
+        functools.partial(factors_kernel, caps, n),
         out_shape=(
-            jax.ShapeDtypeStruct((cap, 2 * width), F32),
-            jax.ShapeDtypeStruct((n, block), jnp.int32),
-            jax.ShapeDtypeStruct((n, block), F32),
+            jax.ShapeDtypeStruct((caps[0], width), F32),
+            jax.ShapeDtypeStruct((caps[1], width), F32),
+            codes,
+            codes,
             jax.ShapeDtypeStruct((1, LANES), F32),
         ),
-        in_specs=[ANY] * 5,
-        out_specs=(VMEM,) * 4,
-        scratch_shapes=[pltpu.VMEM(v.shape, v.dtype) for v in (anc1, anc2, first_factor, second_factor, second_link)] + [pltpu.SemaphoreType.DMA((5,))],
-        cost_estimate=pl.CostEstimate(flops=6 * cap * width * width, bytes_accessed=4 * width * (2 * block + width), transcendentals=0),
+        in_specs=[ANY] * 4,
+        out_specs=(VMEM,) * 5,
+        scratch_shapes=[pltpu.VMEM(v.shape, v.dtype) for v in (anc1, anc2, first_factor, second_factor)] + [pltpu.SemaphoreType.DMA((4,))],
+        cost_estimate=pl.CostEstimate(flops=8 * sum(caps) * block * width, bytes_accessed=8 * width * block, transcendentals=0),
         name="factors",
-    )(anc1, anc2, first_factor, second_factor, second_link)
-
-
-def call_payload(cap, n, code, factors, mine, theirs):
+    )(anc1, anc2, first_factor, second_factor)
+
+
+def call_payload(caps, n, code, first_c, second_c, mine, theirs):
     _, _, block = mine.shape
-    both, half = factors.shape[1], cap // 2
+    cap, width = first_c.shape
     counts = (n - 1, n - 2)
-    flats = [jax.ShapeDtypeStruct(((both // LANES + chunks_of(count * cap)) * half, LANES), F32) for count in counts]
+    flats = [jax.ShapeDtypeStruct((flat_rows(caps, width, count), LANES), F32) for count in counts]
     return pl.pallas_call(
-        functools.partial(payload_kernel, cap, n, counts),
-        out_shape=(jax.ShapeDtypeStruct((cap, both + n * cap), F32), *flats),
-        in_specs=[VMEM, VMEM, ANY, VMEM],
+        functools.partial(payload_kernel, caps, n, counts),
+        out_shape=(jax.ShapeDtypeStruct((cap, width + n * cap), F32), *flats),
+        in_specs=[VMEM, VMEM, VMEM, ANY, VMEM],
         out_specs=(VMEM,) * 3,
         scratch_shapes=[
             pltpu.VMEM((n * block, block), F32),
@@ -375,14 +425,19 @@
         ],
         cost_estimate=pl.CostEstimate(flops=8 * cap * block * n * block, bytes_accessed=8 * n * block * block, transcendentals=0),
         name="payload",
-    )(code, factors, mine, theirs)
-
-
-def gather_branch(cap, n, code, m2, own, own_up, own_down, second_link, first_corner, second_corner):
-    block = code.shape[1]
+    )(code, first_c, second_c, mine, theirs)
+
+
+def flat_rows(caps, width, count):
+    return width // LANES * (caps[0] // 2 + caps[1] // 2) + chunks_of(count * caps[0]) * (caps[0] // 2)
+
+
+def gather_branch(caps, n, code1, code2, second_c, own, own_up, own_down, second_link, first_corner, second_corner):
+    cap = caps[0]
+    block = code1.shape[1]
     width = second_link.shape[0]
     half_width = second_corner.shape[1]
-    half, both = cap // 2, 2 * width
+    both = 2 * width
     square = jax.ShapeDtypeStruct((width, half_width), F32)
     tall = jax.ShapeDtypeStruct((block, half_width), F32)
 
@@ -401,40 +456,37 @@
         ]
 
     params = pltpu.CompilerParams(vmem_limit_bytes=40 << 20)
-    cross0, diag0 = pl.pallas_call(
+    part = pltpu.VMEM((width, width), BF16)
+    cross0, diag0, link_h, link_l = pl.pallas_call(
         side_kernel,
-        out_shape=(square, square),
+        out_shape=(square, square, part, part),
         in_specs=[VMEM] * 2,
-        out_specs=(VMEM, VMEM),
+        out_specs=(VMEM,) * 4,
         scratch_shapes=[pltpu.VMEM((width, half_width), F32)],
         cost_estimate=pl.CostEstimate(flops=12 * width * width * half_width, bytes_accessed=20 * width * width, transcendentals=0),
         name="side",
     )(first_corner, second_link)
 
-    def flat_rows(count):
-        return (both // LANES + chunks_of(count * cap)) * half
-
     up, down = own_up, own_down
     state = ()
     for k in range(1, n // 2):
-        up = lax.ppermute(up[: flat_rows(n + 1 - 2 * k)], "row", ups)
-        down = lax.ppermute(down[: flat_rows(n - 2 * k)], "row", downs)
+        up = lax.ppermute(up[: flat_rows(caps, width, n + 1 - 2 * k)], "row", ups)
+        down = lax.ppermute(down[: flat_rows(caps, width, n - 2 * k)], "row", downs)
         up_far, down_far = lax.ppermute(up, "col", swap), lax.ppermute(down, "col", swap)
         blocks = 3 if k == 1 else 2
         size = blocks * cap
         later = (n - 1 - 2 * k) * LANES
-        ins = [*state, own, up, up_far, down, down_far]
+        ins = [own, code1, code2, link_h, link_l, *(state or (second_c,)), up, up_far, down, down_far]
         outs = [jax.ShapeDtypeStruct(shape, F32) for shape in ((later, both), (width, 2 * half_width), (width, half_width), (cap, 2 * half_width))]
         state = pl.pallas_call(
-            functools.partial(update_kernel, cap, n, k),
+            functools.partial(update_kernel, caps, n, k),
             out_shape=tuple(outs),
             in_specs=[VMEM] * len(ins),
             out_specs=(VMEM,) * len(outs),
             scratch_shapes=[
-                pltpu.VMEM((size, both + chunks_of((n - 1) * cap) * LANES), F32),
+                pltpu.VMEM((size, width + chunks_of((n - 1) * cap) * LANES), F32),
+                pltpu.VMEM((blocks * caps[1], width), F32),
                 pltpu.VMEM((size, size), F32),
-                pltpu.VMEM((size, both), BF16),
-                pltpu.VMEM((size, both), BF16),
                 pltpu.VMEM((size, later), BF16),
                 pltpu.VMEM((size, later), BF16),
             ]
@@ -442,19 +494,19 @@
             compiler_params=params,
             cost_estimate=pl.CostEstimate(flops=6 * size * width * (2 * size + 2 * later + 6 * half_width), bytes_accessed=4 * size * width * 8, transcendentals=0),
         )(*ins)
-    rows = flat_rows(1)
+    rows = flat_rows(caps, width, 1)
     cut = 3 * rows // 40 * 8
     k = n // 2
     up = lax.ppermute(up[:cut], "row", ups)
     down = lax.ppermute(down[cut:rows], "row", downs)
     up_far, down_far = lax.ppermute(up, "col", swap), lax.ppermute(down, "col", swap)
     return pl.pallas_call(
-        functools.partial(last_kernel, cap, n),
+        functools.partial(last_kernel, caps, n),
         out_shape=(tall, square, tall, square, square),
-        in_specs=[VMEM] * 11 + [ANY] * 4,
+        in_specs=[VMEM] * 13 + [ANY] * 4,
         out_specs=(ANY,) * 5,
         scratch_shapes=[pltpu.VMEM((rows, LANES), F32)] * 2
-        + [pltpu.VMEM((cap, both + chunks_of(cap) * LANES), F32)]
+        + [pltpu.VMEM((cap, width + chunks_of(cap) * LANES), F32), pltpu.VMEM((caps[1], width), F32)]
         + scratch_of(1)
         + [pltpu.VMEM(shape.shape, F32) for shape in (tall, square, tall, square, square)]
         + [pltpu.VMEM(square.shape, F32)] * 4
@@ -462,30 +514,31 @@
         compiler_params=params,
         cost_estimate=pl.CostEstimate(flops=6 * cap * width * (2 * width + 6 * half_width), bytes_accessed=4 * width * width * 5, transcendentals=0),
         name="last",
-    )(up, down, up_far, down_far, *state, own, code, m2, first_corner, second_corner, cross0, diag0)
+    )(up, down, up_far, down_far, *state, own, code1, code2, link_h, link_l, first_corner, second_corner, cross0, diag0)
 
 
 def gather_plan(n, known_inverse, first_factor, first_corner, first_ancestors, second_factor, second_link, second_corner, second_ancestors):
     _, _, block = known_inverse.shape
     theirs = lax.ppermute(known_inverse, "col", [(0, 1), (1, 0)])
     anc1, anc2 = first_ancestors[None, :], second_ancestors[None, :]
-    mean = -(-first_ancestors.shape[0] // n)
-    cap = min(-(-mean * 5 // 64) * 16, block)
-    factors, code, m2, most = call_factors(cap, n, anc1, anc2, first_factor, second_factor, second_link)
-    own = call_payload(cap, n, code, factors, known_inverse, theirs)
-
-    def compact(own, code, m2, known_inverse, theirs, anc1, anc2, first_factor, second_factor, second_link, first_corner, second_corner):
-        return gather_branch(cap, n, code, m2, *own, second_link, first_corner, second_corner)
-
-    def general(own, code, m2, known_inverse, theirs, anc1, anc2, first_factor, second_factor, second_link, first_corner, second_corner):
-        factors, code, m2, _ = call_factors(block, n, anc1, anc2, first_factor, second_factor, second_link)
-        own = call_payload(block, n, code, factors, known_inverse, theirs)
-        return gather_branch(block, n, code, m2, *own, second_link, first_corner, second_corner)
-
-    operands = (own, code, m2, known_inverse, theirs, anc1, anc2, first_factor, second_factor, second_link, first_corner, second_corner)
-    if cap == block:
+    mean1, mean2 = -(-first_ancestors.shape[0] // n), -(-second_ancestors.shape[0] // n)
+    caps = (min(-(-mean1 * 5 // 64) * 16, block), min(-(-mean2 * 3 // 32) * 16, block))
+    first_c, second_c, code1, code2, over = call_factors(caps, n, anc1, anc2, first_factor, second_factor)
+    own = call_payload(caps, n, code1, first_c, second_c, known_inverse, theirs)
+
+    def compact(own, second_c, code1, code2, known_inverse, theirs, anc1, anc2, first_factor, second_factor, second_link, first_corner, second_corner):
+        return gather_branch(caps, n, code1, code2, second_c, *own, second_link, first_corner, second_corner)
+
+    def general(own, second_c, code1, code2, known_inverse, theirs, anc1, anc2, first_factor, second_factor, second_link, first_corner, second_corner):
+        every = (block, block)
+        first_c, second_c, code1, code2, _ = call_factors(every, n, anc1, anc2, first_factor, second_factor)
+        own = call_payload(every, n, code1, first_c, second_c, known_inverse, theirs)
+        return gather_branch(every, n, code1, code2, second_c, *own, second_link, first_corner, second_corner)
+
+    operands = (own, second_c, code1, code2, known_inverse, theirs, anc1, anc2, first_factor, second_factor, second_link, first_corner, second_corner)
+    if caps == (block, block):
         return compact(*operands)
-    return lax.cond(most[0, 0] <= cap, compact, general, *operands)
+    return lax.cond(over[0, 0] <= 0, compact, general, *operands)
 
 
 def solution(mesh):

time: 52.2 us -> 50.5 us (0.967)
  waiting for transfers between devices: 15.4 us -> 12.1 us
  Pallas kernels: 23 us -> 24.1 us
    ppermute x6, waiting for transfers between devices: 15.4 us -> 11.8 us  [the longest x3 6.47 us: gather_branch(): up = lax.ppermute(up[:flat_rows(caps, width, n + 1 - 2 * k)], 'row', ups)]
    ppermute x4, starting transfers between devices: 0.09 us -> 1.38 us  [gather_branch(): lax.ppermute(up, 'col', swap)]
    pallas_call x7, Pallas kernels: 23 us -> 24.1 us  [the longest x3 10.6 us: gather_branch(): pl.pallas_call(functools.partial(update_kernel, caps, n, k), out_shape=tu...]
    ppermute x4, starting transfers between devices: 1.41 us -> 0.52 us  [gather_branch(): lax.ppermute(down, 'col', swap)]
    ppermute x1, starting transfers between devices: 1.03 us -> 1.86 us  [gather_branch(): up = lax.ppermute(up[:cut], 'row', ups)]
    ppermute x1, starting transfers between devices: 1.13 us -> 0.53 us  [gather_branch(): down = lax.ppermute(down[cut:rows], 'row', downs)]
  transfers between devices with their start and end apart: 17 -> 17, of which waited for: 4 -> 3; matrix products, arithmetic and copies ran while one was open for 0% -> 0% of each run, Pallas kernels for 30% -> 34%
where the time goes in v5:
time: 50.5 us; the launch traced here: 50.3 us
  Pallas kernels  24.1 us (48%)
  waiting for transfers between devices  12.1 us (24%)
  starting transfers between devices  11.7 us (23%)
  between operations  1.52 us (3%)
  loops' own time  0.7 us (1%)
    pallas_call x3, Pallas kernels, gather_branch(): pl.pallas_call(functools.partial(update_kernel, caps, n, k), out_shape=tu...  10.6 us
    ppermute x3, waiting for transfers between devices, gather_branch(): up = lax.ppermute(up[:flat_rows(caps, width, n + 1 - 2 * k)], 'row', ups)  6.47 us
    ppermute x3, starting transfers between devices, gather_branch(): up = lax.ppermute(up[:flat_rows(caps, width, n + 1 - 2 * k)], 'row', ups)  6.11 us
    ppermute x3, waiting for transfers between devices, gather_branch(): down = lax.ppermute(down[:flat_rows(caps, width, n - 2 * k)], 'row', downs)  5.37 us
    pallas_call x1, Pallas kernels, gather_branch(): pl.pallas_call(side_kernel, out_shape=(square, square, part, part), in_sp...  4.16 us
    pallas_call x1, Pallas kernels, call_payload(): pl.pallas_call(functools.partial(payload_kernel, caps, n, counts), out_sh...  3.53 us
    pallas_call x1, Pallas kernels, gather_branch(): pl.pallas_call(functools.partial(last_kernel, caps, n), out_shape=(tall,...  3.48 us
    pallas_call x1, Pallas kernels, call_factors(): pl.pallas_call(functools.partial(factors_kernel, caps, n), out_shape=(jax...  2.3 us
  transfers between devices with their start and end apart: 17, of which 3 were waited for; matrix products, arithmetic and copies ran while one was open for 0% of the time, Pallas kernels for 34%

profile of v5, /device:TPU:0, one launch (start us, length us, event | category | flops | bytes accessed | tf_op | source)
XLA Modules:
  0.0 50.3 jit_solution(16910667583700295018)
XLA Ops:
  0.6 0.6 %collective-permute-start.32 = (f32[8,64,128]{2,1,0:T(8,128)}, f32[8,64,128]{2,1,0:T(8,128)S(1)}, u32[]{:S(2)}, u32[]{:S(2)}) collective-permute-start(f32[8,64,128]{2,1,0:T(8,128)} %mine_h.1), channel_id=1, source_target_pairs={{0,1},{1,0},{2,3},{3,2},{4,5},{5,4},{6,7},{7,6},{8,9},{9,8},{10,11... | collective-permute-start | bytes 786440 | tf_op jit(solution)/shard_map/ppermute | solution.py:522
  1.2 2.3 %factors.3 = (f32[80,512]{1,0:T(8,128)}, f32[48,512]{1,0:T(8,128)}, s32[8,128]{1,0:T(8,128)S(1)}, s32[8,128]{1,0:T(8,128)S(1)}, f32[1,128]{1,0:T(1,128)}) custom-call(s32[1,512]{1,0:T(1,128)} %bitcast.4, s32[1,256]{1,0:T(1,128)} %bitcast.6, f32[128,512]{1,0:T(8,128)} %first_h.1, f32[128,512]{1,0:T(8,128)} %second_h.1), custom_call_target="tpu_custom_call" | custom-call | flops 67108864 | bytes 524288 | tf_op jit(solution)/shard_map/factors/pallas_call | solution.py:391
  4.2 0.0 collective-permute-done.32.theirs
  4.2 3.5 %payload.3 = (f32[80,1152]{1,0:T(8,128)}, f32[456,128]{1,0:T(8,128)}, f32[416,128]{1,0:T(8,128)}) custom-call(s32[8,128]{1,0:T(8,128)S(1)} %get-tuple-element.107.code, f32[80,512]{1,0:T(8,128)} %get-tuple-element.108.first_c, f32[48,512]{1,0:T(8,128)} %get-tuple-element.109.second_c, f32[8,64,128]{2,1,0:T(8,128)} %mine_h.1, ...), custom_call_target="tpu_custom_call" | custom-call | flops 83886080 | bytes 1048576 | tf_op jit(solution)/shard_map/payload/pallas_call | solution.py:413
  7.7 42.3 %conditional.1 = ((f32[128,256]{1,0:T(8,128)}, f32[512,256]{1,0:T(8,128)}, f32[128,256]{1,0:T(8,128)}, f32[512,256]{1,0:T(8,128)}, f32[512,256]{1,0:T(8,128)})) conditional(s32[]{:T(128)} %bitcast.2, (s32[1,512]{1,0:T(1,128)}, s32[1,256]{1,0:T(1,128)}, f32[128,512]{1,0:T(8,128)}, f32[128,512]{1,0:T(8,128)}, f32[8,64,128]{2,1,0:T(8,128)}, ...), branch_computations={%region_0.0_spmd, %region_1.0_spmd} | conditional | flops 10334765056 | bytes 69698464 | solution.py:541
  8.0 2.6 %collective-permute-start.16 = (f32[456,128]{1,0:T(8,128)}, f32[456,128]{1,0:T(8,128)S(1)}, u32[]{:S(2)}, u32[]{:S(2)}) collective-permute-start(f32[456,128]{1,0:T(8,128)} %get-tuple-element.68), channel_id=1, source_target_pairs={{0,4},{4,8},{8,12},{12,14},{14,10},{10,6},{6,2},{2,0},{1,5},{5,9},... | collective-permute-start | bytes 700424 | tf_op jit(solution)/shard_map/cond/branch_1_fun/ppermute | solution.py:473
  10.6 0.0 collective-permute-start.20
  10.6 6.5 %collective-permute-done.16.refs_6_ = f32[456,128]{1,0:T(8,128)S(1)} collective-permute-done((f32[456,128]{1,0:T(8,128)}, f32[456,128]{1,0:T(8,128)S(1)}, u32[]{:S(2)}, u32[]{:S(2)}) %collective-permute-start.16) | collective-permute-done | bytes 233504 | tf_op jit(solution)/shard_map/cond/branch_1_fun/ppermute | solution.py:473
  17.1 1.9 %collective-permute-start.17 = (f32[416,128]{1,0:T(8,128)S(1)}, f32[416,128]{1,0:T(8,128)S(1)}, u32[]{:S(2)}, u32[]{:S(2)}) collective-permute-start(f32[416,128]{1,0:T(8,128)S(1)} %slice.46), channel_id=1, source_target_pairs={{0,4},{4,8},{8,12},{12,14},{14,10},{10,6},{6,2},{2,0},{1,5},{5,9},... | collective-permute-start | bytes 638984 | tf_op jit(solution)/shard_map/cond/branch_1_fun/ppermute | solution.py:473
  19.0 0.0 collective-permute-done.20.refs_8_
  19.0 0.2 collective-permute-start.21
  19.2 0.5 %collective-permute-start.27 = (f32[416,128]{1,0:T(8,128)S(1)}, f32[416,128]{1,0:T(8,128)S(1)}, u32[]{:S(2)}, u32[]{:S(2)}) collective-permute-start(f32[416,128]{1,0:T(8,128)S(1)} %collective-permute-done.20.refs_8_), channel_id=1, source_target_pairs={{0,1},{1,0},{2,3},{3,2},{4,5},{5,4},{6,7},{7,6},{8,9},{9,8},{10,11... | collective-permute-start | bytes 638984 | tf_op jit(solution)/shard_map/cond/branch_1_fun/ppermute | solution.py:475
  19.7 5.4 %collective-permute-done.21.refs_11_ = f32[376,128]{1,0:T(8,128)S(1)} collective-permute-done((f32[376,128]{1,0:T(8,128)S(1)}, f32[376,128]{1,0:T(8,128)S(1)}, u32[]{:S(2)}, u32[]{:S(2)}) %collective-permute-start.21) | collective-permute-done | bytes 192544 | tf_op jit(solution)/shard_map/cond/branch_1_fun/ppermute | solution.py:474
  25.1 0.5 %collective-permute-start.22 = (f32[336,128]{1,0:T(8,128)S(1)}, f32[336,128]{1,0:T(8,128)S(1)}, u32[]{:S(2)}, u32[]{:S(2)}) collective-permute-start(f32[336,128]{1,0:T(8,128)S(1)} %slice.50), channel_id=1, source_target_pairs={{4,0},{8,4},{12,8},{14,12},{10,14},{6,10},{2,6},{0,2},{5,1},{9,5},... | collective-permute-start | bytes 516104 | tf_op jit(solution)/shard_map/cond/branch_1_fun/ppermute | solution.py:474
  25.7 1.6 %collective-permute-start.18 = (f32[336,128]{1,0:T(8,128)S(1)}, f32[336,128]{1,0:T(8,128)S(1)}, u32[]{:S(2)}, u32[]{:S(2)}) collective-permute-start(f32[336,128]{1,0:T(8,128)S(1)} %slice.47), channel_id=1, source_target_pairs={{0,4},{4,8},{8,12},{12,14},{14,10},{10,6},{6,2},{2,0},{1,5},{5,9},... | collective-permute-start | bytes 516104 | tf_op jit(solution)/shard_map/cond/branch_1_fun/ppermute | solution.py:473
  27.3 4.2 %side.3 = (f32[512,256]{1,0:T(8,128)}, f32[512,256]{1,0:T(8,128)}, bf16[512,512]{1,0:T(8,128)(2,1)S(1)}, bf16[512,512]{1,0:T(8,128)(2,1)S(1)}) custom-call(f32[512,512]{1,0:T(8,128)} %get-tuple-element.73.corner.corner1, f32[512,512]{1,0:T(8,128)} %get-tuple-element.74.link), custom_call_target="tpu_custom_call" | custom-call | flops 805306368 | bytes 5242880 | tf_op jit(solution)/shard_map/cond/branch_1_fun/side/pallas_call | solution.py:460
  31.4 0.0 collective-permute-start.29
  31.4 0.0 collective-permute-done.22.refs_11_
  31.4 0.5 %collective-permute-start.28 = (f32[416,128]{1,0:T(8,128)S(1)}, f32[416,128]{1,0:T(8,128)S(1)}, u32[]{:S(2)}, u32[]{:S(2)}) collective-permute-start(f32[416,128]{1,0:T(8,128)S(1)} %collective-permute-done.17.refs_9_), channel_id=1, source_target_pairs={{0,1},{1,0},{2,3},{3,2},{4,5},{5,4},{6,7},{7,6},{8,9},{9,8},{10,11... | collective-permute-start | bytes 638984 | tf_op jit(solution)/shard_map/cond/branch_1_fun/ppermute | solution.py:475
  31.9 0.0 collective-permute-done.27.refs_9_
  32.0 0.5 %collective-permute-start.23 = (f32[120,128]{1,0:T(8,128)S(1)}, f32[120,128]{1,0:T(8,128)S(1)}, u32[]{:S(2)}, u32[]{:S(2)}) collective-permute-start(f32[120,128]{1,0:T(8,128)S(1)} %slice.51), channel_id=1, source_target_pairs={{4,0},{8,4},{12,8},{14,12},{10,14},{6,10},{2,6},{0,2},{5,1},{9,5},... | collective-permute-start | bytes 184328 | tf_op jit(solution)/shard_map/cond/branch_1_fun/ppermute | solution.py:501
  32.5 0.5 %collective-permute-start.30 = (f32[336,128]{1,0:T(8,128)S(1)}, f32[336,128]{1,0:T(8,128)S(1)}, u32[]{:S(2)}, u32[]{:S(2)}) collective-permute-start(f32[336,128]{1,0:T(8,128)S(1)} %collective-permute-done.18.refs_9_), channel_id=1, source_target_pairs={{0,1},{1,0},{2,3},{3,2},{4,5},{5,4},{6,7},{7,6},{8,9},{9,8},{10,11... | collective-permute-start | bytes 516104 | tf_op jit(solution)/shard_map/cond/branch_1_fun/ppermute | solution.py:475
  33.0 5.3 %branch_1_fun.3 = (f32[640,1024]{1,0:T(8,128)S(1)}, f32[512,512]{1,0:T(8,128)S(1)}, f32[512,256]{1,0:T(8,128)S(1)}, f32[80,512]{1,0:T(8,128)S(1)}) custom-call(f32[80,1152]{1,0:T(8,128)S(1)} %copy-done.12, s32[8,128]{1,0:T(8,128)S(1)} %get-tuple-element.71.refs_1_.code1, s32[8,128]{1,0:T(8,128)S(1)} %get-tuple-element.72.refs_2_.code2, ...), custom_call_target="tpu_custom_call" | custom-call | flops 2430074880 | bytes 3932160 | tf_op jit(solution)/shard_map/cond/branch_1_fun/pallas_call | solution.py:481
  38.3 1.9 %collective-permute-start.19 = (f32[176,128]{1,0:T(8,128)S(1)}, f32[176,128]{1,0:T(8,128)S(1)}, u32[]{:S(2)}, u32[]{:S(2)}) collective-permute-start(f32[176,128]{1,0:T(8,128)S(1)} %slice.48), channel_id=1, source_target_pairs={{0,4},{4,8},{8,12},{12,14},{14,10},{10,6},{6,2},{2,0},{1,5},{5,9},... | collective-permute-start | bytes 270344 | tf_op jit(solution)/shard_map/cond/branch_1_fun/ppermute | solution.py:500
  40.2 2.8 %branch_1_fun.4 = (f32[384,1024]{1,0:T(8,128)S(1)}, f32[512,512]{1,0:T(8,128)S(1)}, f32[512,256]{1,0:T(8,128)S(1)}, f32[80,512]{1,0:T(8,128)S(1)}) custom-call(f32[80,1152]{1,0:T(8,128)S(1)} %copy-done.12, s32[8,128]{1,0:T(8,128)S(1)} %get-tuple-element.71.refs_1_.code1, s32[8,128]{1,0:T(8,128)S(1)} %get-tuple-element.72.refs_2_.code2, ...), custom_call_target="tpu_custom_call" | custom-call | flops 1289748480 | bytes 2621440 | tf_op jit(solution)/shard_map/cond/branch_1_fun/pallas_call | solution.py:481
  43.1 0.2 collective-permute-done.19.up
  43.3 0.4 collective-permute-start.24
  43.7 0.0 copy-start.2
  43.7 0.0 copy-start.11
  43.7 0.0 copy-start.14
  43.7 2.5 %branch_1_fun.5 = (f32[128,1024]{1,0:T(8,128)S(1)}, f32[512,512]{1,0:T(8,128)S(1)}, f32[512,256]{1,0:T(8,128)S(1)}, f32[80,512]{1,0:T(8,128)S(1)}) custom-call(f32[80,1152]{1,0:T(8,128)S(1)} %copy-done.12, s32[8,128]{1,0:T(8,128)S(1)} %get-tuple-element.71.refs_1_.code1, s32[8,128]{1,0:T(8,128)S(1)} %get-tuple-element.72.refs_2_.code2, ...), custom_call_target="tpu_custom_call" | custom-call | flops 1038090240 | bytes 2621440 | tf_op jit(solution)/shard_map/cond/branch_1_fun/pallas_call | solution.py:481
  46.2 3.5 %last.3 = (f32[128,256]{1,0:T(8,128)}, f32[512,256]{1,0:T(8,128)}, f32[128,256]{1,0:T(8,128)}, f32[512,256]{1,0:T(8,128)}, f32[512,256]{1,0:T(8,128)}) custom-call(f32[176,128]{1,0:T(8,128)S(1)} %collective-permute-done.19.up, f32[120,128]{1,0:T(8,128)S(1)} %collective-permute-done.23.down, f32[176,128]{1,0:T(8,128)S(1)} %collective-permute-done.24.up_far, ...), custom_call_target="tpu_custom_call" | custom-call | flops 629145600 | bytes 5242880 | tf_op jit(solution)/shard_map/cond/branch_1_fun/last/pallas_call | solution.py:503
  (26 shorter events, 0.1 us)
Async XLA Ops:
  0.6 3.5 %collective-permute-start.32 = (f32[8,64,128]{2,1,0:T(8,128)}, f32[8,64,128]{2,1,0:T(8,128)S(1)}, u32[]{:S(2)}, u32[]{:S(2)}) collective-permute-start(f32[8,64,128]{2,1,0:T(8,128)} %mine_h.1), channel_id=1, source_target_pairs={{0,1},{1,0},{2,3},{3,2},{4,5},{5,4},{6,7},{7,6},{8,9},{9,8},{10,11... | collective-permute-start | bytes 786440 | tf_op jit(solution)/shard_map/ppermute | solution.py:522
  7.9 25.1 %copy-start.12 = (f32[80,1152]{1,0:T(8,128)S(1)}, f32[80,1152]{1,0:T(8,128)}, u32[]{:S(2)}) copy-start(f32[80,1152]{1,0:T(8,128)} %get-tuple-element.70.refs_0_.own) | copy-start | bytes 1105924 | tf_op jit(solution)/shard_map/cond
  8.0 9.1 %collective-permute-start.16 = (f32[456,128]{1,0:T(8,128)}, f32[456,128]{1,0:T(8,128)S(1)}, u32[]{:S(2)}, u32[]{:S(2)}) collective-permute-start(f32[456,128]{1,0:T(8,128)} %get-tuple-element.68), channel_id=1, source_target_pairs={{0,4},{4,8},{8,12},{12,14},{14,10},{10,6},{6,2},{2,0},{1,5},{5,9},... | collective-permute-start | bytes 700424 | tf_op jit(solution)/shard_map/cond/branch_1_fun/ppermute | solution.py:473
  10.6 8.4 %collective-permute-start.20 = (f32[416,128]{1,0:T(8,128)}, f32[416,128]{1,0:T(8,128)S(1)}, u32[]{:S(2)}, u32[]{:S(2)}) collective-permute-start(f32[416,128]{1,0:T(8,128)} %get-tuple-element.69), channel_id=1, source_target_pairs={{4,0},{8,4},{12,8},{14,12},{10,14},{6,10},{2,6},{0,2},{5,1},{9,5},... | collective-permute-start | bytes 638984 | tf_op jit(solution)/shard_map/cond/branch_1_fun/ppermute | solution.py:474
  17.1 8.6 %collective-permute-start.17 = (f32[416,128]{1,0:T(8,128)S(1)}, f32[416,128]{1,0:T(8,128)S(1)}, u32[]{:S(2)}, u32[]{:S(2)}) collective-permute-start(f32[416,128]{1,0:T(8,128)S(1)} %slice.46), channel_id=1, source_target_pairs={{0,4},{4,8},{8,12},{12,14},{14,10},{10,6},{6,2},{2,0},{1,5},{5,9},... | collective-permute-start | bytes 638984 | tf_op jit(solution)/shard_map/cond/branch_1_fun/ppermute | solution.py:473
  19.0 6.1 %collective-permute-start.21 = (f32[376,128]{1,0:T(8,128)S(1)}, f32[376,128]{1,0:T(8,128)S(1)}, u32[]{:S(2)}, u32[]{:S(2)}) collective-permute-start(f32[376,128]{1,0:T(8,128)S(1)} %slice.49), channel_id=1, source_target_pairs={{4,0},{8,4},{12,8},{14,12},{10,14},{6,10},{2,6},{0,2},{5,1},{9,5},... | collective-permute-start | bytes 577544 | tf_op jit(solution)/shard_map/cond/branch_1_fun/ppermute | solution.py:474
  19.2 13.3 %collective-permute-start.26 = (f32[456,128]{1,0:T(8,128)S(1)}, f32[456,128]{1,0:T(8,128)S(1)}, u32[]{:S(2)}, u32[]{:S(2)}) collective-permute-start(f32[456,128]{1,0:T(8,128)S(1)} %collective-permute-done.16.refs_6_), channel_id=1, source_target_pairs={{0,1},{1,0},{2,3},{3,2},{4,5},{5,4},{6,7},{7,6},{8,9},{9,8},{10,11... | collective-permute-start | bytes 700424 | tf_op jit(solution)/shard_map/cond/branch_1_fun/ppermute | solution.py:475
  19.2 12.7 %collective-permute-start.27 = (f32[416,128]{1,0:T(8,128)S(1)}, f32[416,128]{1,0:T(8,128)S(1)}, u32[]{:S(2)}, u32[]{:S(2)}) collective-permute-start(f32[416,128]{1,0:T(8,128)S(1)} %collective-permute-done.20.refs_8_), channel_id=1, source_target_pairs={{0,1},{1,0},{2,3},{3,2},{4,5},{5,4},{6,7},{7,6},{8,9},{9,8},{10,11... | collective-permute-start | bytes 638984 | tf_op jit(solution)/shard_map/cond/branch_1_fun/ppermute | solution.py:475
  25.1 6.3 %collective-permute-start.22 = (f32[336,128]{1,0:T(8,128)S(1)}, f32[336,128]{1,0:T(8,128)S(1)}, u32[]{:S(2)}, u32[]{:S(2)}) collective-permute-start(f32[336,128]{1,0:T(8,128)S(1)} %slice.50), channel_id=1, source_target_pairs={{4,0},{8,4},{12,8},{14,12},{10,14},{6,10},{2,6},{0,2},{5,1},{9,5},... | collective-permute-start | bytes 516104 | tf_op jit(solution)/shard_map/cond/branch_1_fun/ppermute | solution.py:474
  25.7 6.8 %collective-permute-start.18 = (f32[336,128]{1,0:T(8,128)S(1)}, f32[336,128]{1,0:T(8,128)S(1)}, u32[]{:S(2)}, u32[]{:S(2)}) collective-permute-start(f32[336,128]{1,0:T(8,128)S(1)} %slice.47), channel_id=1, source_target_pairs={{0,4},{4,8},{8,12},{12,14},{14,10},{10,6},{6,2},{2,0},{1,5},{5,9},... | collective-permute-start | bytes 516104 | tf_op jit(solution)/shard_map/cond/branch_1_fun/ppermute | solution.py:473
  31.4 6.9 %collective-permute-start.29 = (f32[376,128]{1,0:T(8,128)S(1)}, f32[376,128]{1,0:T(8,128)S(1)}, u32[]{:S(2)}, u32[]{:S(2)}) collective-permute-start(f32[376,128]{1,0:T(8,128)S(1)} %collective-permute-done.21.refs_11_), channel_id=1, source_target_pairs={{0,1},{1,0},{2,3},{3,2},{4,5},{5,4},{6,7},{7,6},{8,9},{9,8},{10,11... | collective-permute-start | bytes 577544 | tf_op jit(solution)/shard_map/cond/branch_1_fun/ppermute | solution.py:475
  31.4 8.8 %collective-permute-start.28 = (f32[416,128]{1,0:T(8,128)S(1)}, f32[416,128]{1,0:T(8,128)S(1)}, u32[]{:S(2)}, u32[]{:S(2)}) collective-permute-start(f32[416,128]{1,0:T(8,128)S(1)} %collective-permute-done.17.refs_9_), channel_id=1, source_target_pairs={{0,1},{1,0},{2,3},{3,2},{4,5},{5,4},{6,7},{7,6},{8,9},{9,8},{10,11... | collective-permute-start | bytes 638984 | tf_op jit(solution)/shard_map/cond/branch_1_fun/ppermute | solution.py:475
  32.0 8.3 %collective-permute-start.23 = (f32[120,128]{1,0:T(8,128)S(1)}, f32[120,128]{1,0:T(8,128)S(1)}, u32[]{:S(2)}, u32[]{:S(2)}) collective-permute-start(f32[120,128]{1,0:T(8,128)S(1)} %slice.51), channel_id=1, source_target_pairs={{4,0},{8,4},{12,8},{14,12},{10,14},{6,10},{2,6},{0,2},{5,1},{9,5},... | collective-permute-start | bytes 184328 | tf_op jit(solution)/shard_map/cond/branch_1_fun/ppermute | solution.py:501
  32.5 11.2 %collective-permute-start.31 = (f32[336,128]{1,0:T(8,128)S(1)}, f32[336,128]{1,0:T(8,128)S(1)}, u32[]{:S(2)}, u32[]{:S(2)}) collective-permute-start(f32[336,128]{1,0:T(8,128)S(1)} %collective-permute-done.22.refs_11_), channel_id=1, source_target_pairs={{0,1},{1,0},{2,3},{3,2},{4,5},{5,4},{6,7},{7,6},{8,9},{9,8},{10,11... | collective-permute-start | bytes 516104 | tf_op jit(solution)/shard_map/cond/branch_1_fun/ppermute | solution.py:475
  32.5 11.2 %collective-permute-start.30 = (f32[336,128]{1,0:T(8,128)S(1)}, f32[336,128]{1,0:T(8,128)S(1)}, u32[]{:S(2)}, u32[]{:S(2)}) collective-permute-start(f32[336,128]{1,0:T(8,128)S(1)} %collective-permute-done.18.refs_9_), channel_id=1, source_target_pairs={{0,1},{1,0},{2,3},{3,2},{4,5},{5,4},{6,7},{7,6},{8,9},{9,8},{10,11... | collective-permute-start | bytes 516104 | tf_op jit(solution)/shard_map/cond/branch_1_fun/ppermute | solution.py:475
  38.3 4.9 %collective-permute-start.19 = (f32[176,128]{1,0:T(8,128)S(1)}, f32[176,128]{1,0:T(8,128)S(1)}, u32[]{:S(2)}, u32[]{:S(2)}) collective-permute-start(f32[176,128]{1,0:T(8,128)S(1)} %slice.48), channel_id=1, source_target_pairs={{0,4},{4,8},{8,12},{12,14},{14,10},{10,6},{6,2},{2,0},{1,5},{5,9},... | collective-permute-start | bytes 270344 | tf_op jit(solution)/shard_map/cond/branch_1_fun/ppermute | solution.py:500
  40.2 6.0 %collective-permute-start.25 = (f32[120,128]{1,0:T(8,128)S(1)}, f32[120,128]{1,0:T(8,128)S(1)}, u32[]{:S(2)}, u32[]{:S(2)}) collective-permute-start(f32[120,128]{1,0:T(8,128)S(1)} %collective-permute-done.23.down), channel_id=1, source_target_pairs={{0,1},{1,0},{2,3},{3,2},{4,5},{5,4},{6,7},{7,6},{8,9},{9,8},{10,11... | collective-permute-start | bytes 184328 | tf_op jit(solution)/shard_map/cond/branch_1_fun/ppermute | solution.py:502
  43.3 2.9 %collective-permute-start.24 = (f32[176,128]{1,0:T(8,128)S(1)}, f32[176,128]{1,0:T(8,128)S(1)}, u32[]{:S(2)}, u32[]{:S(2)}) collective-permute-start(f32[176,128]{1,0:T(8,128)S(1)} %collective-permute-done.19.up), channel_id=1, source_target_pairs={{0,1},{1,0},{2,3},{3,2},{4,5},{5,4},{6,7},{7,6},{8,9},{9,8},{10,11... | collective-permute-start | bytes 270344 | tf_op jit(solution)/shard_map/cond/branch_1_fun/ppermute | solution.py:502
  43.7 2.5 %copy-start.1 = (f32[512,256]{1,0:T(8,128)S(1)}, f32[512,256]{1,0:T(8,128)}, u32[]{:S(2)}) copy-start(f32[512,256]{1,0:T(8,128)} %get-tuple-element.91.cross0) | copy-start | bytes 1572868 | tf_op jit(solution)/shard_map/cond
  43.7 2.6 %copy-start.2 = (f32[512,256]{1,0:T(8,128)S(1)}, f32[512,256]{1,0:T(8,128)}, u32[]{:S(2)}) copy-start(f32[512,256]{1,0:T(8,128)} %get-tuple-element.92.diag0) | copy-start | bytes 1572868 | tf_op jit(solution)/shard_map/cond
  43.7 2.5 %copy-start.11 = (f32[512,512]{1,0:T(8,128)S(1)}, f32[512,512]{1,0:T(8,128)}, u32[]{:S(2)}) copy-start(f32[512,512]{1,0:T(8,128)} %get-tuple-element.73.corner.corner1) | copy-start | bytes 3145732 | tf_op jit(solution)/shard_map/cond
  43.7 2.5 %copy-start.14 = (f32[512,256]{1,0:T(8,128)S(1)}, f32[512,256]{1,0:T(8,128)}, u32[]{:S(2)}) copy-start(f32[512,256]{1,0:T(8,128)} %get-tuple-element.90.corner2) | copy-start | bytes 1572868 | tf_op jit(solution)/shard_map/cond

commit v6 on v5

--- a/solution.py
+++ b/solution.py
@@ -143,7 +143,7 @@
         mask = marks(ancestors[...], n, block)
         code[...] = slot_codes(mask)
         excess = jnp.maximum(excess, jnp.max(jnp.sum(mask, axis=1, keepdims=True), axis=0, keepdims=True) - cap)
-    over[...] = jnp.broadcast_to(excess, over.shape)
+    over[0, 0] = excess[0, 0].astype(jnp.int32)
     for load, source, code, cap, out in zip(loads[2:], (first, second), (code1, code2), caps, (first_c, second_c)):
         pick = picker(code[pl.ds(row, 1), :], cap)
         load.wait()
@@ -183,11 +183,13 @@
     images[...] = dot2(pick, split(cols[...]), NT)
     arrivals = arrivals_of(n)
     place = place_of(row, n)
+    values = []
     for d in range(n):
         g = row_of(lax.rem(place + d, n), n)
         spread = spreads[rows_at(g * cap, cap, 16), :]
         image = images[:, pl.ds(pl.multiple_of(g * block, block), block)]
-        value = dot2(spread, split(image), NT, flip=True)
+        values.append(dot2(spread, split(image), NT, flip=True))
+    for d, value in enumerate(values):
         x = arrivals.index(d if d <= n // 2 else d - n)
         own[:, width + x * cap : width + (x + 1) * cap] = value
         for way, slot in ((0, (n - d) % n), (1, d)):
@@ -387,18 +389,18 @@
 
 def call_factors(caps, n, anc1, anc2, first_factor, second_factor):
     block, width = first_factor.shape
-    codes = jax.ShapeDtypeStruct((n, block), jnp.int32)
+    codes = pltpu.VMEM((n, block), jnp.int32)
     return pl.pallas_call(
         functools.partial(factors_kernel, caps, n),
         out_shape=(
-            jax.ShapeDtypeStruct((caps[0], width), F32),
-            jax.ShapeDtypeStruct((caps[1], width), F32),
+            pltpu.VMEM((caps[0], width), F32),
+            pltpu.VMEM((caps[1], width), F32),
             codes,
             codes,
-            jax.ShapeDtypeStruct((1, LANES), F32),
+            pltpu.SMEM((1, 1), jnp.int32),
         ),
         in_specs=[ANY] * 4,
-        out_specs=(VMEM,) * 5,
+        out_specs=(VMEM,) * 4 + (SMEM,),
         scratch_shapes=[pltpu.VMEM(v.shape, v.dtype) for v in (anc1, anc2, first_factor, second_factor)] + [pltpu.SemaphoreType.DMA((4,))],
         cost_estimate=pl.CostEstimate(flops=8 * sum(caps) * block * width, bytes_accessed=8 * width * block, transcendentals=0),
         name="factors",
@@ -425,7 +427,7 @@
         ],
         cost_estimate=pl.CostEstimate(flops=8 * cap * block * n * block, bytes_accessed=8 * n * block * block, transcendentals=0),
         name="payload",
-    )(code, first_c, second_c, mine, theirs)
+    )(code, pltpu.with_memory_space_constraint(first_c, pltpu.VMEM), second_c, mine, theirs)
 
 
 def flat_rows(caps, width, count):
@@ -495,7 +497,7 @@
             cost_estimate=pl.CostEstimate(flops=6 * size * width * (2 * size + 2 * later + 6 * half_width), bytes_accessed=4 * size * width * 8, transcendentals=0),
         )(*ins)
     rows = flat_rows(caps, width, 1)
-    cut = 3 * rows // 40 * 8
+    cut = 7 * rows // 80 * 8
     k = n // 2
     up = lax.ppermute(up[:cut], "row", ups)
     down = lax.ppermute(down[cut:rows], "row", downs)

time: 50.5 us -> 48.6 us (0.962)
  Pallas kernels: 24.1 us -> 21.6 us
  local copies, waits for them, and re-layouts: 0.09 us -> 1.43 us
  waiting for transfers between devices: 12.1 us -> 12.8 us
  starting transfers between devices: 11.7 us -> 11 us
  between operations: 1.52 us -> 0.88 us
    ppermute x4, starting transfers between devices: 1.38 us -> 0.09 us  [gather_branch(): lax.ppermute(up, 'col', swap)]
    ppermute x1, starting transfers between devices: 1.86 us -> 0.88 us  [gather_branch(): up = lax.ppermute(up[:cut], 'row', ups)]
    pallas_call x1, Pallas kernels: 3.53 us -> 2.59 us  [call_payload(): pl.pallas_call(functools.partial(payload_kernel, caps, n, counts), out_sh...]
    ppermute x1, starting transfers between devices: 0.53 us -> 1.46 us  [gather_branch(): down = lax.ppermute(down[cut:rows], 'row', downs)]
    pallas_call x3, Pallas kernels: 10.6 us -> 9.69 us  [gather_branch(): pl.pallas_call(functools.partial(update_kernel, caps, n, k), out_shape=tu...]
    ppermute x3, waiting for transfers between devices: 6.47 us -> 7.32 us  [gather_branch(): up = lax.ppermute(up[:flat_rows(caps, width, n + 1 - 2 * k)], 'row', ups)]
    slice x2, local copies, waits for them, and re-layouts: 0.03 us -> 0.7 us  [gather_branch(): up = lax.ppermute(up[:flat_rows(caps, width, n + 1 - 2 * k)], 'row', ups)]
    slice x2, local copies, waits for them, and re-layouts: 0.03 us -> 0.68 us  [gather_branch(): down = lax.ppermute(down[:flat_rows(caps, width, n - 2 * k)], 'row', downs)]
  transfers between devices with their start and end apart: 17 -> 17, of which waited for: 3 -> 4; matrix products, arithmetic and copies ran while one was open for 0% -> 3% of each run, Pallas kernels for 34% -> 32%
where the time goes in v6:
time: 48.6 us; the launch traced here: 48.4 us
  Pallas kernels  21.6 us (44%)
  waiting for transfers between devices  12.8 us (26%)
  starting transfers between devices  11 us (23%)
  local copies, waits for them, and re-layouts  1.43 us (3%)
  between operations  0.88 us (2%)
  loops' own time  0.75 us (2%)
    pallas_call x3, Pallas kernels, gather_branch(): pl.pallas_call(functools.partial(update_kernel, caps, n, k), out_shape=tu...  9.69 us
    ppermute x3, waiting for transfers between devices, gather_branch(): up = lax.ppermute(up[:flat_rows(caps, width, n + 1 - 2 * k)], 'row', ups)  7.32 us
    ppermute x3, starting transfers between devices, gather_branch(): up = lax.ppermute(up[:flat_rows(caps, width, n + 1 - 2 * k)], 'row', ups)  6.08 us
    ppermute x3, waiting for transfers between devices, gather_branch(): down = lax.ppermute(down[:flat_rows(caps, width, n - 2 * k)], 'row', downs)  5.43 us
    pallas_call x1, Pallas kernels, gather_branch(): pl.pallas_call(side_kernel, out_shape=(square, square, part, part), in_sp...  4.19 us
    pallas_call x1, Pallas kernels, gather_branch(): pl.pallas_call(functools.partial(last_kernel, caps, n), out_shape=(tall,...  3.47 us
    pallas_call x1, Pallas kernels, call_payload(): pl.pallas_call(functools.partial(payload_kernel, caps, n, counts), out_sh...  2.59 us
    pallas_call x1, Pallas kernels, call_factors(): pl.pallas_call(functools.partial(factors_kernel, caps, n), out_shape=(plt...  1.67 us
  transfers between devices with their start and end apart: 17, of which 4 were waited for; matrix products, arithmetic and copies ran while one was open for 3% of the time, Pallas kernels for 32%

profile of v6, /device:TPU:0, one launch (start us, length us, event | category | flops | bytes accessed | tf_op | source)
XLA Modules:
  0.0 48.4 jit_solution(2951709692972264909)
XLA Ops:
  0.6 0.6 %collective-permute-start.32 = (f32[8,64,128]{2,1,0:T(8,128)}, f32[8,64,128]{2,1,0:T(8,128)S(1)}, u32[]{:S(2)}, u32[]{:S(2)}) collective-permute-start(f32[8,64,128]{2,1,0:T(8,128)} %mine_h.1), channel_id=1, source_target_pairs={{0,1},{1,0},{2,3},{3,2},{4,5},{5,4},{6,7},{7,6},{8,9},{9,8},{10,11... | collective-permute-start | bytes 786440 | tf_op jit(solution)/shard_map/ppermute | solution.py:524
  1.2 1.7 %factors.3 = (f32[80,512]{1,0:T(8,128)S(1)}, f32[48,512]{1,0:T(8,128)S(1)}, s32[8,128]{1,0:T(8,128)S(1)}, s32[8,128]{1,0:T(8,128)S(1)}, s32[1,1]{1,0:T(1,128)S(4)}) custom-call(s32[1,512]{1,0:T(1,128)} %bitcast.3, s32[1,256]{1,0:T(1,128)} %bitcast.5, f32[128,512]{1,0:T(8,128)} %first_h.1, f32[128,512]{1,0:T(8,128)} %second_h.1), custom_call_target="tpu_custom_call" | custom-call | flops 67108864 | bytes 524288 | tf_op jit(solution)/shard_map/factors/pallas_call | solution.py:393
  2.9 2.6 %payload.3 = (f32[80,1152]{1,0:T(8,128)}, f32[456,128]{1,0:T(8,128)}, f32[416,128]{1,0:T(8,128)}) custom-call(s32[8,128]{1,0:T(8,128)S(1)} %get-tuple-element.107.code, f32[80,512]{1,0:T(8,128)S(1)} %get-tuple-element.108.first_c, f32[48,512]{1,0:T(8,128)S(1)} %get-tuple-element.109.second_c, f32[8,64,128]{2,1,0:T(8,128)} %mine_h.1, ...), custom_call_target="tpu_custom_call" | custom-call | flops 83886080 | bytes 1048576 | tf_op jit(solution)/shard_map/payload/pallas_call | solution.py:415
  5.5 42.7 %conditional.1 = ((f32[128,256]{1,0:T(8,128)}, f32[512,256]{1,0:T(8,128)}, f32[128,256]{1,0:T(8,128)}, f32[512,256]{1,0:T(8,128)}, f32[512,256]{1,0:T(8,128)})) conditional(s32[]{:T(128)} %bitcast.2, (s32[1,512]{1,0:T(1,128)}, s32[1,256]{1,0:T(1,128)}, f32[128,512]{1,0:T(8,128)}, f32[128,512]{1,0:T(8,128)}, f32[8,64,128]{2,1,0:T(8,128)}, ...), branch_computations={%region_0.0_spmd, %region_1.0_spmd} | conditional | flops 10334765056 | bytes 68125576 | solution.py:543
  5.7 0.0 copy-start.7
  5.7 2.7 %collective-permute-start.16 = (f32[456,128]{1,0:T(8,128)}, f32[456,128]{1,0:T(8,128)S(1)}, u32[]{:S(2)}, u32[]{:S(2)}) collective-permute-start(f32[456,128]{1,0:T(8,128)} %get-tuple-element.68), channel_id=1, source_target_pairs={{0,4},{4,8},{8,12},{12,14},{14,10},{10,6},{6,2},{2,0},{1,5},{5,9},... | collective-permute-start | bytes 700424 | tf_op jit(solution)/shard_map/cond/branch_1_fun/ppermute | solution.py:475
  8.4 6.4 %collective-permute-done.16.refs_6_ = f32[456,128]{1,0:T(8,128)S(1)} collective-permute-done((f32[456,128]{1,0:T(8,128)}, f32[456,128]{1,0:T(8,128)S(1)}, u32[]{:S(2)}, u32[]{:S(2)}) %collective-permute-start.16) | collective-permute-done | bytes 233504 | tf_op jit(solution)/shard_map/cond/branch_1_fun/ppermute | solution.py:475
  14.9 1.9 %collective-permute-start.17 = (f32[416,128]{1,0:T(8,128)S(1)}, f32[416,128]{1,0:T(8,128)S(1)}, u32[]{:S(2)}, u32[]{:S(2)}) collective-permute-start(f32[416,128]{1,0:T(8,128)S(1)} %slice.42), channel_id=1, source_target_pairs={{0,4},{4,8},{8,12},{12,14},{14,10},{10,6},{6,2},{2,0},{1,5},{5,9},... | collective-permute-start | bytes 638984 | tf_op jit(solution)/shard_map/cond/branch_1_fun/ppermute | solution.py:475
  16.8 0.0 collective-permute-done.20.refs_8_
  16.8 0.2 collective-permute-start.21
  17.0 0.5 %collective-permute-start.27 = (f32[416,128]{1,0:T(8,128)S(1)}, f32[416,128]{1,0:T(8,128)S(1)}, u32[]{:S(2)}, u32[]{:S(2)}) collective-permute-start(f32[416,128]{1,0:T(8,128)S(1)} %collective-permute-done.20.refs_8_), channel_id=1, source_target_pairs={{0,1},{1,0},{2,3},{3,2},{4,5},{5,4},{6,7},{7,6},{8,9},{9,8},{10,11... | collective-permute-start | bytes 638984 | tf_op jit(solution)/shard_map/cond/branch_1_fun/ppermute | solution.py:477
  17.5 5.3 %collective-permute-done.21.refs_11_ = f32[376,128]{1,0:T(8,128)S(1)} collective-permute-done((f32[376,128]{1,0:T(8,128)S(1)}, f32[376,128]{1,0:T(8,128)S(1)}, u32[]{:S(2)}, u32[]{:S(2)}) %collective-permute-start.21) | collective-permute-done | bytes 192544 | tf_op jit(solution)/shard_map/cond/branch_1_fun/ppermute | solution.py:476
  22.9 0.7 %slice.46 = f32[336,128]{1,0:T(8,128)} slice(f32[376,128]{1,0:T(8,128)S(1)} %collective-permute-done.21.refs_11_), slice={[0:336], [0:128]} | slice | bytes 344064 | tf_op jit(solution)/shard_map/cond/branch_1_fun/slice | solution.py:476
  23.5 0.5 collective-permute-start.22
  24.0 0.7 %slice.43 = f32[336,128]{1,0:T(8,128)} slice(f32[416,128]{1,0:T(8,128)S(1)} %collective-permute-done.17.refs_9_), slice={[0:336], [0:128]} | slice | bytes 344064 | tf_op jit(solution)/shard_map/cond/branch_1_fun/slice | solution.py:475
  24.7 1.5 %collective-permute-start.18 = (f32[336,128]{1,0:T(8,128)}, f32[336,128]{1,0:T(8,128)S(1)}, u32[]{:S(2)}, u32[]{:S(2)}) collective-permute-start(f32[336,128]{1,0:T(8,128)} %slice.43), channel_id=1, source_target_pairs={{0,4},{4,8},{8,12},{12,14},{14,10},{10,6},{6,2},{2,0},{1,5},{5,9},... | collective-permute-start | bytes 516104 | tf_op jit(solution)/shard_map/cond/branch_1_fun/ppermute | solution.py:475
  26.3 4.2 %side.3 = (f32[512,256]{1,0:T(8,128)}, f32[512,256]{1,0:T(8,128)}, bf16[512,512]{1,0:T(8,128)(2,1)S(1)}, bf16[512,512]{1,0:T(8,128)(2,1)S(1)}) custom-call(f32[512,512]{1,0:T(8,128)} %get-tuple-element.73.corner.corner1, f32[512,512]{1,0:T(8,128)} %get-tuple-element.74.link), custom_call_target="tpu_custom_call" | custom-call | flops 805306368 | bytes 5242880 | tf_op jit(solution)/shard_map/cond/branch_1_fun/side/pallas_call | solution.py:462
  30.5 0.1 collective-permute-done.22.refs_11_
  30.6 0.9 %collective-permute-done.18.refs_9_ = f32[336,128]{1,0:T(8,128)S(1)} collective-permute-done((f32[336,128]{1,0:T(8,128)}, f32[336,128]{1,0:T(8,128)S(1)}, u32[]{:S(2)}, u32[]{:S(2)}) %collective-permute-start.18) | collective-permute-done | bytes 172064 | tf_op jit(solution)/shard_map/cond/branch_1_fun/ppermute | solution.py:475
  31.4 1.5 %collective-permute-start.23 = (f32[96,128]{1,0:T(8,128)S(1)}, f32[96,128]{1,0:T(8,128)S(1)}, u32[]{:S(2)}, u32[]{:S(2)}) collective-permute-start(f32[96,128]{1,0:T(8,128)S(1)} %slice.47), channel_id=1, source_target_pairs={{4,0},{8,4},{12,8},{14,12},{10,14},{6,10},{2,6},{0,2},{5,1},{9,5},... | collective-permute-start | bytes 147464 | tf_op jit(solution)/shard_map/cond/branch_1_fun/ppermute | solution.py:503
  32.9 0.1 collective-permute-start.31
  33.0 0.9 %collective-permute-start.19 = (f32[200,128]{1,0:T(8,128)S(1)}, f32[200,128]{1,0:T(8,128)S(1)}, u32[]{:S(2)}, u32[]{:S(2)}) collective-permute-start(f32[200,128]{1,0:T(8,128)S(1)} %slice.44), channel_id=1, source_target_pairs={{0,4},{4,8},{8,12},{12,14},{14,10},{10,6},{6,2},{2,0},{1,5},{5,9},... | collective-permute-start | bytes 307208 | tf_op jit(solution)/shard_map/cond/branch_1_fun/ppermute | solution.py:502
  33.9 4.4 %branch_1_fun.3 = (f32[640,1024]{1,0:T(8,128)S(1)}, f32[512,512]{1,0:T(8,128)S(1)}, f32[512,256]{1,0:T(8,128)S(1)}, f32[80,512]{1,0:T(8,128)S(1)}) custom-call(f32[80,1152]{1,0:T(8,128)S(1)} %copy-done.13, s32[8,128]{1,0:T(8,128)S(1)} %get-tuple-element.71.refs_1_.code1, s32[8,128]{1,0:T(8,128)S(1)} %get-tuple-element.72.refs_2_.code2, ...), custom_call_target="tpu_custom_call" | custom-call | flops 2430074880 | bytes 3932160 | tf_op jit(solution)/shard_map/cond/branch_1_fun/pallas_call | solution.py:483
  38.4 0.6 %collective-permute-start.25 = (f32[96,128]{1,0:T(8,128)S(1)}, f32[96,128]{1,0:T(8,128)S(1)}, u32[]{:S(2)}, u32[]{:S(2)}) collective-permute-start(f32[96,128]{1,0:T(8,128)S(1)} %collective-permute-done.23.down), channel_id=1, source_target_pairs={{0,1},{1,0},{2,3},{3,2},{4,5},{5,4},{6,7},{7,6},{8,9},{9,8},{10,11... | collective-permute-start | bytes 147464 | tf_op jit(solution)/shard_map/cond/branch_1_fun/ppermute | solution.py:504
  38.9 0.1 collective-permute-start.24
  39.0 2.8 %branch_1_fun.4 = (f32[384,1024]{1,0:T(8,128)S(1)}, f32[512,512]{1,0:T(8,128)S(1)}, f32[512,256]{1,0:T(8,128)S(1)}, f32[80,512]{1,0:T(8,128)S(1)}) custom-call(f32[80,1152]{1,0:T(8,128)S(1)} %copy-done.13, s32[8,128]{1,0:T(8,128)S(1)} %get-tuple-element.71.refs_1_.code1, s32[8,128]{1,0:T(8,128)S(1)} %get-tuple-element.72.refs_2_.code2, ...), custom_call_target="tpu_custom_call" | custom-call | flops 1289748480 | bytes 2621440 | tf_op jit(solution)/shard_map/cond/branch_1_fun/pallas_call | solution.py:483
  41.9 0.0 copy-start.1
  41.9 0.0 copy-start.2
  41.9 0.0 copy-start.12
  41.9 0.0 copy-start.15
  41.9 2.4 %branch_1_fun.5 = (f32[128,1024]{1,0:T(8,128)S(1)}, f32[512,512]{1,0:T(8,128)S(1)}, f32[512,256]{1,0:T(8,128)S(1)}, f32[80,512]{1,0:T(8,128)S(1)}) custom-call(f32[80,1152]{1,0:T(8,128)S(1)} %copy-done.13, s32[8,128]{1,0:T(8,128)S(1)} %get-tuple-element.71.refs_1_.code1, s32[8,128]{1,0:T(8,128)S(1)} %get-tuple-element.72.refs_2_.code2, ...), custom_call_target="tpu_custom_call" | custom-call | flops 1038090240 | bytes 2621440 | tf_op jit(solution)/shard_map/cond/branch_1_fun/pallas_call | solution.py:483
  44.4 3.5 %last.3 = (f32[128,256]{1,0:T(8,128)}, f32[512,256]{1,0:T(8,128)}, f32[128,256]{1,0:T(8,128)}, f32[512,256]{1,0:T(8,128)}, f32[512,256]{1,0:T(8,128)}) custom-call(f32[200,128]{1,0:T(8,128)S(1)} %collective-permute-done.19.up, f32[96,128]{1,0:T(8,128)S(1)} %collective-permute-done.23.down, f32[200,128]{1,0:T(8,128)S(1)} %collective-permute-done.24.up_far, ...), custom_call_target="tpu_custom_call" | custom-call | flops 629145600 | bytes 5242880 | tf_op jit(solution)/shard_map/cond/branch_1_fun/last/pallas_call | solution.py:505
  (30 shorter events, 0.1 us)
Async XLA Ops:
  0.6 2.2 %collective-permute-start.32 = (f32[8,64,128]{2,1,0:T(8,128)}, f32[8,64,128]{2,1,0:T(8,128)S(1)}, u32[]{:S(2)}, u32[]{:S(2)}) collective-permute-start(f32[8,64,128]{2,1,0:T(8,128)} %mine_h.1), channel_id=1, source_target_pairs={{0,1},{1,0},{2,3},{3,2},{4,5},{5,4},{6,7},{7,6},{8,9},{9,8},{10,11... | collective-permute-start | bytes 786440 | tf_op jit(solution)/shard_map/ppermute | solution.py:524
  5.7 20.5 %copy-start.7 = (f32[48,512]{1,0:T(8,128)}, f32[48,512]{1,0:T(8,128)S(1)}, u32[]{:S(2)}) copy-start(f32[48,512]{1,0:T(8,128)S(1)} %get-tuple-element.77.refs_5_) | copy-start | bytes 294916 | tf_op jit(solution)/shard_map/cond
  5.7 28.1 %copy-start.13 = (f32[80,1152]{1,0:T(8,128)S(1)}, f32[80,1152]{1,0:T(8,128)}, u32[]{:S(2)}) copy-start(f32[80,1152]{1,0:T(8,128)} %get-tuple-element.70.refs_0_.own) | copy-start | bytes 1105924 | tf_op jit(solution)/shard_map/cond
  5.7 9.1 %collective-permute-start.16 = (f32[456,128]{1,0:T(8,128)}, f32[456,128]{1,0:T(8,128)S(1)}, u32[]{:S(2)}, u32[]{:S(2)}) collective-permute-start(f32[456,128]{1,0:T(8,128)} %get-tuple-element.68), channel_id=1, source_target_pairs={{0,4},{4,8},{8,12},{12,14},{14,10},{10,6},{6,2},{2,0},{1,5},{5,9},... | collective-permute-start | bytes 700424 | tf_op jit(solution)/shard_map/cond/branch_1_fun/ppermute | solution.py:475
  8.4 8.3 %collective-permute-start.20 = (f32[416,128]{1,0:T(8,128)}, f32[416,128]{1,0:T(8,128)S(1)}, u32[]{:S(2)}, u32[]{:S(2)}) collective-permute-start(f32[416,128]{1,0:T(8,128)} %get-tuple-element.69), channel_id=1, source_target_pairs={{4,0},{8,4},{12,8},{14,12},{10,14},{6,10},{2,6},{0,2},{5,1},{9,5},... | collective-permute-start | bytes 638984 | tf_op jit(solution)/shard_map/cond/branch_1_fun/ppermute | solution.py:476
  14.9 9.2 %collective-permute-start.17 = (f32[416,128]{1,0:T(8,128)S(1)}, f32[416,128]{1,0:T(8,128)S(1)}, u32[]{:S(2)}, u32[]{:S(2)}) collective-permute-start(f32[416,128]{1,0:T(8,128)S(1)} %slice.42), channel_id=1, source_target_pairs={{0,4},{4,8},{8,12},{12,14},{14,10},{10,6},{6,2},{2,0},{1,5},{5,9},... | collective-permute-start | bytes 638984 | tf_op jit(solution)/shard_map/cond/branch_1_fun/ppermute | solution.py:475
  16.8 6.1 %collective-permute-start.21 = (f32[376,128]{1,0:T(8,128)S(1)}, f32[376,128]{1,0:T(8,128)S(1)}, u32[]{:S(2)}, u32[]{:S(2)}) collective-permute-start(f32[376,128]{1,0:T(8,128)S(1)} %slice.45), channel_id=1, source_target_pairs={{4,0},{8,4},{12,8},{14,12},{10,14},{6,10},{2,6},{0,2},{5,1},{9,5},... | collective-permute-start | bytes 577544 | tf_op jit(solution)/shard_map/cond/branch_1_fun/ppermute | solution.py:476
  17.0 16.0 %collective-permute-start.26 = (f32[456,128]{1,0:T(8,128)S(1)}, f32[456,128]{1,0:T(8,128)S(1)}, u32[]{:S(2)}, u32[]{:S(2)}) collective-permute-start(f32[456,128]{1,0:T(8,128)S(1)} %collective-permute-done.16.refs_6_), channel_id=1, source_target_pairs={{0,1},{1,0},{2,3},{3,2},{4,5},{5,4},{6,7},{7,6},{8,9},{9,8},{10,11... | collective-permute-start | bytes 700424 | tf_op jit(solution)/shard_map/cond/branch_1_fun/ppermute | solution.py:477
  17.0 15.9 %collective-permute-start.27 = (f32[416,128]{1,0:T(8,128)S(1)}, f32[416,128]{1,0:T(8,128)S(1)}, u32[]{:S(2)}, u32[]{:S(2)}) collective-permute-start(f32[416,128]{1,0:T(8,128)S(1)} %collective-permute-done.20.refs_8_), channel_id=1, source_target_pairs={{0,1},{1,0},{2,3},{3,2},{4,5},{5,4},{6,7},{7,6},{8,9},{9,8},{10,11... | collective-permute-start | bytes 638984 | tf_op jit(solution)/shard_map/cond/branch_1_fun/ppermute | solution.py:477
  22.9 11.0 %collective-permute-start.29 = (f32[376,128]{1,0:T(8,128)S(1)}, f32[376,128]{1,0:T(8,128)S(1)}, u32[]{:S(2)}, u32[]{:S(2)}) collective-permute-start(f32[376,128]{1,0:T(8,128)S(1)} %collective-permute-done.21.refs_11_), channel_id=1, source_target_pairs={{0,1},{1,0},{2,3},{3,2},{4,5},{5,4},{6,7},{7,6},{8,9},{9,8},{10,11... | collective-permute-start | bytes 577544 | tf_op jit(solution)/shard_map/cond/branch_1_fun/ppermute | solution.py:477
  23.5 7.0 %collective-permute-start.22 = (f32[336,128]{1,0:T(8,128)}, f32[336,128]{1,0:T(8,128)S(1)}, u32[]{:S(2)}, u32[]{:S(2)}) collective-permute-start(f32[336,128]{1,0:T(8,128)} %slice.46), channel_id=1, source_target_pairs={{4,0},{8,4},{12,8},{14,12},{10,14},{6,10},{2,6},{0,2},{5,1},{9,5},... | collective-permute-start | bytes 516104 | tf_op jit(solution)/shard_map/cond/branch_1_fun/ppermute | solution.py:476
  24.7 6.7 %collective-permute-start.18 = (f32[336,128]{1,0:T(8,128)}, f32[336,128]{1,0:T(8,128)S(1)}, u32[]{:S(2)}, u32[]{:S(2)}) collective-permute-start(f32[336,128]{1,0:T(8,128)} %slice.43), channel_id=1, source_target_pairs={{0,4},{4,8},{8,12},{12,14},{14,10},{10,6},{6,2},{2,0},{1,5},{5,9},... | collective-permute-start | bytes 516104 | tf_op jit(solution)/shard_map/cond/branch_1_fun/ppermute | solution.py:475
  26.3 7.6 %copy-start.8 = (f32[48,512]{1,0:T(8,128)S(1)}, f32[48,512]{1,0:T(8,128)}, u32[]{:S(2)}) copy-start(f32[48,512]{1,0:T(8,128)} %copy-done.7) | copy-start | bytes 294916 | tf_op jit(solution)/shard_map/cond
  30.5 8.5 %collective-permute-start.28 = (f32[416,128]{1,0:T(8,128)S(1)}, f32[416,128]{1,0:T(8,128)S(1)}, u32[]{:S(2)}, u32[]{:S(2)}) collective-permute-start(f32[416,128]{1,0:T(8,128)S(1)} %collective-permute-done.17.refs_9_), channel_id=1, source_target_pairs={{0,1},{1,0},{2,3},{3,2},{4,5},{5,4},{6,7},{7,6},{8,9},{9,8},{10,11... | collective-permute-start | bytes 638984 | tf_op jit(solution)/shard_map/cond/branch_1_fun/ppermute | solution.py:477
  31.4 6.9 %collective-permute-start.23 = (f32[96,128]{1,0:T(8,128)S(1)}, f32[96,128]{1,0:T(8,128)S(1)}, u32[]{:S(2)}, u32[]{:S(2)}) collective-permute-start(f32[96,128]{1,0:T(8,128)S(1)} %slice.47), channel_id=1, source_target_pairs={{4,0},{8,4},{12,8},{14,12},{10,14},{6,10},{2,6},{0,2},{5,1},{9,5},... | collective-permute-start | bytes 147464 | tf_op jit(solution)/shard_map/cond/branch_1_fun/ppermute | solution.py:503
  32.9 8.9 %collective-permute-start.31 = (f32[336,128]{1,0:T(8,128)S(1)}, f32[336,128]{1,0:T(8,128)S(1)}, u32[]{:S(2)}, u32[]{:S(2)}) collective-permute-start(f32[336,128]{1,0:T(8,128)S(1)} %collective-permute-done.22.refs_11_), channel_id=1, source_target_pairs={{0,1},{1,0},{2,3},{3,2},{4,5},{5,4},{6,7},{7,6},{8,9},{9,8},{10,11... | collective-permute-start | bytes 516104 | tf_op jit(solution)/shard_map/cond/branch_1_fun/ppermute | solution.py:477
  33.0 5.9 %collective-permute-start.19 = (f32[200,128]{1,0:T(8,128)S(1)}, f32[200,128]{1,0:T(8,128)S(1)}, u32[]{:S(2)}, u32[]{:S(2)}) collective-permute-start(f32[200,128]{1,0:T(8,128)S(1)} %slice.44), channel_id=1, source_target_pairs={{0,4},{4,8},{8,12},{12,14},{14,10},{10,6},{6,2},{2,0},{1,5},{5,9},... | collective-permute-start | bytes 307208 | tf_op jit(solution)/shard_map/cond/branch_1_fun/ppermute | solution.py:502
  33.9 8.0 %collective-permute-start.30 = (f32[336,128]{1,0:T(8,128)S(1)}, f32[336,128]{1,0:T(8,128)S(1)}, u32[]{:S(2)}, u32[]{:S(2)}) collective-permute-start(f32[336,128]{1,0:T(8,128)S(1)} %collective-permute-done.18.refs_9_), channel_id=1, source_target_pairs={{0,1},{1,0},{2,3},{3,2},{4,5},{5,4},{6,7},{7,6},{8,9},{9,8},{10,11... | collective-permute-start | bytes 516104 | tf_op jit(solution)/shard_map/cond/branch_1_fun/ppermute | solution.py:477
  38.4 6.0 %collective-permute-start.25 = (f32[96,128]{1,0:T(8,128)S(1)}, f32[96,128]{1,0:T(8,128)S(1)}, u32[]{:S(2)}, u32[]{:S(2)}) collective-permute-start(f32[96,128]{1,0:T(8,128)S(1)} %collective-permute-done.23.down), channel_id=1, source_target_pairs={{0,1},{1,0},{2,3},{3,2},{4,5},{5,4},{6,7},{7,6},{8,9},{9,8},{10,11... | collective-permute-start | bytes 147464 | tf_op jit(solution)/shard_map/cond/branch_1_fun/ppermute | solution.py:504
  38.9 5.4 %collective-permute-start.24 = (f32[200,128]{1,0:T(8,128)S(1)}, f32[200,128]{1,0:T(8,128)S(1)}, u32[]{:S(2)}, u32[]{:S(2)}) collective-permute-start(f32[200,128]{1,0:T(8,128)S(1)} %collective-permute-done.19.up), channel_id=1, source_target_pairs={{0,1},{1,0},{2,3},{3,2},{4,5},{5,4},{6,7},{7,6},{8,9},{9,8},{10,11... | collective-permute-start | bytes 307208 | tf_op jit(solution)/shard_map/cond/branch_1_fun/ppermute | solution.py:504
  41.9 2.5 %copy-start.1 = (f32[512,256]{1,0:T(8,128)S(1)}, f32[512,256]{1,0:T(8,128)}, u32[]{:S(2)}) copy-start(f32[512,256]{1,0:T(8,128)} %get-tuple-element.91.cross0) | copy-start | bytes 1572868 | tf_op jit(solution)/shard_map/cond
  41.9 2.5 %copy-start.2 = (f32[512,256]{1,0:T(8,128)S(1)}, f32[512,256]{1,0:T(8,128)}, u32[]{:S(2)}) copy-start(f32[512,256]{1,0:T(8,128)} %get-tuple-element.92.diag0) | copy-start | bytes 1572868 | tf_op jit(solution)/shard_map/cond
  41.9 2.5 %copy-start.12 = (f32[512,512]{1,0:T(8,128)S(1)}, f32[512,512]{1,0:T(8,128)}, u32[]{:S(2)}) copy-start(f32[512,512]{1,0:T(8,128)} %get-tuple-element.73.corner.corner1) | copy-start | bytes 3145732 | tf_op jit(solution)/shard_map/cond
  41.9 2.5 %copy-start.15 = (f32[512,256]{1,0:T(8,128)S(1)}, f32[512,256]{1,0:T(8,128)}, u32[]{:S(2)}) copy-start(f32[512,256]{1,0:T(8,128)} %get-tuple-element.90.corner2) | copy-start | bytes 1572868 | tf_op jit(solution)/shard_map/cond

commit v7 on v6

--- a/solution.py
+++ b/solution.py
@@ -175,7 +175,9 @@
     for g in range(groups):
         cols[rows_at(g * block + (1 - col) * share, share), :] = theirs[g]
         spreads[g * cap : (g + 1) * cap, :] = picker(code[g : g + 1, :], cap)
-    own_ud[...] = jnp.zeros(own_ud.shape, F32)
+    for way in range(2):
+        stop = chunks_of(counts[way] * cap) * LANES
+        own_ud[way, :, stop - LANES : stop] = jnp.zeros((cap, LANES), F32)
     pick = picker(code[pl.ds(row, 1), :], cap)
     loads[0].wait()
     for g in range(groups):
@@ -247,12 +249,14 @@
     size = cap * len(distances)
     first = split(blk[:, :width])
     lh[:size, :width], ll[:size, :width] = first
-    image = dot3(first, (link[0][...], link[1][...]), NN)
+    seconds = []
     for k, distance in enumerate(distances):
         g = source_row(distance, n)
         spread = dot(picker(code1[pl.ds(g, 1), :], cap), picker(code2[pl.ds(g, 1), :], cap2), NT).astype(BF16)
+        seconds.append(dot2(spread, split(sblk[k * cap2 : (k + 1) * cap2, :]), NN))
+    image = dot3(first, (link[0][...], link[1][...]), NN)
+    for k, second in enumerate(seconds):
         rows = slice(k * cap, (k + 1) * cap)
-        second = dot2(spread, split(sblk[k * cap2 : (k + 1) * cap2, :]), NN)
         lh[rows, width:], ll[rows, width:] = split(second - image[rows, :])
 
 
@@ -324,21 +328,24 @@
     values = dot3(split(middle[...]), (sh, sl), NN)
     if not fresh:
         values = values + jnp.concatenate([old_v[:cap, :], old_v[LANES : LANES + cap, :]], axis=0)
-    cross, close = pairs(size, values, lh, ll, rh, rl)
     to_come = dot3((kh[...], kl[...]), (sh, sl), TN)
     part = split(own[:, width + news[0] * cap : width + later * cap])
     f_at, t_at = columns(both, half_width)
     image_f = dot3(part, (lh[:size, f_at], ll[:size, f_at]), NN)
     image_t = dot3(part, (lh[:size, t_at], ll[:size, t_at]), NN)
     if fresh:
-        ab[...], ee[...], v_next[...] = cross, close, to_come
+        v_next[...] = to_come
         image[:, :half_width], image[:, half_width:] = image_f, image_t
+    else:
+        v_next[...] = old_v[2 * LANES :, :] + to_come
+        image[:, :half_width] = old_image[:, :half_width] + image_f
+        image[:, half_width:] = old_image[:, half_width:] + image_t
+    cross, close = pairs(size, values, lh, ll, rh, rl)
+    if fresh:
+        ab[...], ee[...] = cross, close
     else:
         ab[...] = old_ab[...] + cross
         ee[...] = old_ee[...] + close
-        v_next[...] = old_v[2 * LANES :, :] + to_come
-        image[:, :half_width] = old_image[:, :half_width] + image_f
-        image[:, half_width:] = old_image[:, half_width:] + image_t
 
 
 def last_kernel(caps, n, up, down, up_far, down_far, old_v, old_ab, old_ee, image, own, code1, code2, link_h, link_l, corner1, corner2, cross0, diag0, *refs):
@@ -361,28 +368,29 @@
     width = both // 2
     assemble(caps, width, (flat, flat_far), blk, sblk, 0)
     factors_of(caps, n, [n // 2], blk, sblk, code1, code2, (link_h, link_l), lh, ll)
-    values = dot3(split(blk[:, width : width + cap] * 0.5), (lh[:cap, :], ll[:cap, :]), NN) + old_v[:cap, :]
-    cross, close = pairs(cap, values, lh, ll, rh, rl)
-    for load in loads:
-        load.wait()
-    copies = []
-
-    def send(value, ref, out):
-        ref[...] = value
-        copies.append(pltpu.make_async_copy(ref, out, sems.at[len(copies)]))
-        copies[-1].start()
-
-    send(corner1_v[...] + (old_ab[:, :half_width] + cross[:, :half_width]), g1_v, g1)
-    send(old_ab[:, half_width:] + cross[:, half_width:] - cross0_v[...], xx_v, xx)
-    send(corner2_v[...] + (diag0_v[...] + (old_ee[...] + close)), g2_v, g2)
     k = split(own[:, width + (n - 1) * cap :])
     pick = picker(code1[pl.ds(row, 1), :], cap)
     pick2 = (pick.astype(F32) * (code2[pl.ds(row, 1), :] >= 0).astype(F32)).astype(BF16)
     f_at, t_at = columns(both, half_width)
     image_f = image[:, :half_width] + dot3(k, (lh[:cap, f_at], ll[:cap, f_at]), NN)
-    send(-dot2(pick, split(image_f), TN), c1_v, c1)
     image_t = image[:, half_width:] + dot3(k, (lh[:cap, t_at], ll[:cap, t_at]), NN)
-    send(-dot2(pick2, split(image_t), TN), c2_v, c2)
+    values = dot3(split(blk[:, width : width + cap] * 0.5), (lh[:cap, :], ll[:cap, :]), NN) + old_v[:cap, :]
+    column_f, column_t = -dot2(pick, split(image_f), TN), -dot2(pick2, split(image_t), TN)
+    cross, close = pairs(cap, values, lh, ll, rh, rl)
+    copies = []
+
+    def send(value, ref, out):
+        ref[...] = value
+        copies.append(pltpu.make_async_copy(ref, out, sems.at[len(copies)]))
+        copies[-1].start()
+
+    send(column_f, c1_v, c1)
+    send(column_t, c2_v, c2)
+    for load in loads:
+        load.wait()
+    send(corner1_v[...] + (old_ab[:, :half_width] + cross[:, :half_width]), g1_v, g1)
+    send(old_ab[:, half_width:] + cross[:, half_width:] - cross0_v[...], xx_v, xx)
+    send(corner2_v[...] + (diag0_v[...] + (old_ee[...] + close)), g2_v, g2)
     for copy in copies:
         copy.wait()
 

time: 48.6 us -> 47.3 us (0.973)
  Pallas kernels: 21.6 us -> 20.8 us
where the time goes in v7:
time: 47.3 us; the launch traced here: 47.1 us
  Pallas kernels  20.8 us (44%)
  waiting for transfers between devices  12.8 us (27%)
  starting transfers between devices  10.8 us (23%)
  local copies, waits for them, and re-layouts  1.43 us (3%)
  between operations  0.84 us (2%)
    pallas_call x3, Pallas kernels, gather_branch(): pl.pallas_call(functools.partial(update_kernel, caps, n, k), out_shape=tu...  9.34 us
    ppermute x3, waiting for transfers between devices, gather_branch(): up = lax.ppermute(up[:flat_rows(caps, width, n + 1 - 2 * k)], 'row', ups)  7.32 us
    ppermute x3, starting transfers between devices, gather_branch(): up = lax.ppermute(up[:flat_rows(caps, width, n + 1 - 2 * k)], 'row', ups)  6.08 us
    ppermute x3, waiting for transfers between devices, gather_branch(): down = lax.ppermute(down[:flat_rows(caps, width, n - 2 * k)], 'row', downs)  5.43 us
    pallas_call x1, Pallas kernels, gather_branch(): pl.pallas_call(side_kernel, out_shape=(square, square, part, part), in_sp...  4.19 us
    pallas_call x1, Pallas kernels, gather_branch(): pl.pallas_call(functools.partial(last_kernel, caps, n), out_shape=(tall,...  3.01 us
    pallas_call x1, Pallas kernels, call_payload(): pl.pallas_call(functools.partial(payload_kernel, caps, n, counts), out_sh...  2.59 us
    pallas_call x1, Pallas kernels, call_factors(): pl.pallas_call(functools.partial(factors_kernel, caps, n), out_shape=(plt...  1.67 us
  transfers between devices with their start and end apart: 17, of which 4 were waited for; matrix products, arithmetic and copies ran while one was open for 3% of the time, Pallas kernels for 32%

profile of v7, /device:TPU:0, one launch (start us, length us, event | category | flops | bytes accessed | tf_op | source)
XLA Modules:
  0.0 47.1 jit_solution(6276343381217823828)
XLA Ops:
  0.6 0.6 %collective-permute-start.32 = (f32[8,64,128]{2,1,0:T(8,128)}, f32[8,64,128]{2,1,0:T(8,128)S(1)}, u32[]{:S(2)}, u32[]{:S(2)}) collective-permute-start(f32[8,64,128]{2,1,0:T(8,128)} %mine_h.1), channel_id=1, source_target_pairs={{0,1},{1,0},{2,3},{3,2},{4,5},{5,4},{6,7},{7,6},{8,9},{9,8},{10,11... | collective-permute-start | bytes 786440 | tf_op jit(solution)/shard_map/ppermute | solution.py:532
  1.2 1.7 %factors.3 = (f32[80,512]{1,0:T(8,128)S(1)}, f32[48,512]{1,0:T(8,128)S(1)}, s32[8,128]{1,0:T(8,128)S(1)}, s32[8,128]{1,0:T(8,128)S(1)}, s32[1,1]{1,0:T(1,128)S(4)}) custom-call(s32[1,512]{1,0:T(1,128)} %bitcast.3, s32[1,256]{1,0:T(1,128)} %bitcast.5, f32[128,512]{1,0:T(8,128)} %first_h.1, f32[128,512]{1,0:T(8,128)} %second_h.1), custom_call_target="tpu_custom_call" | custom-call | flops 67108864 | bytes 524288 | tf_op jit(solution)/shard_map/factors/pallas_call | solution.py:401
  2.9 2.6 %payload.3 = (f32[80,1152]{1,0:T(8,128)}, f32[456,128]{1,0:T(8,128)}, f32[416,128]{1,0:T(8,128)}) custom-call(s32[8,128]{1,0:T(8,128)S(1)} %get-tuple-element.107.code, f32[80,512]{1,0:T(8,128)S(1)} %get-tuple-element.108.first_c, f32[48,512]{1,0:T(8,128)S(1)} %get-tuple-element.109.second_c, f32[8,64,128]{2,1,0:T(8,128)} %mine_h.1, ...), custom_call_target="tpu_custom_call" | custom-call | flops 83886080 | bytes 1048576 | tf_op jit(solution)/shard_map/payload/pallas_call | solution.py:423
  5.5 41.4 %conditional.1 = ((f32[128,256]{1,0:T(8,128)}, f32[512,256]{1,0:T(8,128)}, f32[128,256]{1,0:T(8,128)}, f32[512,256]{1,0:T(8,128)}, f32[512,256]{1,0:T(8,128)})) conditional(s32[]{:T(128)} %bitcast.2, (s32[1,512]{1,0:T(1,128)}, s32[1,256]{1,0:T(1,128)}, f32[128,512]{1,0:T(8,128)}, f32[128,512]{1,0:T(8,128)}, f32[8,64,128]{2,1,0:T(8,128)}, ...), branch_computations={%region_0.0_spmd, %region_1.0_spmd} | conditional | flops 10334765056 | bytes 68125576 | solution.py:551
  5.7 0.0 copy-start.7
  5.7 2.7 %collective-permute-start.16 = (f32[456,128]{1,0:T(8,128)}, f32[456,128]{1,0:T(8,128)S(1)}, u32[]{:S(2)}, u32[]{:S(2)}) collective-permute-start(f32[456,128]{1,0:T(8,128)} %get-tuple-element.68), channel_id=1, source_target_pairs={{0,4},{4,8},{8,12},{12,14},{14,10},{10,6},{6,2},{2,0},{1,5},{5,9},... | collective-permute-start | bytes 700424 | tf_op jit(solution)/shard_map/cond/branch_1_fun/ppermute | solution.py:483
  8.4 6.4 %collective-permute-done.16.refs_6_ = f32[456,128]{1,0:T(8,128)S(1)} collective-permute-done((f32[456,128]{1,0:T(8,128)}, f32[456,128]{1,0:T(8,128)S(1)}, u32[]{:S(2)}, u32[]{:S(2)}) %collective-permute-start.16) | collective-permute-done | bytes 233504 | tf_op jit(solution)/shard_map/cond/branch_1_fun/ppermute | solution.py:483
  14.9 1.9 %collective-permute-start.17 = (f32[416,128]{1,0:T(8,128)S(1)}, f32[416,128]{1,0:T(8,128)S(1)}, u32[]{:S(2)}, u32[]{:S(2)}) collective-permute-start(f32[416,128]{1,0:T(8,128)S(1)} %slice.42), channel_id=1, source_target_pairs={{0,4},{4,8},{8,12},{12,14},{14,10},{10,6},{6,2},{2,0},{1,5},{5,9},... | collective-permute-start | bytes 638984 | tf_op jit(solution)/shard_map/cond/branch_1_fun/ppermute | solution.py:483
  16.8 0.2 collective-permute-start.21
  17.0 0.5 %collective-permute-start.27 = (f32[416,128]{1,0:T(8,128)S(1)}, f32[416,128]{1,0:T(8,128)S(1)}, u32[]{:S(2)}, u32[]{:S(2)}) collective-permute-start(f32[416,128]{1,0:T(8,128)S(1)} %collective-permute-done.20.refs_8_), channel_id=1, source_target_pairs={{0,1},{1,0},{2,3},{3,2},{4,5},{5,4},{6,7},{7,6},{8,9},{9,8},{10,11... | collective-permute-start | bytes 638984 | tf_op jit(solution)/shard_map/cond/branch_1_fun/ppermute | solution.py:485
  17.5 5.3 %collective-permute-done.21.refs_11_ = f32[376,128]{1,0:T(8,128)S(1)} collective-permute-done((f32[376,128]{1,0:T(8,128)S(1)}, f32[376,128]{1,0:T(8,128)S(1)}, u32[]{:S(2)}, u32[]{:S(2)}) %collective-permute-start.21) | collective-permute-done | bytes 192544 | tf_op jit(solution)/shard_map/cond/branch_1_fun/ppermute | solution.py:484
  22.9 0.7 %slice.46 = f32[336,128]{1,0:T(8,128)} slice(f32[376,128]{1,0:T(8,128)S(1)} %collective-permute-done.21.refs_11_), slice={[0:336], [0:128]} | slice | bytes 344064 | tf_op jit(solution)/shard_map/cond/branch_1_fun/slice | solution.py:484
  23.5 0.5 %collective-permute-start.22 = (f32[336,128]{1,0:T(8,128)}, f32[336,128]{1,0:T(8,128)S(1)}, u32[]{:S(2)}, u32[]{:S(2)}) collective-permute-start(f32[336,128]{1,0:T(8,128)} %slice.46), channel_id=1, source_target_pairs={{4,0},{8,4},{12,8},{14,12},{10,14},{6,10},{2,6},{0,2},{5,1},{9,5},... | collective-permute-start | bytes 516104 | tf_op jit(solution)/shard_map/cond/branch_1_fun/ppermute | solution.py:484
  24.0 0.7 %slice.43 = f32[336,128]{1,0:T(8,128)} slice(f32[416,128]{1,0:T(8,128)S(1)} %collective-permute-done.17.refs_9_), slice={[0:336], [0:128]} | slice | bytes 344064 | tf_op jit(solution)/shard_map/cond/branch_1_fun/slice | solution.py:483
  24.7 1.5 %collective-permute-start.18 = (f32[336,128]{1,0:T(8,128)}, f32[336,128]{1,0:T(8,128)S(1)}, u32[]{:S(2)}, u32[]{:S(2)}) collective-permute-start(f32[336,128]{1,0:T(8,128)} %slice.43), channel_id=1, source_target_pairs={{0,4},{4,8},{8,12},{12,14},{14,10},{10,6},{6,2},{2,0},{1,5},{5,9},... | collective-permute-start | bytes 516104 | tf_op jit(solution)/shard_map/cond/branch_1_fun/ppermute | solution.py:483
  26.3 4.2 %side.3 = (f32[512,256]{1,0:T(8,128)}, f32[512,256]{1,0:T(8,128)}, bf16[512,512]{1,0:T(8,128)(2,1)S(1)}, bf16[512,512]{1,0:T(8,128)(2,1)S(1)}) custom-call(f32[512,512]{1,0:T(8,128)} %get-tuple-element.73.corner.corner1, f32[512,512]{1,0:T(8,128)} %get-tuple-element.74.link), custom_call_target="tpu_custom_call" | custom-call | flops 805306368 | bytes 5242880 | tf_op jit(solution)/shard_map/cond/branch_1_fun/side/pallas_call | solution.py:470
  30.5 0.1 collective-permute-done.22.refs_11_
  30.6 0.9 %collective-permute-done.18.refs_9_ = f32[336,128]{1,0:T(8,128)S(1)} collective-permute-done((f32[336,128]{1,0:T(8,128)}, f32[336,128]{1,0:T(8,128)S(1)}, u32[]{:S(2)}, u32[]{:S(2)}) %collective-permute-start.18) | collective-permute-done | bytes 172064 | tf_op jit(solution)/shard_map/cond/branch_1_fun/ppermute | solution.py:483
  31.4 1.5 %collective-permute-start.23 = (f32[96,128]{1,0:T(8,128)S(1)}, f32[96,128]{1,0:T(8,128)S(1)}, u32[]{:S(2)}, u32[]{:S(2)}) collective-permute-start(f32[96,128]{1,0:T(8,128)S(1)} %slice.47), channel_id=1, source_target_pairs={{4,0},{8,4},{12,8},{14,12},{10,14},{6,10},{2,6},{0,2},{5,1},{9,5},... | collective-permute-start | bytes 147464 | tf_op jit(solution)/shard_map/cond/branch_1_fun/ppermute | solution.py:511
  32.9 0.1 collective-permute-start.31
  33.0 0.6 %collective-permute-start.19 = (f32[200,128]{1,0:T(8,128)S(1)}, f32[200,128]{1,0:T(8,128)S(1)}, u32[]{:S(2)}, u32[]{:S(2)}) collective-permute-start(f32[200,128]{1,0:T(8,128)S(1)} %slice.44), channel_id=1, source_target_pairs={{0,4},{4,8},{8,12},{12,14},{14,10},{10,6},{6,2},{2,0},{1,5},{5,9},... | collective-permute-start | bytes 307208 | tf_op jit(solution)/shard_map/cond/branch_1_fun/ppermute | solution.py:510
  33.6 0.2 collective-permute-start.30
  33.8 4.3 %branch_1_fun.3 = (f32[640,1024]{1,0:T(8,128)S(1)}, f32[512,512]{1,0:T(8,128)S(1)}, f32[512,256]{1,0:T(8,128)S(1)}, f32[80,512]{1,0:T(8,128)S(1)}) custom-call(f32[80,1152]{1,0:T(8,128)S(1)} %copy-done.13, s32[8,128]{1,0:T(8,128)S(1)} %get-tuple-element.71.refs_1_.code1, s32[8,128]{1,0:T(8,128)S(1)} %get-tuple-element.72.refs_2_.code2, ...), custom_call_target="tpu_custom_call" | custom-call | flops 2430074880 | bytes 3932160 | tf_op jit(solution)/shard_map/cond/branch_1_fun/pallas_call | solution.py:491
  38.1 0.5 collective-permute-start.25
  38.5 0.1 collective-permute-start.24
  38.7 2.6 %branch_1_fun.4 = (f32[384,1024]{1,0:T(8,128)S(1)}, f32[512,512]{1,0:T(8,128)S(1)}, f32[512,256]{1,0:T(8,128)S(1)}, f32[80,512]{1,0:T(8,128)S(1)}) custom-call(f32[80,1152]{1,0:T(8,128)S(1)} %copy-done.13, s32[8,128]{1,0:T(8,128)S(1)} %get-tuple-element.71.refs_1_.code1, s32[8,128]{1,0:T(8,128)S(1)} %get-tuple-element.72.refs_2_.code2, ...), custom_call_target="tpu_custom_call" | custom-call | flops 1289748480 | bytes 2621440 | tf_op jit(solution)/shard_map/cond/branch_1_fun/pallas_call | solution.py:491
  41.3 0.0 copy-start.1
  41.3 0.0 copy-start.2
  41.4 0.0 copy-start.12
  41.4 0.0 copy-start.15
  41.4 2.4 %branch_1_fun.5 = (f32[128,1024]{1,0:T(8,128)S(1)}, f32[512,512]{1,0:T(8,128)S(1)}, f32[512,256]{1,0:T(8,128)S(1)}, f32[80,512]{1,0:T(8,128)S(1)}) custom-call(f32[80,1152]{1,0:T(8,128)S(1)} %copy-done.13, s32[8,128]{1,0:T(8,128)S(1)} %get-tuple-element.71.refs_1_.code1, s32[8,128]{1,0:T(8,128)S(1)} %get-tuple-element.72.refs_2_.code2, ...), custom_call_target="tpu_custom_call" | custom-call | flops 1038090240 | bytes 2621440 | tf_op jit(solution)/shard_map/cond/branch_1_fun/pallas_call | solution.py:491
  43.9 3.0 %last.3 = (f32[128,256]{1,0:T(8,128)}, f32[512,256]{1,0:T(8,128)}, f32[128,256]{1,0:T(8,128)}, f32[512,256]{1,0:T(8,128)}, f32[512,256]{1,0:T(8,128)}) custom-call(f32[200,128]{1,0:T(8,128)S(1)} %collective-permute-done.19.up, f32[96,128]{1,0:T(8,128)S(1)} %collective-permute-done.23.down, f32[200,128]{1,0:T(8,128)S(1)} %collective-permute-done.24.up_far, ...), custom_call_target="tpu_custom_call" | custom-call | flops 629145600 | bytes 5242880 | tf_op jit(solution)/shard_map/cond/branch_1_fun/last/pallas_call | solution.py:513
  (30 shorter events, 0.1 us)
Async XLA Ops:
  0.6 2.2 %collective-permute-start.32 = (f32[8,64,128]{2,1,0:T(8,128)}, f32[8,64,128]{2,1,0:T(8,128)S(1)}, u32[]{:S(2)}, u32[]{:S(2)}) collective-permute-start(f32[8,64,128]{2,1,0:T(8,128)} %mine_h.1), channel_id=1, source_target_pairs={{0,1},{1,0},{2,3},{3,2},{4,5},{5,4},{6,7},{7,6},{8,9},{9,8},{10,11... | collective-permute-start | bytes 786440 | tf_op jit(solution)/shard_map/ppermute | solution.py:532
  5.7 20.5 %copy-start.7 = (f32[48,512]{1,0:T(8,128)}, f32[48,512]{1,0:T(8,128)S(1)}, u32[]{:S(2)}) copy-start(f32[48,512]{1,0:T(8,128)S(1)} %get-tuple-element.77.refs_5_) | copy-start | bytes 294916 | tf_op jit(solution)/shard_map/cond
  5.7 28.0 %copy-start.13 = (f32[80,1152]{1,0:T(8,128)S(1)}, f32[80,1152]{1,0:T(8,128)}, u32[]{:S(2)}) copy-start(f32[80,1152]{1,0:T(8,128)} %get-tuple-element.70.refs_0_.own) | copy-start | bytes 1105924 | tf_op jit(solution)/shard_map/cond
  5.7 9.1 %collective-permute-start.16 = (f32[456,128]{1,0:T(8,128)}, f32[456,128]{1,0:T(8,128)S(1)}, u32[]{:S(2)}, u32[]{:S(2)}) collective-permute-start(f32[456,128]{1,0:T(8,128)} %get-tuple-element.68), channel_id=1, source_target_pairs={{0,4},{4,8},{8,12},{12,14},{14,10},{10,6},{6,2},{2,0},{1,5},{5,9},... | collective-permute-start | bytes 700424 | tf_op jit(solution)/shard_map/cond/branch_1_fun/ppermute | solution.py:483
  8.4 8.3 %collective-permute-start.20 = (f32[416,128]{1,0:T(8,128)}, f32[416,128]{1,0:T(8,128)S(1)}, u32[]{:S(2)}, u32[]{:S(2)}) collective-permute-start(f32[416,128]{1,0:T(8,128)} %get-tuple-element.69), channel_id=1, source_target_pairs={{4,0},{8,4},{12,8},{14,12},{10,14},{6,10},{2,6},{0,2},{5,1},{9,5},... | collective-permute-start | bytes 638984 | tf_op jit(solution)/shard_map/cond/branch_1_fun/ppermute | solution.py:484
  14.9 9.2 %collective-permute-start.17 = (f32[416,128]{1,0:T(8,128)S(1)}, f32[416,128]{1,0:T(8,128)S(1)}, u32[]{:S(2)}, u32[]{:S(2)}) collective-permute-start(f32[416,128]{1,0:T(8,128)S(1)} %slice.42), channel_id=1, source_target_pairs={{0,4},{4,8},{8,12},{12,14},{14,10},{10,6},{6,2},{2,0},{1,5},{5,9},... | collective-permute-start | bytes 638984 | tf_op jit(solution)/shard_map/cond/branch_1_fun/ppermute | solution.py:483
  16.8 6.1 %collective-permute-start.21 = (f32[376,128]{1,0:T(8,128)S(1)}, f32[376,128]{1,0:T(8,128)S(1)}, u32[]{:S(2)}, u32[]{:S(2)}) collective-permute-start(f32[376,128]{1,0:T(8,128)S(1)} %slice.45), channel_id=1, source_target_pairs={{4,0},{8,4},{12,8},{14,12},{10,14},{6,10},{2,6},{0,2},{5,1},{9,5},... | collective-permute-start | bytes 577544 | tf_op jit(solution)/shard_map/cond/branch_1_fun/ppermute | solution.py:484
  17.0 16.0 %collective-permute-start.26 = (f32[456,128]{1,0:T(8,128)S(1)}, f32[456,128]{1,0:T(8,128)S(1)}, u32[]{:S(2)}, u32[]{:S(2)}) collective-permute-start(f32[456,128]{1,0:T(8,128)S(1)} %collective-permute-done.16.refs_6_), channel_id=1, source_target_pairs={{0,1},{1,0},{2,3},{3,2},{4,5},{5,4},{6,7},{7,6},{8,9},{9,8},{10,11... | collective-permute-start | bytes 700424 | tf_op jit(solution)/shard_map/cond/branch_1_fun/ppermute | solution.py:485
  17.0 15.9 %collective-permute-start.27 = (f32[416,128]{1,0:T(8,128)S(1)}, f32[416,128]{1,0:T(8,128)S(1)}, u32[]{:S(2)}, u32[]{:S(2)}) collective-permute-start(f32[416,128]{1,0:T(8,128)S(1)} %collective-permute-done.20.refs_8_), channel_id=1, source_target_pairs={{0,1},{1,0},{2,3},{3,2},{4,5},{5,4},{6,7},{7,6},{8,9},{9,8},{10,11... | collective-permute-start | bytes 638984 | tf_op jit(solution)/shard_map/cond/branch_1_fun/ppermute | solution.py:485
  22.9 10.7 %collective-permute-start.29 = (f32[376,128]{1,0:T(8,128)S(1)}, f32[376,128]{1,0:T(8,128)S(1)}, u32[]{:S(2)}, u32[]{:S(2)}) collective-permute-start(f32[376,128]{1,0:T(8,128)S(1)} %collective-permute-done.21.refs_11_), channel_id=1, source_target_pairs={{0,1},{1,0},{2,3},{3,2},{4,5},{5,4},{6,7},{7,6},{8,9},{9,8},{10,11... | collective-permute-start | bytes 577544 | tf_op jit(solution)/shard_map/cond/branch_1_fun/ppermute | solution.py:485
  23.5 7.0 %collective-permute-start.22 = (f32[336,128]{1,0:T(8,128)}, f32[336,128]{1,0:T(8,128)S(1)}, u32[]{:S(2)}, u32[]{:S(2)}) collective-permute-start(f32[336,128]{1,0:T(8,128)} %slice.46), channel_id=1, source_target_pairs={{4,0},{8,4},{12,8},{14,12},{10,14},{6,10},{2,6},{0,2},{5,1},{9,5},... | collective-permute-start | bytes 516104 | tf_op jit(solution)/shard_map/cond/branch_1_fun/ppermute | solution.py:484
  24.7 6.7 %collective-permute-start.18 = (f32[336,128]{1,0:T(8,128)}, f32[336,128]{1,0:T(8,128)S(1)}, u32[]{:S(2)}, u32[]{:S(2)}) collective-permute-start(f32[336,128]{1,0:T(8,128)} %slice.43), channel_id=1, source_target_pairs={{0,4},{4,8},{8,12},{12,14},{14,10},{10,6},{6,2},{2,0},{1,5},{5,9},... | collective-permute-start | bytes 516104 | tf_op jit(solution)/shard_map/cond/branch_1_fun/ppermute | solution.py:483
  26.3 7.5 %copy-start.8 = (f32[48,512]{1,0:T(8,128)S(1)}, f32[48,512]{1,0:T(8,128)}, u32[]{:S(2)}) copy-start(f32[48,512]{1,0:T(8,128)} %copy-done.7) | copy-start | bytes 294916 | tf_op jit(solution)/shard_map/cond
  30.5 8.1 %collective-permute-start.28 = (f32[416,128]{1,0:T(8,128)S(1)}, f32[416,128]{1,0:T(8,128)S(1)}, u32[]{:S(2)}, u32[]{:S(2)}) collective-permute-start(f32[416,128]{1,0:T(8,128)S(1)} %collective-permute-done.17.refs_9_), channel_id=1, source_target_pairs={{0,1},{1,0},{2,3},{3,2},{4,5},{5,4},{6,7},{7,6},{8,9},{9,8},{10,11... | collective-permute-start | bytes 638984 | tf_op jit(solution)/shard_map/cond/branch_1_fun/ppermute | solution.py:485
  31.4 6.6 %collective-permute-start.23 = (f32[96,128]{1,0:T(8,128)S(1)}, f32[96,128]{1,0:T(8,128)S(1)}, u32[]{:S(2)}, u32[]{:S(2)}) collective-permute-start(f32[96,128]{1,0:T(8,128)S(1)} %slice.47), channel_id=1, source_target_pairs={{4,0},{8,4},{12,8},{14,12},{10,14},{6,10},{2,6},{0,2},{5,1},{9,5},... | collective-permute-start | bytes 147464 | tf_op jit(solution)/shard_map/cond/branch_1_fun/ppermute | solution.py:511
  32.9 8.4 %collective-permute-start.31 = (f32[336,128]{1,0:T(8,128)S(1)}, f32[336,128]{1,0:T(8,128)S(1)}, u32[]{:S(2)}, u32[]{:S(2)}) collective-permute-start(f32[336,128]{1,0:T(8,128)S(1)} %collective-permute-done.22.refs_11_), channel_id=1, source_target_pairs={{0,1},{1,0},{2,3},{3,2},{4,5},{5,4},{6,7},{7,6},{8,9},{9,8},{10,11... | collective-permute-start | bytes 516104 | tf_op jit(solution)/shard_map/cond/branch_1_fun/ppermute | solution.py:485
  33.0 5.5 %collective-permute-start.19 = (f32[200,128]{1,0:T(8,128)S(1)}, f32[200,128]{1,0:T(8,128)S(1)}, u32[]{:S(2)}, u32[]{:S(2)}) collective-permute-start(f32[200,128]{1,0:T(8,128)S(1)} %slice.44), channel_id=1, source_target_pairs={{0,4},{4,8},{8,12},{12,14},{14,10},{10,6},{6,2},{2,0},{1,5},{5,9},... | collective-permute-start | bytes 307208 | tf_op jit(solution)/shard_map/cond/branch_1_fun/ppermute | solution.py:510
  33.6 7.7 %collective-permute-start.30 = (f32[336,128]{1,0:T(8,128)S(1)}, f32[336,128]{1,0:T(8,128)S(1)}, u32[]{:S(2)}, u32[]{:S(2)}) collective-permute-start(f32[336,128]{1,0:T(8,128)S(1)} %collective-permute-done.18.refs_9_), channel_id=1, source_target_pairs={{0,1},{1,0},{2,3},{3,2},{4,5},{5,4},{6,7},{7,6},{8,9},{9,8},{10,11... | collective-permute-start | bytes 516104 | tf_op jit(solution)/shard_map/cond/branch_1_fun/ppermute | solution.py:485
  38.1 5.7 %collective-permute-start.25 = (f32[96,128]{1,0:T(8,128)S(1)}, f32[96,128]{1,0:T(8,128)S(1)}, u32[]{:S(2)}, u32[]{:S(2)}) collective-permute-start(f32[96,128]{1,0:T(8,128)S(1)} %collective-permute-done.23.down), channel_id=1, source_target_pairs={{0,1},{1,0},{2,3},{3,2},{4,5},{5,4},{6,7},{7,6},{8,9},{9,8},{10,11... | collective-permute-start | bytes 147464 | tf_op jit(solution)/shard_map/cond/branch_1_fun/ppermute | solution.py:512
  38.5 5.3 %collective-permute-start.24 = (f32[200,128]{1,0:T(8,128)S(1)}, f32[200,128]{1,0:T(8,128)S(1)}, u32[]{:S(2)}, u32[]{:S(2)}) collective-permute-start(f32[200,128]{1,0:T(8,128)S(1)} %collective-permute-done.19.up), channel_id=1, source_target_pairs={{0,1},{1,0},{2,3},{3,2},{4,5},{5,4},{6,7},{7,6},{8,9},{9,8},{10,11... | collective-permute-start | bytes 307208 | tf_op jit(solution)/shard_map/cond/branch_1_fun/ppermute | solution.py:512
  41.3 2.5 %copy-start.1 = (f32[512,256]{1,0:T(8,128)S(1)}, f32[512,256]{1,0:T(8,128)}, u32[]{:S(2)}) copy-start(f32[512,256]{1,0:T(8,128)} %get-tuple-element.91.cross0) | copy-start | bytes 1572868 | tf_op jit(solution)/shard_map/cond
  41.3 2.5 %copy-start.2 = (f32[512,256]{1,0:T(8,128)S(1)}, f32[512,256]{1,0:T(8,128)}, u32[]{:S(2)}) copy-start(f32[512,256]{1,0:T(8,128)} %get-tuple-element.92.diag0) | copy-start | bytes 1572868 | tf_op jit(solution)/shard_map/cond
  41.4 2.5 %copy-start.12 = (f32[512,512]{1,0:T(8,128)S(1)}, f32[512,512]{1,0:T(8,128)}, u32[]{:S(2)}) copy-start(f32[512,512]{1,0:T(8,128)} %get-tuple-element.73.corner.corner1) | copy-start | bytes 3145732 | tf_op jit(solution)/shard_map/cond
  41.4 2.5 %copy-start.15 = (f32[512,256]{1,0:T(8,128)S(1)}, f32[512,256]{1,0:T(8,128)}, u32[]{:S(2)}) copy-start(f32[512,256]{1,0:T(8,128)} %get-tuple-element.90.corner2) | copy-start | bytes 1572868 | tf_op jit(solution)/shard_map/cond
